TPU v7x, 32 devices: a whole 2x2x4 slice. The times are simulated.
32 devices in a mesh: dp: 4 (over y, x), seq: 8 (over z, core).
Axes of the slice: x: 2, y: 2, z: 4, core: 2. Of those that a mesh axis runs over, the one named last changes fastest.
Arguments:
- hidden_in: bfloat16 [4, 1024, 2048], P('dp', 'seq'), may hold values from -6 to 6
- segment_ids: int32 [4, 1024], P('dp', 'seq'), may hold values from 0 to 3, never falling along the last dimension, each value on 1 to 512 neighbouring positions
- grad_out: bfloat16 [4, 1024, 2048], P('dp', 'seq'), may hold values from -6 to 6
- attn_gain: float32 [2048], replicated, may hold values from 0.5 to 1.5
- w_query: float32 [2048, 1536], P(('dp', 'seq')), may hold values from -0.125 to 0.125
- w_key: float32 [2048, 1536], P(('dp', 'seq')), may hold values from -0.125 to 0.125
- w_value: float32 [2048, 3072], P(('dp', 'seq')), may hold values from -0.125 to 0.125
- w_decay: float32 [2048, 6], P(('dp', 'seq')), may hold values from -0.125 to 0.125
- w_beta: float32 [2048, 6], P(('dp', 'seq')), may hold values from -0.125 to 0.125
- w_outgate: float32 [2048, 3072], P(('dp', 'seq')), may hold values from -0.125 to 0.125
- a_log: float32 [6], replicated, may hold values from -10 to -3
- conv_query: float32 [4, 1536], replicated, may hold values from -3 to 3
- conv_key: float32 [4, 1536], replicated, may hold values from -3 to 3
- conv_value: float32 [4, 3072], replicated, may hold values from -3 to 3
- out_gain: float32 [512], replicated, may hold values from 0.5 to 1.5
- w_output: float32 [2048, 3072], P(('dp', 'seq')), may hold values from -0.109375 to 0.109375
- mlp_gain: float32 [2048], replicated, may hold values from 0.5 to 1.5
- w_gate: float32 [2048, 5632], P(('dp', 'seq')), may hold values from -0.125 to 0.125
- w_up: float32 [2048, 5632], P(('dp', 'seq')), may hold values from -0.125 to 0.125
- w_down: float32 [2048, 5632], P(('dp', 'seq')), may hold values from -0.078125 to 0.078125
Outputs:
- hidden_out: bfloat16 [4, 1024, 2048], P('dp', 'seq')
- grad_in: bfloat16 [4, 1024, 2048], P('dp', 'seq')
- grad_attn_gain: float32 [2048], replicated
- grad_w_query: float32 [2048, 1536], P(('dp', 'seq'))
- grad_w_key: float32 [2048, 1536], P(('dp', 'seq'))
- grad_w_value: float32 [2048, 3072], P(('dp', 'seq'))
- grad_w_decay: float32 [2048, 6], P(('dp', 'seq'))
- grad_w_beta: float32 [2048, 6], P(('dp', 'seq'))
- grad_w_outgate: float32 [2048, 3072], P(('dp', 'seq'))
- grad_a_log: float32 [6], replicated
- grad_conv_query: float32 [4, 1536], replicated
- grad_conv_key: float32 [4, 1536], replicated
- grad_conv_value: float32 [4, 3072], replicated
- grad_out_gain: float32 [512], replicated
- grad_w_output: float32 [2048, 3072], P(('dp', 'seq'))
- grad_mlp_gain: float32 [2048], replicated
- grad_w_gate: float32 [2048, 5632], P(('dp', 'seq'))
- grad_w_up: float32 [2048, 5632], P(('dp', 'seq'))
- grad_w_down: float32 [2048, 5632], P(('dp', 'seq'))
Inputs may be any that keep to these rules, and one draw needn't show every extreme that they name: `segment_ids`: document numbers of a packed row start at 0 and never fall; a document holds at most half of the row's 1024 tokens, and one holds exactly that many.
All inputs are finite; a program needn't handle non-finite values.
Results may differ from a plain program's by a relative error of at most 0.015.
The roundings to bfloat16 on the way count: a program that leaves them out, or rounds other values in their place, can miss the bound.
Values may be sent and summed in bfloat16 or wider, within the bound.
A program may use at most 768 MiB of HBM per device.

v0:
```python
from functools import partial

import jax
import jax.numpy as jnp
from jax import lax
from jax.sharding import PartitionSpec as P

CONV = 4
BLOCK = 64


EPSILON = 1e-06
EXACT_PRECISION = lax.Precision.HIGHEST


def passed_along(x, axis, by):
    devices = lax.axis_size(axis)
    pairs = [(i, i + by) for i in range(devices) if 0 <= i + by < devices]
    return lax.ppermute(x, axis, pairs)


def rms_scale(values):
    return values * lax.rsqrt(jnp.mean(values * values, axis=-1, keepdims=True) + EPSILON)


def unit_rows(values):
    return values * lax.rsqrt(jnp.sum(values * values, axis=-1, keepdims=True) + EPSILON)


def swiglu(gate_values, up_values):
    return jax.nn.silu(gate_values) * up_values


def gated_norm(mixed, gate_pre, gain):
    gate = jax.nn.silu(gate_pre).reshape(mixed.shape)
    return (rms_scale(mixed) * gain * gate).reshape(gate_pre.shape)


def contract_last(left, right):
    return lax.dot_general(
        left, right, (((1,), (1,)), ((), ())), preferred_element_type=jnp.float32
    )


def contract_first(left, right):
    return lax.dot_general(
        left, right, (((0,), (0,)), ((), ())), preferred_element_type=jnp.float32
    )


def prepare(seg_ext, pre_ext, decay_pre, beta_pre, a_log, conv_query, conv_key, conv_value):
    kernel = jnp.concatenate([conv_query, conv_key, conv_value], axis=1)
    margin = CONV - 1
    length = pre_ext.shape[0] - margin
    heads = a_log.shape[0]
    key_width = conv_query.shape[1]
    key_size = key_width // heads
    mixed = jnp.zeros((length, kernel.shape[1]), jnp.float32)
    for lag in range(CONV):
        offset = margin - lag
        same = (seg_ext[margin:] == seg_ext[offset : offset + length]).astype(jnp.float32)
        mixed = mixed + kernel[lag] * pre_ext[offset : offset + length] * same[:, None]
    active = jax.nn.silu(mixed)
    queries = unit_rows(active[:, :key_width].reshape(length, heads, key_size)) * key_size ** (-0.5)
    key_vecs = unit_rows(active[:, key_width : 2 * key_width].reshape(length, heads, key_size))
    value_vecs = active[:, 2 * key_width :].reshape(length, heads, -1)
    beta_gate = jax.nn.sigmoid(beta_pre)
    decay_log = -jnp.exp(a_log) * jax.nn.softplus(decay_pre)
    return (queries, key_vecs, value_vecs, beta_gate, decay_log)


def local_blocks(segment, seg_first, queries, key_vecs, value_vecs, beta_gate, decay_log):
    length, heads, key_size = queries.shape
    value_size = value_vecs.shape[2]
    blocks = length // BLOCK
    width = value_size + key_size
    extended = jnp.concatenate(
        [value_vecs, jnp.zeros((length, heads, key_size), jnp.float32)], axis=2
    )
    before = jnp.concatenate([seg_first[None], segment[:-1]])

    def split_heads(values):
        return jnp.moveaxis(values.reshape((blocks, BLOCK) + values.shape[1:]), 2, 1)

    block_ids = segment.reshape(blocks, BLOCK)
    first_ids = before.reshape(blocks, BLOCK)[:, 0]
    order = jnp.arange(BLOCK)
    lower = order[:, None] >= order[None, :]
    below = (order[:, None] > order[None, :]).astype(jnp.float32)
    start_state = jnp.concatenate(
        [
            jnp.zeros((heads, key_size, value_size), jnp.float32),
            jnp.broadcast_to(jnp.eye(key_size, dtype=jnp.float32), (heads, key_size, key_size)),
        ],
        axis=2,
    )

    def one_block(state, block):
        query_block, key_block, value_block, beta_block, decay_block, id_block, id_first = block
        running = jnp.cumsum(decay_block, axis=1)
        live = (id_block[:, None] == id_block[None, :]) & lower
        spread = running[:, :, None] - running[:, None, :]
        decay = jnp.where(live, jnp.exp(jnp.where(live, spread, 0.0)), 0.0)
        from_start = jnp.exp(running) * (id_block == id_first).astype(jnp.float32)
        inner = jnp.einsum("hik,hjk->hij", key_block, key_block, precision=EXACT_PRECISION)
        system = jnp.eye(BLOCK, dtype=jnp.float32) + beta_block[:, :, None] * inner * (
            decay * below
        )
        targets = beta_block[:, :, None] * jnp.concatenate(
            [value_block, from_start[:, :, None] * key_block], axis=2
        )
        solved = jax.scipy.linalg.solve_triangular(system, targets, lower=True)
        update = solved[:, :, :width] - jnp.einsum(
            "hik,hkw->hiw", solved[:, :, width:], state, precision=EXACT_PRECISION
        )
        scores = (
            jnp.einsum("hik,hjk->hij", query_block, key_block, precision=EXACT_PRECISION) * decay
        )
        output = from_start[:, :, None] * jnp.einsum(
            "hik,hkw->hiw", query_block, state, precision=EXACT_PRECISION
        ) + jnp.einsum("hij,hjw->hiw", scores, update, precision=EXACT_PRECISION)
        tail = decay[:, -1, :]
        state = from_start[:, -1][:, None, None] * state + jnp.einsum(
            "hjk,hjw->hkw", tail[:, :, None] * key_block, update, precision=EXACT_PRECISION
        )
        return (state, output)

    inputs = (
        split_heads(queries),
        split_heads(key_vecs),
        split_heads(extended),
        split_heads(beta_gate),
        split_heads(decay_log),
        block_ids,
        first_ids,
    )
    state, outputs = lax.scan(one_block, start_state, inputs)
    outputs = jnp.moveaxis(outputs, 1, 2).reshape(length, heads, width)
    return (
        outputs[:, :, :value_size],
        outputs[:, :, value_size:],
        state[:, :, :value_size],
        state[:, :, value_size:],
    )


def owner_sums(term_maker, owned):
    return lax.psum_scatter(
        term_maker(jnp.int32(0), lax.axis_size(("dp", "seq")) * owned),
        ("dp", "seq"),
        scatter_dimension=0,
        tiled=True,
    )


def split_columns(values, widths):
    columns = []
    offset = 0
    for size in widths:
        columns.append(values[:, offset : offset + size])
        offset = offset + size
    return columns


def local(
    hidden_in,
    segment_ids,
    grad_out,
    attn_gain,
    w_query,
    w_key,
    w_value,
    w_decay,
    w_beta,
    w_outgate,
    a_log,
    conv_query,
    conv_key,
    conv_value,
    out_gain,
    w_output,
    mlp_gain,
    w_gate,
    w_up,
    w_down,
):
    inputs = hidden_in[0].astype(jnp.float32)
    segment = segment_ids[0]
    grad_low = grad_out[0]
    length = inputs.shape[0]
    heads = a_log.shape[0]
    key_width = w_query.shape[1]
    value_width = w_value.shape[1]
    key_size = key_width // heads
    value_size = out_gain.shape[0]
    hidden_width = w_gate.shape[1]
    owned = w_query.shape[0]
    margin = CONV - 1
    chain_steps = lax.axis_size("seq") - 1
    normed, norm_pull = jax.vjp(rms_scale, inputs)
    normed_low = (normed * attn_gain).astype(jnp.bfloat16)
    widths = (key_width, key_width, value_width, heads, heads, value_width)
    pieces = (
        lax.all_gather(w_query.astype(jnp.bfloat16), ("dp", "seq"), axis=0, tiled=True),
        lax.all_gather(w_key.astype(jnp.bfloat16), ("dp", "seq"), axis=0, tiled=True),
        lax.all_gather(w_value.astype(jnp.bfloat16), ("dp", "seq"), axis=0, tiled=True),
        lax.all_gather(w_decay.astype(jnp.bfloat16), ("dp", "seq"), axis=0, tiled=True),
        lax.all_gather(w_beta.astype(jnp.bfloat16), ("dp", "seq"), axis=0, tiled=True),
        lax.all_gather(w_outgate.astype(jnp.bfloat16), ("dp", "seq"), axis=0, tiled=True),
    )
    part = normed_low
    query_pre, key_pre, value_pre, decay_pre, beta_pre, gate_pre = tuple(
        (jnp.dot(part, piece, preferred_element_type=jnp.float32) for piece in pieces)
    )
    pre_low = jnp.concatenate([query_pre, key_pre, value_pre], axis=1).astype(jnp.bfloat16)
    rim_values, rim_ids = passed_along(
        (pre_low[-margin:], segment[-margin:].astype(jnp.bfloat16)), "seq", 1
    )
    seg_ext = jnp.concatenate([rim_ids.astype(jnp.int32), segment])
    pre_ext = jnp.concatenate([rim_values, pre_low], axis=0).astype(jnp.float32)
    prepared, prepare_pull = jax.vjp(
        partial(prepare, seg_ext),
        pre_ext,
        decay_pre,
        beta_pre,
        a_log,
        conv_query,
        conv_key,
        conv_value,
    )
    block_outs, block_pull = jax.vjp(
        partial(local_blocks, segment, seg_ext[margin - 1]),
        prepared[0],
        prepared[1],
        prepared[2],
        prepared[3],
        prepared[4],
    )
    own_output, query_effect, offset_state, transfer = block_outs

    def pass_forward(step, incoming):
        leaving = (
            jnp.einsum("hij,hjw->hiw", transfer, incoming, precision=EXACT_PRECISION) + offset_state
        )
        return passed_along(leaving.astype(jnp.bfloat16), "seq", 1).astype(leaving.dtype)

    carried_state = lax.fori_loop(
        0, chain_steps, pass_forward, jnp.zeros((heads, key_size, value_size), jnp.float32)
    )
    mixer_output = own_output + jnp.einsum(
        "uwl,wlf->uwf", query_effect, carried_state, precision=EXACT_PRECISION
    )
    gated, gate_pull = jax.vjp(gated_norm, mixer_output, gate_pre, out_gain)
    gated_low = gated.astype(jnp.bfloat16)
    attended = contract_last(
        gated_low, lax.all_gather(w_output.astype(jnp.bfloat16), ("dp", "seq"), axis=0, tiled=True)
    )
    middle = inputs + attended
    normed_two, norm_pull_two = jax.vjp(rms_scale, middle)
    normed_two_low = (normed_two * mlp_gain).astype(jnp.bfloat16)
    pieces = (
        lax.all_gather(w_gate.astype(jnp.bfloat16), ("dp", "seq"), axis=0, tiled=True),
        lax.all_gather(w_up.astype(jnp.bfloat16), ("dp", "seq"), axis=0, tiled=True),
    )
    part = normed_two_low
    gate_mlp = jnp.dot(part, pieces[0], preferred_element_type=jnp.float32)
    up_mlp = jnp.dot(part, pieces[1], preferred_element_type=jnp.float32)
    hidden, swiglu_pull = jax.vjp(swiglu, gate_mlp, up_mlp)
    hidden_low = hidden.astype(jnp.bfloat16)
    mlp_part = contract_last(
        hidden_low, lax.all_gather(w_down.astype(jnp.bfloat16), ("dp", "seq"), axis=0, tiled=True)
    )
    result = (middle + mlp_part).astype(jnp.bfloat16)
    part = grad_low
    grad_hidden = jnp.dot(
        part,
        lax.all_gather(w_down.astype(jnp.bfloat16), ("dp", "seq"), axis=0, tiled=True),
        preferred_element_type=jnp.float32,
    )
    grad_gate, grad_up = swiglu_pull(grad_hidden)
    gate_grad_low = grad_gate.astype(jnp.bfloat16)
    up_grad_low = grad_up.astype(jnp.bfloat16)
    pieces = lax.all_gather(
        (w_gate.astype(jnp.bfloat16), w_up.astype(jnp.bfloat16)), ("dp", "seq"), axis=0, tiled=True
    )
    grad_normed_two = contract_last(gate_grad_low, pieces[0]) + contract_last(
        up_grad_low, pieces[1]
    )
    grad_mlp_gain = jnp.sum(grad_normed_two * normed_two, axis=0)
    grad_middle = grad_low.astype(jnp.float32) + norm_pull_two(grad_normed_two * mlp_gain)[0]

    def mlp_terms(start, count):
        return jnp.concatenate(
            [
                contract_first(normed_two_low, gate_grad_low),
                contract_first(normed_two_low, up_grad_low),
                contract_first(grad_low, hidden_low),
            ],
            axis=1,
        )

    mlp_rows = owner_sums(mlp_terms, owned)
    attended_grad_low = grad_middle.astype(jnp.bfloat16)
    part = attended_grad_low
    grad_gated = jnp.dot(
        part,
        lax.all_gather(w_output.astype(jnp.bfloat16), ("dp", "seq"), axis=0, tiled=True),
        preferred_element_type=jnp.float32,
    )
    mixed_gradient, grad_gate_pre, grad_out_gain = gate_pull(grad_gated)

    def output_terms(start, count):
        return contract_first(attended_grad_low, gated_low)

    output_rows = owner_sums(output_terms, owned)
    state_effect = jnp.einsum(
        "igd,igy->gdy", query_effect, mixed_gradient, precision=EXACT_PRECISION
    )
    transposed = jnp.swapaxes(transfer, 1, 2)

    def pass_backward(step, incoming):
        leaving = (
            jnp.einsum("hij,hjw->hiw", transposed, incoming, precision=EXACT_PRECISION)
            + state_effect
        )
        return passed_along(leaving.astype(jnp.bfloat16), "seq", -1).astype(leaving.dtype)

    incoming_state = lax.fori_loop(0, chain_steps, pass_backward, jnp.zeros_like(state_effect))
    gradient_effect = jnp.einsum(
        "fmo,muo->fmu", mixed_gradient, carried_state, precision=EXACT_PRECISION
    )
    transfer_gradient = jnp.einsum(
        "cun,cyn->cuy", incoming_state, carried_state, precision=EXACT_PRECISION
    )
    grads_prepared = block_pull(
        (mixed_gradient, gradient_effect, incoming_state, transfer_gradient)
    )
    grad_ext, grad_decay, grad_beta, grad_alog, grad_conv_one, grad_conv_two, grad_conv_three = (
        prepare_pull(grads_prepared)
    )
    returned = passed_along(grad_ext[:margin].astype(jnp.bfloat16), "seq", -1).astype(jnp.float32)
    grad_pre = grad_ext[margin:].at[length - margin :].add(returned)
    pre_grad_low = grad_pre.astype(jnp.bfloat16)
    grads_low = (
        pre_grad_low[:, :key_width],
        pre_grad_low[:, key_width : 2 * key_width],
        pre_grad_low[:, 2 * key_width :],
        grad_decay.astype(jnp.bfloat16),
        grad_beta.astype(jnp.bfloat16),
        grad_gate_pre.astype(jnp.bfloat16),
    )
    pieces = lax.all_gather(
        (
            w_query.astype(jnp.bfloat16),
            w_key.astype(jnp.bfloat16),
            w_value.astype(jnp.bfloat16),
            w_decay.astype(jnp.bfloat16),
            w_beta.astype(jnp.bfloat16),
            w_outgate.astype(jnp.bfloat16),
        ),
        ("dp", "seq"),
        axis=0,
        tiled=True,
    )
    combined = contract_last(grads_low[0], pieces[0])
    for grad_part, piece in zip(grads_low[1:], pieces[1:]):
        combined = combined + contract_last(grad_part, piece)
    grad_attn_gain = jnp.sum(combined * normed, axis=0)
    grad_inputs = grad_middle + norm_pull(combined * attn_gain)[0]

    def mixer_terms(start, count):
        return jnp.concatenate(
            [contract_first(normed_low, grad_part) for grad_part in grads_low], axis=1
        )

    mixer_rows = owner_sums(mixer_terms, owned)
    query_rows, key_rows, value_rows, decay_rows, beta_rows, outgate_rows = split_columns(
        mixer_rows, widths
    )
    gate_rows, up_rows, down_rows = split_columns(
        mlp_rows, (hidden_width, hidden_width, hidden_width)
    )
    summed = lax.psum(
        (
            grad_attn_gain,
            grad_alog,
            grad_conv_one,
            grad_conv_two,
            grad_conv_three,
            grad_out_gain,
            grad_mlp_gain,
        ),
        ("dp", "seq"),
    )
    return (
        result[None],
        grad_inputs.astype(jnp.bfloat16)[None],
        summed[0],
        query_rows,
        key_rows,
        value_rows,
        decay_rows,
        beta_rows,
        outgate_rows,
        summed[1],
        summed[2],
        summed[3],
        summed[4],
        summed[5],
        output_rows,
        summed[6],
        gate_rows,
        up_rows,
        down_rows,
    )


def solution(mesh):
    placed = (
        P("dp", "seq", None),
        P("dp", "seq"),
        P("dp", "seq", None),
        P(),
        P(("dp", "seq"), None),
        P(("dp", "seq"), None),
        P(("dp", "seq"), None),
        P(("dp", "seq"), None),
        P(("dp", "seq"), None),
        P(("dp", "seq"), None),
        P(),
        P(),
        P(),
        P(),
        P(),
        P(("dp", "seq"), None),
        P(),
        P(("dp", "seq"), None),
        P(("dp", "seq"), None),
        P(("dp", "seq"), None),
    )
    return jax.shard_map(
        local,
        mesh=mesh,
        in_specs=placed,
        out_specs=(
            P("dp", "seq", None),
            P("dp", "seq", None),
            P(),
            P(("dp", "seq"), None),
            P(("dp", "seq"), None),
            P(("dp", "seq"), None),
            P(("dp", "seq"), None),
            P(("dp", "seq"), None),
            P(("dp", "seq"), None),
            P(),
            P(),
            P(),
            P(),
            P(),
            P(("dp", "seq"), None),
            P(),
            P(("dp", "seq"), None),
            P(("dp", "seq"), None),
            P(("dp", "seq"), None),
        ),
        check_vma=False,
    )
```

profile of v0, /device:TPU:0, one launch (start us, length us, event | category | flops | bytes accessed | tf_op | source)
XLA Modules:
  0.0 4433.5 jit_solution(5568150301816575693)
XLA Ops:
  25.3 43.5 all-gather.1
  70.6 37.1 all-gather
  118.6 37.2 all-gather.11.cloned.1.call-done
  159.6 94.3 %all-gather.15.cloned.1.call-done = bf16[2048,3072]{1,0:T(8,128)(2,1)} async-done(((bf16[64,3072]{1,0:T(8,128)(2,1)}), bf16[2048,3072]{1,0:T(8,128)(2,1)}) %all-gather.15.cloned.1.call-update) | async-done | bytes 12582928 | tf_op jit(solution)/shard_map/all_gather | solution.py:206
  262.9 88.8 %all-gather.17.cloned.1.call-done = bf16[2048,3072]{1,0:T(8,128)(2,1)} async-done(((bf16[64,3072]{1,0:T(8,128)(2,1)}), bf16[2048,3072]{1,0:T(8,128)(2,1)}) %all-gather.17.cloned.1.call-update) | async-done | bytes 12582928 | tf_op jit(solution)/shard_map/all_gather | solution.py:209
  393.4 161.1 %while.116 = (s32[]{:T(128)}, f32[6,256,768]{2,1,0:T(8,128)}, f32[2,6,64,768]{3,2,1,0:T(8,128)}, pred[2,6,64,64]{3,2,1,0:T(32,128)(4,1)}, f32[2,6,64,64]{3,2,1,0...) while((s32[]{:T(128)}, f32[6,256,768]{2,1,0:T(8,128)}, ...), condition=%wide.region_5.6_spmd.clone.clone, body=%wide.region_3.5_spmd.clone.clone.sunk | while | flops 3402752512 | bytes 197493040 | solution.py:137
  413.0 30.8 custom-call.54
  492.5 30.8 custom-call.54
  573.3 310.1 %while.117 = (s32[]{:T(128)}, f32[6,256,512]{2,1,0:T(8,128)S(1)}, f32[6,256,256]{2,1,0:T(8,128)}, f32[6,256,512]{2,1,0:T(8,128)}, s32[]{:T(128)}, /*index=5*/s32[]{:T(128)}) while((s32[]{:T(128)}, f32[6,256,512]{2,1,0:T(8,128)S(1)}, f32[6,256,256]{2,1,0:T(8,128)}, f32[6,256,512]{2,1,0:T(8,128)}, s32[]{:T(128)}, ...), condition=%wide.region_7.8_spmd.clone, body=%wide.region_6.7_spmd.clone.sunk | while | flops 2419064832 | bytes 20447352 | solution.py:247
  592.8 25.2 collective-permute-start
  628.3 38.6 collective-permute-start
  677.2 40.6 collective-permute-start
  728.1 50.5 %collective-permute-start = (bf16[6,256,512]{2,1,0:T(8,128)(2,1)}, bf16[6,256,512]{2,1,0:T(8,128)(2,1)}, u32[]{:S(2)}, u32[]{:S(2)}) collective-permute-start(bf16[6,256,512]{2,1,0:T(8,128)(2,1)} %add_convert_fusion.4), channel_id=1, source_target_pairs={{0,1},{1,2},{2,3},{3,4},{4,5},{5,6},{6,7},{8,9},{9,10},{10,11},{11... | collective-permute-start | bytes 4718600 | tf_op jit(solution)/shard_map/while/body/eval_jaxpr/ppermute | solution.py:19
  789.0 39.6 collective-permute-start
  838.9 40.4 collective-permute-start
  903.4 12.6 fusion.251
  916.0 13.3 fusion.252
  929.3 11.3 all-gather.25.cloned.1.call-done
  940.6 13.5 multiply_convert_fusion
  954.2 17.8 convolution_bitcast_fusion
  972.0 17.9 fusion.257
  989.9 18.5 fusion.256
  1008.4 88.7 %pad_maximum_fusion.2 = f32[2048,16896]{1,0:T(8,128)} fusion(f32[2048,5632]{1,0:T(8,128)} %convolution_bitcast_fusion, f32[2048,5632]{1,0:T(8,128)} %fusion.257, f32[2048,5632]{1,0:T(8,128)} %fusion.256), kind=kLoop, calls=%fused_computation.228 | loop fusion | flops 69206016 | bytes 276824064 | tf_op jit(solution)/shard_map/concatenate | solution.py:293
  1101.0 11.9 fusion.253
  1112.9 12.8 multiply_reduce_fusion.7
  1127.2 9.6 fusion.212
  1163.6 475.6 %while.118 = (s32[]{:T(128)}, f32[6,256,512]{2,1,0:T(8,128)}, f32[6,256,256]{2,1,0:T(8,128)}, f32[6,256,512]{2,1,0:T(8,128)}, s32[]{:T(128)}, /*index=5*/s32[]{:T(128)}) while((s32[]{:T(128)}, f32[6,256,512]{2,1,0:T(8,128)}, f32[6,256,256]{2,1,0:T(8,128)}, f32[6,256,512]{2,1,0:T(8,128)}, s32[]{:T(128)}, ...), condition=%wide.region_13.14_spmd.clone, body=%wide.region_12.13_spmd.clone.sunk | while | flops 2419064832 | bytes 20447352 | solution.py:328
  1171.4 44.8 %collective-permute-done.1 = bf16[6,256,512]{2,1,0:T(8,128)(2,1)} collective-permute-done((bf16[6,256,512]{2,1,0:T(8,128)(2,1)}, bf16[6,256,512]{2,1,0:T(8,128)(2,1)}, u32[]{:S(2)}, u32[]{:S(2)}) %collective-permute-start.1) | collective-permute-done | bytes 1572896 | tf_op jit(solution)/shard_map/while/body/eval_jaxpr/ppermute | solution.py:19
  1228.8 69.3 %collective-permute-done.1 = bf16[6,256,512]{2,1,0:T(8,128)(2,1)} collective-permute-done((bf16[6,256,512]{2,1,0:T(8,128)(2,1)}, bf16[6,256,512]{2,1,0:T(8,128)(2,1)}, u32[]{:S(2)}, u32[]{:S(2)}) %collective-permute-start.1) | collective-permute-done | bytes 1572896 | tf_op jit(solution)/shard_map/while/body/eval_jaxpr/ppermute | solution.py:19
  1310.6 54.4 %collective-permute-done.1 = bf16[6,256,512]{2,1,0:T(8,128)(2,1)} collective-permute-done((bf16[6,256,512]{2,1,0:T(8,128)(2,1)}, bf16[6,256,512]{2,1,0:T(8,128)(2,1)}, u32[]{:S(2)}, u32[]{:S(2)}) %collective-permute-start.1) | collective-permute-done | bytes 1572896 | tf_op jit(solution)/shard_map/while/body/eval_jaxpr/ppermute | solution.py:19
  1377.4 55.7 %collective-permute-done.1 = bf16[6,256,512]{2,1,0:T(8,128)(2,1)} collective-permute-done((bf16[6,256,512]{2,1,0:T(8,128)(2,1)}, bf16[6,256,512]{2,1,0:T(8,128)(2,1)}, u32[]{:S(2)}, u32[]{:S(2)}) %collective-permute-start.1) | collective-permute-done | bytes 1572896 | tf_op jit(solution)/shard_map/while/body/eval_jaxpr/ppermute | solution.py:19
  1445.7 54.9 %collective-permute-done.1 = bf16[6,256,512]{2,1,0:T(8,128)(2,1)} collective-permute-done((bf16[6,256,512]{2,1,0:T(8,128)(2,1)}, bf16[6,256,512]{2,1,0:T(8,128)(2,1)}, u32[]{:S(2)}, u32[]{:S(2)}) %collective-permute-start.1) | collective-permute-done | bytes 1572896 | tf_op jit(solution)/shard_map/while/body/eval_jaxpr/ppermute | solution.py:19
  1513.0 55.6 %collective-permute-done.1 = bf16[6,256,512]{2,1,0:T(8,128)(2,1)} collective-permute-done((bf16[6,256,512]{2,1,0:T(8,128)(2,1)}, bf16[6,256,512]{2,1,0:T(8,128)(2,1)}, u32[]{:S(2)}, u32[]{:S(2)}) %collective-permute-start.1) | collective-permute-done | bytes 1572896 | tf_op jit(solution)/shard_map/while/body/eval_jaxpr/ppermute | solution.py:19
  1581.0 54.4 %collective-permute-done.1 = bf16[6,256,512]{2,1,0:T(8,128)(2,1)} collective-permute-done((bf16[6,256,512]{2,1,0:T(8,128)(2,1)}, bf16[6,256,512]{2,1,0:T(8,128)(2,1)}, u32[]{:S(2)}, u32[]{:S(2)}) %collective-permute-start.1) | collective-permute-done | bytes 1572896 | tf_op jit(solution)/shard_map/while/body/eval_jaxpr/ppermute | solution.py:19
  1651.7 193.8 %while.115 = (s32[]{:T(128)}, f32[6,256,768]{2,1,0:T(8,128)}, f32[2,6,64,256]{3,2,1,0:T(8,128)}, f32[2,6,64,256]{3,2,1,0:T(8,128)}, f32[2,6,64,768]{3,2,0,1:T(8,...) while((s32[]{:T(128)}, f32[6,256,768]{2,1,0:T(8,128)}, ...), condition=%wide.region_24.25_spmd.clone, body=%wide.region_14.24_spmd.clone.sunk | while | flops 6825234432 | bytes 292086912 | solution.py:137
  1690.3 30.9 custom-call.53
  1773.1 30.9 custom-call.53
  1882.3 10.6 fusion.225
  1894.6 36.8 collective-permute-done.4
  1944.9 10.6 fusion.195
  1955.5 87.2 %concatenate.45 = f32[2048,9228]{1,0:T(8,128)} concatenate(f32[2048,1536]{1,0:T(8,128)} %fusion.206, f32[2048,1536]{1,0:T(8,128)} %fusion.203, f32[2048,3072]{1,0:T(8,128)} %fusion.195, f32[2048,6]{1,0:T(8,128)} %fusion.229, f32[2048,6]{1,0:T(8,128)} %fusion.227, f32[2048,3072]{1,0:T(8,128)} %fusion.225), dimensions={1} | concatenate | bytes 151191552 | tf_op jit(solution)/shard_map/concatenate | solution.py:372
  2059.3 9.3 fusion.197
  2073.7 10.3 fusion.210
  2085.2 13.1 fusion.173
  2099.5 1124.9 %all-reduce.26.cloned.1.call-done = f32[2048,16896]{1,0:T(8,128)} async-done(((f32[2048,16896]{1,0:T(8,128)}), f32[2048,16896]{1,0:T(8,128)}) %all-reduce.26.cloned.1.call-update) | async-done | bytes 138412048
  3229.5 805.6 %reduce-scatter.3.cloned.1.call-done = f32[64,9228]{1,0:T(8,128)} async-done(((f32[2048,9228]{1,0:T(8,128)}), f32[64,9228]{1,0:T(8,128)}) %reduce-scatter.3.cloned.1.call-update) | async-done | bytes 2362384 | tf_op jit(solution)/shard_map/reduce_scatter | solution.py:148
  4042.1 122.8 %all-reduce.28.cloned.1.call-done = (f32[2048]{0:T(1024)}, f32[6]{0:T(128)}, f32[4,1536]{1,0:T(4,128)}, f32[4,1536]{1,0:T(4,128)}, f32[4,3072]{1,0:T(4,128)}, /*index=5*/f32[512]{0:T(512)}, f32[2048]{0:T(1024)}) async-done(((f32[2048]{0:T(1024)}, f32[6]{0:T(128)}, f32[4,1536]{1,0:T(4,128)}, f32[4,1536]{1,0:T(4,128)}, f32[4,3072]{1,0:T(4,128)}, /*index=5*/f32[512]{0:T(512)}, f32[2048]{0:T(1024)}), ...) | async-done | bytes 116776 | tf_op jit(solution)/shard_map/psum | solution.py:383
  4165.0 252.1 %reduce-scatter.5.cloned.1.call-done = f32[64,3072]{1,0:T(8,128)} async-done(((f32[2048,3072]{1,0:T(8,128)}), f32[64,3072]{1,0:T(8,128)}) %reduce-scatter.5.cloned.1.call-update) | async-done | bytes 786448 | tf_op jit(solution)/shard_map/reduce_scatter | solution.py:148
  (991 shorter events, 624.8 us)
Async XLA Ops:
  7.2 107.6 %all-gather.13.cloned.1.call-start = ((), (), s32[]{:S(2)}) async-start(), calls=%async_computation.3 | async-start | bytes 6488064 | tf_op jit(solution)/shard_map/all_gather | solution.py:205
  9.0 146.8 %all-gather.11.cloned.1.call-start = ((), (), s32[]{:S(2)}) async-start(), calls=%async_computation.2 | async-start | bytes 6488064 | tf_op jit(solution)/shard_map/all_gather | solution.py:204
  10.8 243.1 %all-gather.15.cloned.1.call-start = ((), (), s32[]{:S(2)}) async-start(), calls=%async_computation.4 | async-start | bytes 12976128 | tf_op jit(solution)/shard_map/all_gather | solution.py:206
  12.8 338.9 %all-gather.17.cloned.1.call-start = ((), (), s32[]{:S(2)}) async-start(), calls=%async_computation.5 | async-start | bytes 12976128 | tf_op jit(solution)/shard_map/all_gather | solution.py:209
  14.9 878.1 %all-gather.19.cloned.1.call-start = ((), (), s32[]{:S(2)}) async-start(), calls=%async_computation.6 | async-start | bytes 12976128 | tf_op jit(solution)/shard_map/all_gather | solution.py:256
  16.9 886.5 %all-gather.21.cloned.1.call-start = ((), (), s32[]{:S(2)}) async-start(), calls=%async_computation.7 | async-start | bytes 23789568 | tf_op jit(solution)/shard_map/all_gather | solution.py:262
  18.0 50.9 %copy-start.14 = (bf16[1,128,2048]{2,1,0:T(8,128)(2,1)S(1)}, bf16[1,128,2048]{2,1,0:T(8,128)(2,1)}, u32[]{:S(2)}) copy-start(bf16[1,128,2048]{2,1,0:T(8,128)(2,1)} %param.30) | copy-start | bytes 1572868
  18.0 51.7 %copy-start.90 = (f32[2048]{0:T(1024)S(1)}, f32[2048]{0:T(1024)}, u32[]{:S(2)}) copy-start(f32[2048]{0:T(1024)} %param.33) | copy-start | bytes 24580
  18.0 898.0 %all-gather.23.cloned.1.call-start = ((), (), s32[]{:S(2)}) async-start(), calls=%async_computation.8 | async-start | bytes 23789568 | tf_op jit(solution)/shard_map/all_gather | solution.py:263
  19.0 51.6 %copy-start.167 = (f32[64,6]{0,1:T(8,128)S(1)}, f32[64,6]{0,1:T(8,128)}, u32[]{:S(2)}) copy-start(f32[64,6]{0,1:T(8,128)} %param.37) | copy-start | bytes 4612
  19.0 88.9 %copy-start.178 = (f32[6]{0:T(128)S(1)}, f32[6]{0:T(128)}, u32[]{:S(2)}) copy-start(f32[6]{0:T(128)} %param.40) | copy-start | bytes 76
  19.0 921.6 %all-gather.25.cloned.1.call-start = ((), (), s32[]{:S(2)}) async-start(), calls=%async_computation.9 | async-start | bytes 23789568 | tf_op jit(solution)/shard_map/all_gather | solution.py:271
  21.4 3202.9 %all-reduce.26.cloned.1.call-start = ((), (), s32[]{:S(2)}) async-start(), calls=%async_computation.12 | async-start | bytes 276824064
  22.7 90.3 %collective-permute-start.2 = (bf16[3]{0:T(256)(128)(2,1)S(1)}, bf16[3]{0:T(256)(128)(2,1)S(1)}, u32[]{:S(2)}, u32[]{:S(2)}) collective-permute-start(bf16[3]{0:T(256)(128)(2,1)S(1)} %slice_bitcast_fusion.3), channel_id=1, source_target_pairs={{0,1},{1,2},{2,3},{3,4},{4,5},{5,6},{6,7},{8,9},{9,10},{10,11},{11... | collective-permute-start | bytes 26 | tf_op jit(solution)/shard_map/ppermute | solution.py:19
  69.7 282.0 %copy-start.116 = (f32[128]{0:T(128)}, f32[128]{0:T(128)S(1)}, u32[]{:S(2)}) copy-start(f32[128]{0:T(128)S(1)} %fusion.223) | copy-start | bytes 1540
  113.0 251.1 %copy-start.104 = (f32[1,6144]{1,0:T(1,128)}, f32[1,6144]{1,0:T(1,128)S(1)}, u32[]{:S(2)}) copy-start(f32[1,6144]{1,0:T(1,128)S(1)} %get-tuple-element.2405) | copy-start | bytes 73732
  113.0 251.1 %copy-start.106 = (f32[1,6144]{1,0:T(1,128)}, f32[1,6144]{1,0:T(1,128)S(1)}, u32[]{:S(2)}) copy-start(f32[1,6144]{1,0:T(1,128)S(1)} %get-tuple-element.2406) | copy-start | bytes 73732
  113.0 251.1 %copy-start.108 = (f32[1,6144]{1,0:T(1,128)}, f32[1,6144]{1,0:T(1,128)S(1)}, u32[]{:S(2)}) copy-start(f32[1,6144]{1,0:T(1,128)S(1)} %get-tuple-element.2407) | copy-start | bytes 73732
  113.0 251.1 %copy-start.110 = (f32[1,6144]{1,0:T(1,128)}, f32[1,6144]{1,0:T(1,128)S(1)}, u32[]{:S(2)}) copy-start(f32[1,6144]{1,0:T(1,128)S(1)} %get-tuple-element.2408) | copy-start | bytes 73732
  114.7 249.4 %copy-start.157 = (f32[128]{0:T(128)}, f32[128]{0:T(128)S(1)}, u32[]{:S(2)}) copy-start(f32[128]{0:T(128)S(1)} %get-tuple-element.2413) | copy-start | bytes 1540
  114.7 249.4 %copy-start.159 = (f32[128]{0:T(128)}, f32[128]{0:T(128)S(1)}, u32[]{:S(2)}) copy-start(f32[128]{0:T(128)S(1)} %get-tuple-element.2414) | copy-start | bytes 1540
  114.7 249.5 %copy-start.161 = (f32[128]{0:T(128)}, f32[128]{0:T(128)S(1)}, u32[]{:S(2)}) copy-start(f32[128]{0:T(128)S(1)} %get-tuple-element.2415) | copy-start | bytes 1540
  159.6 100.9 %copy-start.73 = (bf16[128,1536]{1,0:T(8,128)(2,1)}, bf16[128,1536]{1,0:T(8,128)(2,1)S(1)}, u32[]{:S(2)}) copy-start(bf16[128,1536]{1,0:T(8,128)(2,1)S(1)} %convolution_convert_fusion.2) | copy-start | bytes 1179652
  260.5 103.1 %collective-permute-start.3 = (bf16[3,6144]{1,0:T(4,128)(2,1)S(1)}, bf16[3,6144]{1,0:T(4,128)(2,1)S(1)}, u32[]{:S(2)}, u32[]{:S(2)}) collective-permute-start(bf16[3,6144]{1,0:T(4,128)(2,1)S(1)} %pad_maximum_fusion.3), channel_id=1, source_target_pairs={{0,1},{1,2},{2,3},{3,4},{4,5},{5,6},{6,7},{8,9},{9,10},{10,11},{11... | collective-permute-start | bytes 110600 | tf_op jit(solution)/shard_map/ppermute | solution.py:19
  408.7 46.7 %slice-start.2 = ((s8[4718592]{0:T(1024)(128)(4,1)}), s8[524288]{0:T(1024)(128)(4,1)S(1)}, s32[]{:S(2)}) async-start(s8[4718592]{0:T(1024)(128)(4,1)} %bitcast.592), calls=%async_computation.16 | async-start | bytes 1048576 | tf_op jit(solution)/shard_map/jvp()/while
  488.2 48.0 %slice-start.2 = ((s8[4718592]{0:T(1024)(128)(4,1)}), s8[524288]{0:T(1024)(128)(4,1)S(1)}, s32[]{:S(2)}) async-start(s8[4718592]{0:T(1024)(128)(4,1)} %bitcast.592), calls=%async_computation.16 | async-start | bytes 1048576 | tf_op jit(solution)/shard_map/jvp()/while
  579.5 5.3 collective-permute-start
  592.8 27.4 collective-permute-start
  628.3 40.9 collective-permute-start
  677.2 42.8 collective-permute-start
  728.1 52.7 %collective-permute-start = (bf16[6,256,512]{2,1,0:T(8,128)(2,1)}, bf16[6,256,512]{2,1,0:T(8,128)(2,1)}, u32[]{:S(2)}, u32[]{:S(2)}) collective-permute-start(bf16[6,256,512]{2,1,0:T(8,128)(2,1)} %add_convert_fusion.4), channel_id=1, source_target_pairs={{0,1},{1,2},{2,3},{3,4},{4,5},{5,6},{6,7},{8,9},{9,10},{10,11},{11... | collective-permute-start | bytes 4718600 | tf_op jit(solution)/shard_map/while/body/eval_jaxpr/ppermute | solution.py:19
  789.0 41.8 collective-permute-start
  838.9 42.7 collective-permute-start
  954.2 17.9 copy-start.43
  1097.1 2937.9 %reduce-scatter.3.cloned.1.call-start = ((), (), s32[]{:S(2)}) async-start(), calls=%async_computation.10 | async-start | bytes 78938112 | tf_op jit(solution)/shard_map/reduce_scatter | solution.py:148
  1170.1 46.1 %collective-permute-start.1 = (bf16[6,256,512]{2,1,0:T(8,128)(2,1)}, bf16[6,256,512]{2,1,0:T(8,128)(2,1)}, u32[]{:S(2)}, u32[]{:S(2)}) collective-permute-start(bf16[6,256,512]{2,1,0:T(8,128)(2,1)} %add_convert_fusion.5), channel_id=1, source_target_pairs={{1,0},{2,1},{3,2},{4,3},{5,4},{6,5},{7,6},{9,8},{10,9},{11,10},{12... | collective-permute-start | bytes 4718600 | tf_op jit(solution)/shard_map/while/body/eval_jaxpr/ppermute | solution.py:19
  1227.5 70.6 %collective-permute-start.1 = (bf16[6,256,512]{2,1,0:T(8,128)(2,1)}, bf16[6,256,512]{2,1,0:T(8,128)(2,1)}, u32[]{:S(2)}, u32[]{:S(2)}) collective-permute-start(bf16[6,256,512]{2,1,0:T(8,128)(2,1)} %add_convert_fusion.5), channel_id=1, source_target_pairs={{1,0},{2,1},{3,2},{4,3},{5,4},{6,5},{7,6},{9,8},{10,9},{11,10},{12... | collective-permute-start | bytes 4718600 | tf_op jit(solution)/shard_map/while/body/eval_jaxpr/ppermute | solution.py:19
  1309.3 55.7 %collective-permute-start.1 = (bf16[6,256,512]{2,1,0:T(8,128)(2,1)}, bf16[6,256,512]{2,1,0:T(8,128)(2,1)}, u32[]{:S(2)}, u32[]{:S(2)}) collective-permute-start(bf16[6,256,512]{2,1,0:T(8,128)(2,1)} %add_convert_fusion.5), channel_id=1, source_target_pairs={{1,0},{2,1},{3,2},{4,3},{5,4},{6,5},{7,6},{9,8},{10,9},{11,10},{12... | collective-permute-start | bytes 4718600 | tf_op jit(solution)/shard_map/while/body/eval_jaxpr/ppermute | solution.py:19
  1376.1 56.9 %collective-permute-start.1 = (bf16[6,256,512]{2,1,0:T(8,128)(2,1)}, bf16[6,256,512]{2,1,0:T(8,128)(2,1)}, u32[]{:S(2)}, u32[]{:S(2)}) collective-permute-start(bf16[6,256,512]{2,1,0:T(8,128)(2,1)} %add_convert_fusion.5), channel_id=1, source_target_pairs={{1,0},{2,1},{3,2},{4,3},{5,4},{6,5},{7,6},{9,8},{10,9},{11,10},{12... | collective-permute-start | bytes 4718600 | tf_op jit(solution)/shard_map/while/body/eval_jaxpr/ppermute | solution.py:19
  1444.4 56.1 %collective-permute-start.1 = (bf16[6,256,512]{2,1,0:T(8,128)(2,1)}, bf16[6,256,512]{2,1,0:T(8,128)(2,1)}, u32[]{:S(2)}, u32[]{:S(2)}) collective-permute-start(bf16[6,256,512]{2,1,0:T(8,128)(2,1)} %add_convert_fusion.5), channel_id=1, source_target_pairs={{1,0},{2,1},{3,2},{4,3},{5,4},{6,5},{7,6},{9,8},{10,9},{11,10},{12... | collective-permute-start | bytes 4718600 | tf_op jit(solution)/shard_map/while/body/eval_jaxpr/ppermute | solution.py:19
  1511.7 56.8 %collective-permute-start.1 = (bf16[6,256,512]{2,1,0:T(8,128)(2,1)}, bf16[6,256,512]{2,1,0:T(8,128)(2,1)}, u32[]{:S(2)}, u32[]{:S(2)}) collective-permute-start(bf16[6,256,512]{2,1,0:T(8,128)(2,1)} %add_convert_fusion.5), channel_id=1, source_target_pairs={{1,0},{2,1},{3,2},{4,3},{5,4},{6,5},{7,6},{9,8},{10,9},{11,10},{12... | collective-permute-start | bytes 4718600 | tf_op jit(solution)/shard_map/while/body/eval_jaxpr/ppermute | solution.py:19
  1579.7 55.7 %collective-permute-start.1 = (bf16[6,256,512]{2,1,0:T(8,128)(2,1)}, bf16[6,256,512]{2,1,0:T(8,128)(2,1)}, u32[]{:S(2)}, u32[]{:S(2)}) collective-permute-start(bf16[6,256,512]{2,1,0:T(8,128)(2,1)} %add_convert_fusion.5), channel_id=1, source_target_pairs={{1,0},{2,1},{3,2},{4,3},{5,4},{6,5},{7,6},{9,8},{10,9},{11,10},{12... | collective-permute-start | bytes 4718600 | tf_op jit(solution)/shard_map/while/body/eval_jaxpr/ppermute | solution.py:19
  1721.1 15.5 slice-start.6
  1804.0 15.1 slice-start.6
  1877.2 54.2 %collective-permute-start.4 = (bf16[3,6144]{1,0:T(4,128)(2,1)S(1)}, bf16[3,6144]{1,0:T(4,128)(2,1)S(1)}, u32[]{:S(2)}, u32[]{:S(2)}) collective-permute-start(bf16[3,6144]{1,0:T(4,128)(2,1)S(1)} %slice.309), channel_id=1, source_target_pairs={{1,0},{2,1},{3,2},{4,3},{5,4},{6,5},{7,6},{9,8},{10,9},{11,10},{12... | collective-permute-start | bytes 110600 | tf_op jit(solution)/shard_map/ppermute | solution.py:19
  2042.8 2122.2 %all-reduce.28.cloned.1.call-start = ((), (), s32[]{:S(2)}) async-start(), calls=%async_computation.13 | async-start | bytes 234496 | tf_op jit(solution)/shard_map/psum | solution.py:383
  2054.2 14.4 slice-start.11
  2073.3 2343.8 %reduce-scatter.5.cloned.1.call-start = ((), (), s32[]{:S(2)}) async-start(), calls=%async_computation.11 | async-start | bytes 25952256 | tf_op jit(solution)/shard_map/reduce_scatter | solution.py:148
  (272 other events, 1340.3 us)
Sparse Core Ops, SparseCore 0:
  11.6 72.3 all-gather.12
  87.5 68.1 all-gather.10
  159.4 94.5 all-gather.14
  257.4 94.2 all-gather.16
  354.6 94.3 all-gather.18
  452.3 143.2 all-gather.20
  598.4 167.3 all-gather.22
  768.7 171.8 all-gather.24
  1097.2 2127.0 all-reduce.25
  3226.5 808.4 reduce-scatter.2
  4043.2 121.7 all-reduce.27
  4171.8 245.2 reduce-scatter.4
where the time goes:
time: 4440 us; the launch traced here: 4430 us
  waiting for transfers between devices  2980 us (67%)
  matrix products  494 us (11%)
  other arithmetic  327 us (7%)
  starting transfers between devices  254 us (6%)
  local copies, waits for them, and re-layouts  251 us (6%)
  blocking collectives  80.6 us (2%)
    unnamed x13, waiting for transfers between devices  1130 us
    reduce_scatter x2, waiting for transfers between devices, owner_sums(): lax.psum_scatter(term_maker(jnp.int32(0), lax.axis_size(('dp', 'seq')) *...  1060 us
    ppermute x17, waiting for transfers between devices, passed_along(): return lax.ppermute(x, axis, pairs)  441 us
    ppermute x17, starting transfers between devices, passed_along(): return lax.ppermute(x, axis, pairs)  253 us
    another operation x8, other arithmetic, one_block(): solved = jax.scipy.linalg.solve_triangular(system, targets, lower=True)  125 us
    psum x1, waiting for transfers between devices, local(): lax.psum((grad_attn_gain, grad_alog, grad_conv_one, grad_conv_two, grad_c...  123 us
    dot_general x10, matrix products, contract_first(): lax.dot_general(left, right, (((0,), (0,)), ((), ())), preferred_element_...  101 us
    all_gather x1, waiting for transfers between devices, local(): lax.all_gather(w_value.astype(jnp.bfloat16), ('dp', 'seq'), axis=0, tiled...  94.3 us
  transfers between devices with their start and end apart: 29, of which 23 were waited for; matrix products, arithmetic and copies ran while one was open for 20% of the time, Pallas kernels for 0%

commit v1 on v0

v1 whole, which is shorter than its diff:
```python
from functools import partial

import jax
import jax.numpy as jnp
from jax import lax
from jax.experimental import pallas as pl
from jax.experimental.pallas import tpu as pltpu
from jax.sharding import Mesh
from jax.sharding import PartitionSpec as P

CONV = 4
EPSILON = 1e-06
EXACT = lax.Precision.HIGHEST
BF16 = jnp.bfloat16
F32 = jnp.float32
BY_MESH = pl.DeviceIdType.MESH
LANES = 128


def rms_scale(values):
    return values * lax.rsqrt(jnp.mean(values * values, axis=-1, keepdims=True) + EPSILON)


def swiglu(gate_values, up_values):
    return jax.nn.silu(gate_values) * up_values


def mm(left, right, over=(1, 0)):
    return lax.dot_general(
        left, right, (((over[0],), (over[1],)), ((), ())), preferred_element_type=F32
    )


def exact(left, right, over=(1, 0)):
    return lax.dot_general(
        left,
        right,
        (((over[0],), (over[1],)), ((), ())),
        precision=EXACT,
        preferred_element_type=F32,
    )


def place():
    return lax.axis_index("dp"), lax.axis_index("zq"), lax.axis_index("c")


def greet(peers):
    barrier = pltpu.get_barrier_semaphore()
    for peer in peers:
        pl.semaphore_signal(barrier, inc=1, device_id=peer, device_id_type=BY_MESH)
    pl.semaphore_wait(barrier, len(peers))


def remote(source, target, send, recv, peer):
    return pltpu.make_async_remote_copy(
        src_ref=source,
        dst_ref=target,
        send_sem=send,
        recv_sem=recv,
        device_id=peer,
        device_id_type=BY_MESH,
    )


def plane_offsets(rows):
    return [(k, flip) for k in range(rows) for flip in (0, 1) if (k, flip) != (0, 0)]


def plane_peer(offset, rows):
    d, z, c = place()
    k, flip = offset
    return (lax.rem(d + k, rows), z, 1 - c if flip else c)


def swap_kernel(rows, x_ref, o_ref, own, send, recv):
    d, z, c = place()
    me = d * 2 + c
    offsets = plane_offsets(rows)
    greet([plane_peer(offset, rows) for offset in offsets])
    copies = []
    for i, offset in enumerate(offsets):
        peer = plane_peer(offset, rows)
        copy = remote(
            x_ref.at[peer[0] * 2 + peer[2]], o_ref.at[me], send.at[i], recv.at[i], peer
        )
        copy.start()
        copies.append(copy)
    keep = pltpu.make_async_copy(x_ref.at[me], o_ref.at[me], own)
    keep.start()
    keep.wait()
    for copy in copies:
        copy.wait()


def spread_kernel(rows, x_ref, o_ref, own, send, recv, pair_send, pair_recv):
    d, z, c = place()
    me = d * 2 + c
    pair = (d, z, 1 - c)
    others = [(lax.rem(d + k, rows), z, c) for k in range(1, rows)]
    greet(others + [pair])
    copies = []
    for i, peer in enumerate(others):
        copy = remote(x_ref, o_ref.at[me], send.at[i], recv.at[i], peer)
        copy.start()
        copies.append(copy)
    hand = remote(x_ref, o_ref.at[me], pair_send.at[0], pair_recv.at[0], pair)
    hand.start()
    keep = pltpu.make_async_copy(x_ref, o_ref.at[me], own)
    keep.start()
    hands = [hand]
    for i, copy in enumerate(copies):
        copy.wait_recv()
        origin = lax.rem(d + rows - (i + 1), rows) * 2 + c
        hand = remote(
            o_ref.at[origin], o_ref.at[origin], pair_send.at[i + 1], pair_recv.at[i + 1], pair
        )
        hand.start()
        hands.append(hand)
    keep.wait()
    for copy in copies:
        copy.wait_send()
    for hand in hands:
        hand.wait()


def fold_kernel(
    rows, x_ref, o_ref, mine, theirs, load, pair_send, pair_recv, send, recv, own
):
    d, z, c = place()
    pair = (d, z, 1 - c)
    others = [(lax.rem(d + k, rows), z, c) for k in range(1, rows)]
    greet(others + [pair])
    order = [lax.rem(d + k, rows) for k in range(1, rows)] + [d]
    hands, loads = [], []
    for i, to in enumerate(order):
        hand = remote(
            x_ref.at[to * 2 + (1 - c)], theirs.at[i], pair_send.at[i], pair_recv.at[i], pair
        )
        hand.start()
        hands.append(hand)
        copy = pltpu.make_async_copy(x_ref.at[to * 2 + c], mine.at[i], load.at[i])
        copy.start()
        loads.append(copy)
    copies = []
    for i in range(rows):
        loads[i].wait()
        hands[i].wait_recv()
        mine[i] = (mine[i].astype(F32) + theirs[i].astype(F32)).astype(BF16)
        if i < rows - 1:
            copy = remote(mine.at[i], o_ref.at[d], send.at[i], recv.at[i], others[i])
        else:
            copy = pltpu.make_async_copy(mine.at[i], o_ref.at[d], own)
        copy.start()
        copies.append(copy)
    for hand in hands:
        hand.wait_send()
    for copy in copies:
        copy.wait()


def column_kernel(count, x_ref, o_ref, own, send, recv):
    d, z, c = place()
    others = [(d, lax.rem(z + k, count), c) for k in range(1, count)]
    greet(others)
    copies = []
    for i, peer in enumerate(others):
        copy = remote(x_ref, o_ref.at[z], send.at[i], recv.at[i], peer)
        copy.start()
        copies.append(copy)
    keep = pltpu.make_async_copy(x_ref, o_ref.at[z], own)
    keep.start()
    keep.wait()
    for copy in copies:
        copy.wait()


def neighbours(count):
    d, z, c = place()
    after = (d, lax.rem(z + c, count), 1 - c)
    before = (d, lax.rem(z + c - 1 + count, count), 1 - c)
    spot = z * 2 + c
    return spot, before, after


def greet_chain(count):
    spot, before, after = neighbours(count)
    barrier = pltpu.get_barrier_semaphore()

    @pl.when(spot > 0)
    def _():
        pl.semaphore_signal(barrier, inc=1, device_id=before, device_id_type=BY_MESH)

    @pl.when(spot < 2 * count - 1)
    def _():
        pl.semaphore_signal(barrier, inc=1, device_id=after, device_id_type=BY_MESH)

    pl.semaphore_wait(
        barrier,
        (spot > 0).astype(jnp.int32) + (spot < 2 * count - 1).astype(jnp.int32),
    )


def hop_kernel(count, forward, x_ref, o_ref, send, recv):
    spot, before, after = neighbours(count)
    greet_chain(count)
    if forward:
        gives, takes, to = spot < 2 * count - 1, spot > 0, after
    else:
        gives, takes, to = spot > 0, spot < 2 * count - 1, before
    copy = remote(x_ref, o_ref, send, recv, to)

    @pl.when(gives)
    def _():
        copy.start()

    @pl.when(takes)
    def _():
        copy.wait_recv()

    @pl.when(jnp.logical_not(takes))
    def _():
        o_ref[...] = jnp.zeros_like(o_ref)

    @pl.when(gives)
    def _():
        copy.wait_send()


def chain_kernel(
    count, heads, forward, high_ref, low_ref, add_ref, o_ref, land, stage, send, recv
):
    spot, before, after = neighbours(count)
    greet_chain(count)
    if forward:
        gives, takes, to = spot < 2 * count - 1, spot > 0, after
    else:
        gives, takes, to = spot > 0, spot < 2 * count - 1, before
    over = (1, 0) if forward else (0, 0)
    copies = [
        remote(stage.at[h], land.at[h], send.at[h], recv.at[h], to) for h in range(heads)
    ]
    for h in range(heads):

        @pl.when(jnp.logical_not(takes))
        def _():
            land[h] = jnp.zeros_like(land[h])

        @pl.when(takes)
        def _():
            copies[h].wait_recv()

        @pl.when(gives)
        def _():
            state = land[h]
            leaving = add_ref[h] + mm(high_ref[h], state, over) + mm(low_ref[h], state, over)
            stage[h] = leaving.astype(BF16)
            copies[h].start()

    for h in range(heads):

        @pl.when(gives)
        def _():
            copies[h].wait_send()

    o_ref[...] = land[...]


ANY = pl.BlockSpec(memory_space=pl.ANY)
IN_VMEM = pl.BlockSpec(memory_space=pltpu.VMEM)


def dma(*shape):
    return pltpu.SemaphoreType.DMA(shape)


def comm_call(body, out, scratch, ident, operands, spec=ANY, cost=30):
    return pl.pallas_call(
        body,
        out_shape=out,
        in_specs=[spec] * len(operands),
        out_specs=spec,
        scratch_shapes=scratch,
        compiler_params=pltpu.CompilerParams(collective_id=ident, has_side_effects=True),
        cost_estimate=pl.CostEstimate(
            flops=0, bytes_accessed=int(cost * 3.0e6), transcendentals=0
        ),
    )(*operands)


def swap(x, ident):
    rows = lax.axis_size("dp")
    links = 2 * rows - 1
    return comm_call(
        partial(swap_kernel, rows),
        jax.ShapeDtypeStruct(x.shape, x.dtype),
        [pltpu.SemaphoreType.DMA, dma(links), dma(links)],
        ident,
        (x,),
    )


def spread(x, ident):
    rows = lax.axis_size("dp")
    return comm_call(
        partial(spread_kernel, rows),
        jax.ShapeDtypeStruct((2 * rows,) + x.shape, x.dtype),
        [pltpu.SemaphoreType.DMA, dma(rows - 1), dma(rows - 1), dma(rows), dma(rows)],
        ident,
        (x,),
    )


def fold(x, ident):
    rows = lax.axis_size("dp")
    part = (rows,) + x.shape[1:]
    received = comm_call(
        partial(fold_kernel, rows),
        jax.ShapeDtypeStruct(part, x.dtype),
        [
            pltpu.VMEM(part, x.dtype),
            pltpu.VMEM(part, x.dtype),
            dma(rows),
            dma(rows),
            dma(rows),
            dma(rows - 1),
            dma(rows - 1),
            pltpu.SemaphoreType.DMA,
        ],
        ident,
        (x,),
    )
    return jnp.sum(received.astype(F32), axis=0)


def column(x, ident):
    count = lax.axis_size("zq")
    return comm_call(
        partial(column_kernel, count),
        jax.ShapeDtypeStruct((count,) + x.shape, x.dtype),
        [pltpu.SemaphoreType.DMA, dma(count - 1), dma(count - 1)],
        ident,
        (x,),
    )


def hop(x, forward, ident):
    count = lax.axis_size("zq")
    return comm_call(
        partial(hop_kernel, count, forward),
        jax.ShapeDtypeStruct(x.shape, x.dtype),
        [pltpu.SemaphoreType.DMA, pltpu.SemaphoreType.DMA],
        ident,
        (x,),
        IN_VMEM,
    )


def chain(high, low, add, forward, ident):
    count = lax.axis_size("zq")
    heads = add.shape[0]
    return comm_call(
        partial(chain_kernel, count, heads, forward),
        jax.ShapeDtypeStruct(add.shape, BF16),
        [
            pltpu.VMEM(add.shape, BF16),
            pltpu.VMEM(add.shape, BF16),
            dma(heads),
            dma(heads),
        ],
        ident,
        (high, low, add),
        IN_VMEM,
    )


def unit_lower_inverse(low):
    size = low.shape[0]
    row = lax.broadcasted_iota(jnp.int32, low.shape, 0)
    col = lax.broadcasted_iota(jnp.int32, low.shape, 1)

    def same(width):
        shift = width.bit_length() - 1
        return (row >> shift) == (col >> shift)

    eye = (row == col).astype(F32)
    width = 8
    near = jnp.where(same(width), low, 0.0)
    square = exact(near, near)
    inverse = eye - near
    inverse = inverse + exact(inverse, square)
    square = exact(square, square)
    inverse = inverse + exact(inverse, square)
    while width < size:
        cross = jnp.where(same(2 * width) & jnp.logical_not(same(width)), low, 0.0)
        inverse = inverse - exact(inverse, exact(cross, inverse))
        width *= 2
    return inverse


def unit_parts(values):
    scale = lax.rsqrt(jnp.sum(values * values, axis=-1, keepdims=True) + EPSILON)
    return values * scale, scale


def unit_back(unit, scale, grad):
    return scale * (grad - unit * jnp.sum(unit * grad, axis=-1, keepdims=True))


def strict_lower(size):
    row = lax.broadcasted_iota(jnp.int32, (size, size), 0)
    col = lax.broadcasted_iota(jnp.int32, (size, size), 1)
    return (row > col).astype(F32)


def chunk_forward_kernel(
    q_ref,
    k_ref,
    v_ref,
    beta_ref,
    decay_ref,
    start_ref,
    tail_ref,
    inverse_ref,
    scores_ref,
    own_ref,
    effect_ref,
    offset_ref,
    high_ref,
    low_ref,
):
    size, key_size = q_ref.shape
    beta, start, tail = beta_ref[0], start_ref[0], tail_ref[0]
    decay = decay_ref[0]
    query = unit_parts(q_ref[...])[0] * key_size ** (-0.5)
    key = unit_parts(k_ref[...])[0]
    inner = exact(key, key, (1, 1))
    inverse = unit_lower_inverse(beta * inner * (decay * strict_lower(size)))
    scores = exact(query, key, (1, 1)) * decay
    update = exact(inverse, beta * v_ref[...])
    reach = exact(inverse, (beta * start) * key)
    inverse_ref[0] = inverse
    scores_ref[0] = scores
    own_ref[...] = exact(scores, update)
    effect_ref[0] = start * query - exact(scores, reach)
    last = tail * key
    offset_ref[0] = exact(last, update, (0, 0))
    row = lax.broadcasted_iota(jnp.int32, (key_size, key_size), 0)
    col = lax.broadcasted_iota(jnp.int32, (key_size, key_size), 1)
    transfer = jnp.where(row == col, start[size - 1 :, :], 0.0) - exact(last, reach, (0, 0))
    high = transfer.astype(BF16)
    high_ref[0] = high
    low_ref[0] = (transfer - high.astype(F32)).astype(BF16)


def gate_forward_kernel(own_ref, effect_ref, state_ref, gate_ref, gain_ref, mixed_ref, gated_ref):
    mixed = own_ref[...] + exact(effect_ref[0], state_ref[0].astype(F32))
    mixed_ref[...] = mixed
    gate = gate_ref[...].astype(F32)
    gated_ref[...] = (
        rms_scale(mixed) * gain_ref[...] * (gate * jax.nn.sigmoid(gate))
    ).astype(BF16)


def gate_backward_kernel(
    mixed_ref, gate_ref, gain_ref, grad_ref, effect_ref, out_ref, gate_grad_ref, gain_grad_ref, add_ref
):
    mixed = mixed_ref[...]
    gate = gate_ref[...].astype(F32)
    grad = grad_ref[...].astype(F32)
    gain = gain_ref[...]
    scale = lax.rsqrt(jnp.mean(mixed * mixed, axis=-1, keepdims=True) + EPSILON)
    normed = mixed * scale
    sig = jax.nn.sigmoid(gate)
    act = gate * sig
    gain_grad_ref[0] = jnp.sum(grad * normed * act, axis=0, keepdims=True)
    gate_grad_ref[...] = (
        grad * normed * gain * (sig * (1.0 + gate * (1.0 - sig)))
    ).astype(BF16)
    inner = grad * gain * act
    mixed_grad = scale * (inner - normed * jnp.mean(inner * normed, axis=-1, keepdims=True))
    out_ref[...] = mixed_grad
    add_ref[0] = exact(effect_ref[0], mixed_grad, (0, 0))


def chunk_backward_kernel(
    q_ref,
    k_ref,
    v_ref,
    beta_ref,
    decay_ref,
    start_ref,
    tail_ref,
    inverse_ref,
    scores_ref,
    state_ref,
    mixed_ref,
    ending_ref,
    dq_ref,
    dk_ref,
    dv_ref,
    dbeta_ref,
    ddecay_ref,
    dstart_ref,
    dtail_ref,
):
    size, key_size = q_ref.shape
    beta, start, tail = beta_ref[0], start_ref[0], tail_ref[0]
    decay, inverse, scores = decay_ref[0], inverse_ref[0], scores_ref[0]
    state = state_ref[0].astype(F32)
    ending = ending_ref[0].astype(F32)
    mixed_grad = mixed_ref[...]
    unit_q, scale_q = unit_parts(q_ref[...])
    query = unit_q * key_size ** (-0.5)
    key, scale_k = unit_parts(k_ref[...])
    below = strict_lower(size)
    inner = exact(key, key, (1, 1))
    raw = exact(query, key, (1, 1))
    recalled = exact(key, state)
    miss = v_ref[...] - start * recalled
    update = exact(inverse, beta * miss)
    mixed_state = exact(mixed_grad, state, (1, 1))
    last = tail * key
    dupdate = exact(scores, mixed_grad, (0, 0)) + exact(last, ending)
    dscores = exact(mixed_grad, update, (1, 1))
    dlast = exact(update, ending, (1, 1))
    dright = exact(inverse, dupdate, (0, 0))
    dlower = -exact(dright, update, (1, 1)) * below
    dv_ref[...] = beta * dright
    dscaled = dscores * decay
    dquery = start * mixed_state + exact(dscaled, key)
    dinner = beta * dlower * decay
    dkey = (
        tail * dlast
        + exact(dscaled, query, (0, 0))
        - exact((beta * start) * dright, state, (1, 1))
        + exact(dinner, key)
        + exact(dinner, key, (0, 0))
    )
    right_recalled = jnp.sum(dright * recalled, axis=-1, keepdims=True)
    dbeta_ref[0] = jnp.sum(dright * miss, axis=-1, keepdims=True) + jnp.sum(
        dlower * inner * decay, axis=-1, keepdims=True
    )
    final = jnp.sum(jnp.sum(ending * state, axis=-1, keepdims=True), axis=0, keepdims=True)
    row = lax.broadcasted_iota(jnp.int32, (size, 1), 0)
    dstart_ref[0] = (
        jnp.sum(query * mixed_state, axis=-1, keepdims=True)
        - beta * right_recalled
        + jnp.where(row == size - 1, final, 0.0)
    )
    dtail_ref[0] = jnp.sum(key * dlast, axis=-1, keepdims=True)
    ddecay_ref[0] = dscores * raw + beta * dlower * inner
    dq_ref[...] = unit_back(unit_q, scale_q, dquery * key_size ** (-0.5))
    dk_ref[...] = unit_back(key, scale_k, dkey)


def by_head(*shape):
    return pl.BlockSpec((1,) + shape, lambda h: (h, 0, 0))


def by_columns(rows, width, offset=0):
    return pl.BlockSpec((rows, width), lambda h: (0, h + offset))


def head_call(body, heads, in_specs, out_specs, out_shape, operands, flops):
    return pl.pallas_call(
        body,
        grid=(heads,),
        in_specs=in_specs,
        out_specs=out_specs,
        out_shape=out_shape,
        cost_estimate=pl.CostEstimate(flops=flops, bytes_accessed=20_000_000, transcendentals=0),
    )(*operands)


def shaped(*shape, dtype=F32):
    return jax.ShapeDtypeStruct(shape, dtype)


def short_conv(seg_ext, pre_ext, conv_query, conv_key, conv_value):
    kernel = jnp.concatenate([conv_query, conv_key, conv_value], axis=1)
    margin = CONV - 1
    length = pre_ext.shape[0] - margin
    mixed = jnp.zeros((length, kernel.shape[1]), F32)
    for lag in range(CONV):
        offset = margin - lag
        same = (seg_ext[margin:] == seg_ext[offset : offset + length]).astype(F32)
        mixed = mixed + kernel[lag] * pre_ext[offset : offset + length] * same[:, None]
    return jax.nn.silu(mixed)


def decays(segment, before, decay_pre, beta_pre, a_log):
    length = segment.shape[0]
    beta = jax.nn.sigmoid(beta_pre)
    decay_log = -jnp.exp(a_log) * jax.nn.softplus(decay_pre)
    order = jnp.arange(length)
    lower = order[:, None] >= order[None, :]
    running = exact(lower.astype(F32), decay_log).T
    live = (segment[:, None] == segment[None, :]) & lower
    gap = running[:, :, None] - running[:, None, :]
    decay = jnp.where(live, jnp.exp(jnp.where(live, gap, 0.0)), 0.0)
    start = jnp.exp(running) * (segment == before).astype(F32)
    live_last = segment == segment[-1]
    last_gap = running[:, -1:] - running
    tail = jnp.where(live_last, jnp.exp(jnp.where(live_last, last_gap, 0.0)), 0.0)
    return beta.T[:, :, None], decay, start[:, :, None], tail[:, :, None]


def local(
    hidden_in,
    segment_ids,
    grad_out,
    attn_gain,
    w_query,
    w_key,
    w_value,
    w_decay,
    w_beta,
    w_outgate,
    a_log,
    conv_query,
    conv_key,
    conv_value,
    out_gain,
    w_output,
    mlp_gain,
    w_gate,
    w_up,
    w_down,
):
    rows, count = lax.axis_size("dp"), lax.axis_size("zq")
    group = 2 * rows
    inputs = hidden_in[0].astype(F32)
    segment = segment_ids[0]
    grad_low = grad_out[0]
    length, width = inputs.shape
    heads = a_log.shape[0]
    key_width, value_width = w_query.shape[1], w_value.shape[1]
    key_size, value_size = key_width // heads, out_gain.shape[0]
    mixer_width = 2 * key_width + value_width
    hidden_width = w_gate.shape[1]
    owned = w_query.shape[0]
    margin = CONV - 1
    spot = lax.axis_index("zq") * 2 + lax.axis_index("c")
    me = lax.axis_index("dp") * 2 + lax.axis_index("c")
    project_width = (mixer_width + value_width) // group
    ffn_width = hidden_width // group
    back_width = value_width // group

    def shuffled(values):
        return (
            values.reshape(-1, rows, count, 2 * owned).swapaxes(1, 2).reshape(-1, width)
        )

    def unshuffled(values):
        return (
            values.reshape(-1, count, rows, 2 * owned).swapaxes(1, 2).reshape(-1, width)
        )

    def cut(values):
        return values.astype(BF16).reshape(owned, group, -1).swapaxes(0, 1)

    def joined(values):
        return values.swapaxes(0, 1).reshape(values.shape[1], -1)

    small = jnp.concatenate([w_decay, w_beta], axis=1).astype(BF16)
    small = jnp.pad(small, ((0, 0), (0, LANES - 2 * heads)))
    mixer_cut = jnp.concatenate(
        [
            cut(jnp.concatenate([w_query, w_key, w_value, w_outgate], axis=1)),
            jnp.broadcast_to(small[None], (group, owned, LANES)),
        ],
        axis=2,
    )
    ffn_cut = jnp.concatenate([cut(w_output), cut(w_gate), cut(w_up), cut(w_down)], axis=2)
    mixer_own = swap(mixer_cut, 0).reshape(group * owned, -1)
    mixer_weights = lax.all_gather(mixer_own, "zq", axis=0, tiled=True)
    ffn_own = swap(ffn_cut, 1).reshape(group * owned, -1)
    ffn_weights = lax.all_gather(ffn_own, "zq", axis=0, tiled=True)
    project = mixer_weights[:, :project_width]
    small_weights = mixer_weights[:, project_width:]
    output_weights = ffn_weights[:, :back_width]
    gate_up = ffn_weights[:, back_width : back_width + 2 * ffn_width]
    down = ffn_weights[:, back_width + 2 * ffn_width :]

    normed, norm_pull = jax.vjp(rms_scale, inputs)
    normed_low = shuffled((normed * attn_gain).astype(BF16))
    normed_all = spread(normed_low, 2).reshape(-1, width)
    grad_all = spread(shuffled(grad_low), 2).reshape(-1, width)
    projected = mm(normed_all, project).astype(BF16)
    mixed_low = joined(swap(projected.reshape(group, length, project_width), 3))
    pre_low = mixed_low[:, :mixer_width]
    gate_pre = mixed_low[:, mixer_width:]
    small_pre = mm(normed_low, small_weights)
    decay_pre, beta_pre = small_pre[:, :heads], small_pre[:, heads : 2 * heads]

    rim = hop(pre_low[length - 16 :], True, 4)[16 - margin :]
    rim_ids = lax.ppermute(
        segment[-margin:],
        ("zq", "c"),
        [(i, i + 1) for i in range(2 * count - 1)],
    )
    seg_ext = jnp.concatenate([rim_ids, segment])
    pre_ext = jnp.concatenate([rim, pre_low], axis=0).astype(F32)
    active, conv_pull = jax.vjp(
        partial(short_conv, seg_ext), pre_ext, conv_query, conv_key, conv_value
    )
    (beta, decay, start, tail), decay_pull = jax.vjp(
        partial(decays, segment, seg_ext[margin - 1]), decay_pre, beta_pre, a_log
    )
    token_specs = [
        by_columns(length, key_size),
        by_columns(length, key_size, heads),
        by_columns(length, value_size, 2 * key_width // value_size),
        by_head(length, 1),
        by_head(length, length),
        by_head(length, 1),
        by_head(length, 1),
    ]
    token_args = (active, active, active, beta, decay, start, tail)
    values_spec = by_columns(length, value_size)
    state_spec = by_head(key_size, value_size)
    inverse, scores, own, effect, offset, high, low = head_call(
        chunk_forward_kernel,
        heads,
        token_specs,
        [
            by_head(length, length),
            by_head(length, length),
            values_spec,
            by_head(length, key_size),
            state_spec,
            by_head(key_size, key_size),
            by_head(key_size, key_size),
        ],
        [
            shaped(heads, length, length),
            shaped(heads, length, length),
            shaped(length, value_width),
            shaped(heads, length, key_size),
            shaped(heads, key_size, value_size),
            shaped(heads, key_size, key_size, dtype=BF16),
            shaped(heads, key_size, key_size, dtype=BF16),
        ],
        token_args,
        6_000_000_000,
    )
    state = chain(high, low, offset, True, 5)
    gain_spec = pl.BlockSpec((1, value_size), lambda h: (0, 0))
    gain_row = out_gain[None]
    mixed, gated = head_call(
        gate_forward_kernel,
        heads,
        [values_spec, by_head(length, key_size), state_spec, values_spec, gain_spec],
        [values_spec, values_spec],
        [shaped(length, value_width), shaped(length, value_width, dtype=BF16)],
        (own, effect, state, gate_pre, gain_row),
        1_000_000_000,
    )
    gated_cut = gated.reshape(length, group, back_width).swapaxes(0, 1)
    gated_all = swap(gated_cut, 6).reshape(-1, back_width)
    attended = fold(
        mm(gated_all, output_weights, (1, 1)).astype(BF16).reshape(group, length, width), 7
    )
    middle = inputs + unshuffled(attended)

    normed_two, norm_pull_two = jax.vjp(rms_scale, middle)
    normed_two_all = spread(shuffled((normed_two * mlp_gain).astype(BF16)), 2).reshape(-1, width)
    both = mm(normed_two_all, gate_up)
    hidden, swiglu_pull = jax.vjp(swiglu, both[:, :ffn_width], both[:, ffn_width:])
    hidden_low = hidden.astype(BF16)
    grad_gate, grad_up = swiglu_pull(mm(grad_all, down))
    both_grad_low = jnp.concatenate([grad_gate, grad_up], axis=1).astype(BF16)
    grad_normed_two = unshuffled(
        fold(mm(both_grad_low, gate_up, (1, 1)).astype(BF16).reshape(group, length, width), 7)
    )
    mlp_part = fold(mm(hidden_low, down, (1, 1)).astype(BF16).reshape(group, length, width), 7)
    result = (middle + unshuffled(mlp_part)).astype(BF16)
    gate_up_rows = mm(normed_two_all, both_grad_low, (0, 0)).astype(BF16)
    down_rows = mm(grad_all, hidden_low, (0, 0)).astype(BF16)
    grad_mlp_gain = jnp.sum(grad_normed_two * normed_two, axis=0)
    grad_middle = grad_low.astype(F32) + norm_pull_two(grad_normed_two * mlp_gain)[0]

    attended_grad_all = spread(shuffled(grad_middle.astype(BF16)), 2).reshape(-1, width)
    grad_gated_all = mm(attended_grad_all, output_weights).astype(BF16)
    grad_gated = joined(swap(grad_gated_all.reshape(group, length, back_width), 6))
    output_rows = mm(attended_grad_all, gated_all, (0, 0)).astype(BF16)
    ffn_rows = lax.psum_scatter(
        jnp.concatenate([output_rows, gate_up_rows, down_rows], axis=1),
        "zq",
        scatter_dimension=0,
        tiled=True,
    )
    mixed_grad, gate_pre_grad, gain_grad, state_add = head_call(
        gate_backward_kernel,
        heads,
        [values_spec, values_spec, gain_spec, values_spec, by_head(length, key_size)],
        [values_spec, values_spec, by_head(1, value_size), state_spec],
        [
            shaped(length, value_width),
            shaped(length, value_width, dtype=BF16),
            shaped(heads, 1, value_size),
            shaped(heads, key_size, value_size),
        ],
        (mixed, gate_pre, gain_row, grad_gated, effect),
        1_000_000_000,
    )
    grad_out_gain = jnp.sum(gain_grad, axis=(0, 1))
    ending = chain(high, low, state_add, False, 8)
    dq, dk, dv, dbeta, ddecay, dstart, dtail = head_call(
        chunk_backward_kernel,
        heads,
        token_specs
        + [
            by_head(length, length),
            by_head(length, length),
            state_spec,
            values_spec,
            state_spec,
        ],
        [
            values_spec if size == value_size else by_columns(length, size)
            for size in (key_size, key_size, value_size)
        ]
        + [by_head(length, 1), by_head(length, length), by_head(length, 1), by_head(length, 1)],
        [
            shaped(length, key_width),
            shaped(length, key_width),
            shaped(length, value_width),
            shaped(heads, length, 1),
            shaped(heads, length, length),
            shaped(heads, length, 1),
            shaped(heads, length, 1),
        ],
        token_args + (inverse, scores, state, mixed_grad, ending),
        12_000_000_000,
    )
    grad_decay, grad_beta, grad_alog = decay_pull((dbeta, ddecay, dstart, dtail))
    grad_ext, grad_conv_one, grad_conv_two, grad_conv_three = conv_pull(
        jnp.concatenate([dq, dk, dv], axis=1)
    )
    rim_grad = jnp.pad(grad_ext[:margin].astype(BF16), ((16 - margin, 0), (0, 0)))
    returned = hop(rim_grad, False, 9).astype(F32)[16 - margin :]
    grad_pre = grad_ext[margin:].at[length - margin :].add(returned)
    small_grad = jnp.concatenate([grad_decay, grad_beta], axis=1).astype(BF16)
    small_grad = jnp.pad(small_grad, ((0, 0), (0, LANES - 2 * heads)))
    wide_grad = jnp.concatenate([grad_pre.astype(BF16), gate_pre_grad], axis=1)
    grads_cut = jnp.concatenate(
        [
            wide_grad.reshape(length, group, project_width).swapaxes(0, 1),
            jnp.broadcast_to(small_grad[None], (group, length, LANES)),
        ],
        axis=2,
    )
    grads_all = swap(grads_cut, 10).reshape(group * length, -1)
    mixer_rows = lax.psum_scatter(
        mm(normed_all, grads_all, (0, 0)).astype(BF16),
        "zq",
        scatter_dimension=0,
        tiled=True,
    )
    combined = fold(
        mm(grads_all[:, :project_width], project, (1, 1))
        .astype(BF16)
        .reshape(group, length, width),
        7,
    )
    combined = unshuffled(combined + mm(small_grad, small_weights, (1, 1)))
    grad_attn_gain = jnp.sum(combined * normed, axis=0)
    grad_inputs = grad_middle + norm_pull(combined * attn_gain)[0]

    ffn_back = joined_rows(swap(ffn_rows.reshape(group, owned, -1), 1))
    output_grad = joined(ffn_back[:, :, :back_width])
    gate_grad = joined(ffn_back[:, :, back_width : back_width + ffn_width])
    up_grad = joined(ffn_back[:, :, back_width + ffn_width : back_width + 2 * ffn_width])
    down_grad = joined(ffn_back[:, :, back_width + 2 * ffn_width :])
    mixer_parts = mixer_rows.reshape(group, owned, -1)
    mixer_back = joined(joined_rows(swap(mixer_parts, 0))[:, :, :project_width])
    small_rows = lax.dynamic_index_in_dim(mixer_parts, me, 0, keepdims=False)
    small_rows = small_rows[:, project_width:].astype(F32)

    pieces = (
        grad_attn_gain,
        grad_alog,
        grad_conv_one,
        grad_conv_two,
        grad_conv_three,
        grad_out_gain,
        grad_mlp_gain,
    )
    flat = jnp.concatenate([piece.reshape(-1) for piece in pieces])
    lines = -(-flat.shape[0] // (8 * LANES)) * 8
    flat = jnp.pad(flat, (0, lines * LANES - flat.shape[0])).reshape(lines, LANES)
    flat = jnp.sum(spread(flat, 11), axis=0)
    flat = jnp.sum(column(flat, 12), axis=0).reshape(-1)
    summed, at = [], 0
    for piece in pieces:
        summed.append(flat[at : at + piece.size].reshape(piece.shape))
        at += piece.size

    return (
        result[None],
        grad_inputs.astype(BF16)[None],
        summed[0],
        mixer_back[:, :key_width],
        mixer_back[:, key_width : 2 * key_width],
        mixer_back[:, 2 * key_width : mixer_width],
        small_rows[:, :heads],
        small_rows[:, heads : 2 * heads],
        mixer_back[:, mixer_width:],
        summed[1],
        summed[2],
        summed[3],
        summed[4],
        summed[5],
        output_grad,
        summed[6],
        gate_grad,
        up_grad,
        down_grad,
    )


def joined_rows(values):
    return values.astype(F32)


def solution(mesh):
    rows, places = mesh.shape["dp"], mesh.shape["seq"]
    fine = Mesh(mesh.devices.reshape(rows, places // 2, 2), ("dp", "zq", "c"))
    tokens = P("dp", ("zq", "c"), None)
    owned = P(("dp", "zq", "c"), None)
    return jax.shard_map(
        local,
        mesh=fine,
        in_specs=(tokens, P("dp", ("zq", "c")), tokens, P())
        + (owned,) * 6
        + (P(),) * 5
        + (owned, P(), owned, owned, owned),
        out_specs=(tokens, tokens, P())
        + (owned,) * 6
        + (P(),) * 5
        + (owned, P(), owned, owned, owned),
        check_vma=False,
    )
```

time: 4440 us -> 1060 us (0.24)
  waiting for transfers between devices: 2980 us -> 87.5 us
  Pallas kernels: 0 us -> 666 us
  matrix products: 494 us -> 97.1 us
  starting transfers between devices: 254 us -> 2.65 us
  other arithmetic: 327 us -> 80.3 us
  local copies, waits for them, and re-layouts: 251 us -> 98.7 us
  blocking collectives: 80.6 us -> 0 us
    unnamed x13 -> x4, waiting for transfers between devices: 1130 us -> 0.07 us
    reduce_scatter x2, waiting for transfers between devices: 1060 us -> 79.4 us  [the longest x1 79.4 us: local(): lax.psum_scatter(jnp.concatenate([output_rows, gate_up_rows, down_rows],...]
    pallas_call x0 -> x26, Pallas kernels: none -> 666 us  [the longest x22 595 us: comm_call(): pl.pallas_call(body, out_shape=out, in_specs=[spec] * len(operands), out_...]
    ppermute x17 -> x1, waiting for transfers between devices: 441 us -> 0.01 us  [local(): lax.ppermute(segment[-margin:], ('zq', 'c'), [(i, i + 1) for i in range(2...]
    dot_general x86 -> x16, matrix products: 478 us -> 97.1 us  [the longest x14 95.3 us: mm(): lax.dot_general(left, right, (((over[0],), (over[1],)), ((), ())), prefer...]
    ppermute x17 -> x1, starting transfers between devices: 253 us -> 2.49 us  [local(): lax.ppermute(segment[-margin:], ('zq', 'c'), [(i, i + 1) for i in range(2...]
    all_gather x8 -> x2, waiting for transfers between devices: 232 us -> 8.07 us  [the longest x1 8.05 us: local(): ffn_weights = lax.all_gather(ffn_own, 'zq', axis=0, tiled=True)]
    psum x1 -> x0, waiting for transfers between devices: 123 us -> none  [local(): lax.psum((grad_attn_gain, grad_alog, grad_conv_one, grad_conv_two, grad_c...]
  transfers between devices with their start and end apart: 29 -> 5, of which waited for: 23 -> 2; matrix products, arithmetic and copies ran while one was open for 20% -> 13% of each run, Pallas kernels for 0% -> 32%
where the time goes in v1:
time: 1060 us; the launch traced here: 1050 us
  Pallas kernels  666 us (63%)
  local copies, waits for them, and re-layouts  98.7 us (9%)
  matrix products  97.1 us (9%)
  waiting for transfers between devices  87.5 us (8%)
  other arithmetic  80.3 us (8%)
  between operations  15.6 us (1%)
    pallas_call x22, Pallas kernels, comm_call(): pl.pallas_call(body, out_shape=out, in_specs=[spec] * len(operands), out_...  595 us
    dot_general x14, matrix products, mm(): lax.dot_general(left, right, (((over[0],), (over[1],)), ((), ())), prefer...  95.3 us
    reduce_scatter x1, waiting for transfers between devices, local(): lax.psum_scatter(jnp.concatenate([output_rows, gate_up_rows, down_rows],...  79.4 us
    pallas_call x4, Pallas kernels, head_call(): pl.pallas_call(body, grid=(heads,), in_specs=in_specs, out_specs=out_spec...  71.1 us
  transfers between devices with their start and end apart: 5, of which 2 were waited for; matrix products, arithmetic and copies ran while one was open for 13% of the time, Pallas kernels for 32%

profile of v1, /device:TPU:0, one launch (start us, length us, event | category | flops | bytes accessed | tf_op | source)
XLA Modules:
  0.0 1048.3 jit_solution(3266942239256680730)
XLA Ops:
  14.6 19.9 %shard_map.340 = bf16[8,64,1280]{2,1,0:T(8,128)(2,1)} custom-call(bf16[8,64,1280]{2,1,0:T(8,128)(2,1)} %pad_maximum_fusion.6.x_ref), custom_call_target="tpu_custom_call" | custom-call | bytes 90000000 | tf_op jit(solution)/shard_map/pallas_call | solution.py:278
  41.0 5.1 concatenate.54.x_ref
  46.1 32.1 %shard_map.347 = bf16[8,64,2496]{2,1,0:T(8,128)(2,1)} custom-call(bf16[8,64,2496]{2,1,0:T(8,128)(2,1)} %concatenate.54.x_ref), custom_call_target="tpu_custom_call" | custom-call | bytes 90000000 | tf_op jit(solution)/shard_map/pallas_call | solution.py:278
  86.6 29.6 %shard_map.339 = bf16[8,128,2048]{2,1,0:T(8,128)(2,1)} custom-call(bf16[128,2048]{1,0:T(8,128)(2,1)} %reshape.480.x_ref), custom_call_target="tpu_custom_call" | custom-call | bytes 90000000 | tf_op jit(solution)/shard_map/pallas_call | solution.py:278
  116.2 28.7 %shard_map.351 = bf16[8,128,2048]{2,1,0:T(8,128)(2,1)} custom-call(bf16[128,2048]{1,0:T(8,128)(2,1)} %reshape.500.x_ref), custom_call_target="tpu_custom_call" | custom-call | bytes 90000000 | tf_op jit(solution)/shard_map/pallas_call | solution.py:278
  147.3 10.0 fusion.8
  157.3 29.2 %shard_map.341 = bf16[8,128,1152]{2,1,0:T(8,128)(2,1)} custom-call(bf16[8,128,1152]{2,1,0:T(8,128)(2,1)} %bitcast.209), custom_call_target="tpu_custom_call" | custom-call | bytes 90000000 | tf_op jit(solution)/shard_map/pallas_call | solution.py:278
  196.3 3.3 shard_map.342
  203.3 4.1 fusion.24
  207.4 29.8 %shard_map.343 = (f32[6,128,128]{2,1,0:T(8,128)}, f32[6,128,128]{2,1,0:T(8,128)}, f32[128,3072]{1,0:T(8,128)}, f32[6,128,256]{2,1,0:T(8,128)}, f32[6,256,512]{2,...) custom-call(f32[128,6144]{1,0:T(8,128)} %get-tuple-element.158.q_ref.k_ref.v_ref, ...), custom_call_target="tpu_custom_call" | custom-call | flops 6000000000 | bytes 20000000 | tf_op jit(solution)/shard_map/pallas_call | solution.py:566
  237.2 13.9 %shard_map.344.state_ref = bf16[6,256,512]{2,1,0:T(8,128)(2,1)} custom-call(bf16[6,256,256]{2,1,0:T(8,128)(2,1)} %get-tuple-element.53.high_ref, bf16[6,256,256]{2,1,0:T(8,128)(2,1)} %get-tuple-element.54.low_ref, f32[6,256,512]{2,1,0:T(8,128)} %get-tuple-element.55.add_ref), custom_call_target="tpu_custom_call" | custom-call | bytes 90000000 | tf_op jit(solution)/shard_map/pallas_call | solution.py:278
  251.1 6.4 shard_map.345
  262.1 61.9 %shard_map.346 = bf16[8,128,384]{2,1,0:T(8,128)(2,1)} custom-call(bf16[8,128,384]{2,1,0:T(8,128)(2,1)} %bitcast.205), custom_call_target="tpu_custom_call" | custom-call | bytes 90000000 | tf_op jit(solution)/shard_map/pallas_call | solution.py:278
  324.0 8.0 all-gather.5.cloned.1.call-done
  332.0 6.0 convolution_convert_fusion.1
  338.0 29.0 %shard_map.348 = bf16[4,128,2048]{2,1,0:T(8,128)(2,1)} custom-call(bf16[8,128,2048]{2,1,0:T(8,128)(2,1)} %bitcast.197), custom_call_target="tpu_custom_call" | custom-call | bytes 90000000 | tf_op jit(solution)/shard_map/pallas_call | solution.py:278
  367.0 3.0 convert_reduce_fusion.3
  379.8 28.8 %shard_map.349 = bf16[8,128,2048]{2,1,0:T(8,128)(2,1)} custom-call(bf16[128,2048]{1,0:T(8,128)(2,1)} %reshape.495.x_ref), custom_call_target="tpu_custom_call" | custom-call | bytes 90000000 | tf_op jit(solution)/shard_map/pallas_call | solution.py:278
  408.6 10.6 %fusion.2 = f32[1024,1408]{1,0:T(8,128)S(1)} fusion(bf16[1024,2048]{1,0:T(8,128)(2,1)} %bitcast.192, bf16[2048,2496]{1,0:T(8,128)(2,1)} %all-gather.5.cloned.1.call-done), kind=kOutput, calls=%fused_computation.5 | convolution fusion | flops 5905580032 | bytes 15728640 | tf_op jit(solution)/shard_map/dot_general | solution.py:29
  419.3 7.5 fusion.19
  426.8 8.8 fusion.14
  435.6 28.8 %shard_map.352 = bf16[4,128,2048]{2,1,0:T(8,128)(2,1)} custom-call(bf16[8,128,2048]{2,1,0:T(8,128)(2,1)} %bitcast.198), custom_call_target="tpu_custom_call" | custom-call | bytes 90000000 | tf_op jit(solution)/shard_map/pallas_call | solution.py:278
  464.4 3.0 convert_reduce_fusion.1
  473.1 3.1 fusion.42
  478.4 28.8 %shard_map.353 = bf16[8,128,2048]{2,1,0:T(8,128)(2,1)} custom-call(bf16[128,2048]{1,0:T(8,128)(2,1)} %reshape.505.x_ref), custom_call_target="tpu_custom_call" | custom-call | bytes 90000000 | tf_op jit(solution)/shard_map/pallas_call | solution.py:278
  507.2 5.9 convolution_convert_fusion.4
  513.1 12.3 %shard_map.354 = bf16[8,128,384]{2,1,0:T(8,128)(2,1)} custom-call(bf16[8,128,384]{2,1,0:T(8,128)(2,1)} %bitcast.217), custom_call_target="tpu_custom_call" | custom-call | bytes 90000000 | tf_op jit(solution)/shard_map/pallas_call | solution.py:278
  527.5 8.2 shard_map.355
  535.7 75.6 %shard_map.356.ending_ref = bf16[6,256,512]{2,1,0:T(8,128)(2,1)} custom-call(bf16[6,256,256]{2,1,0:T(8,128)(2,1)} %get-tuple-element.53.high_ref, bf16[6,256,256]{2,1,0:T(8,128)(2,1)} %get-tuple-element.54.low_ref, f32[6,256,512]{2,1,0:T(8,128)} %get-tuple-element.61.add_ref), custom_call_target="tpu_custom_call" | custom-call | bytes 90000000 | tf_op jit(solution)/shard_map/pallas_call | solution.py:278
  611.4 26.6 %shard_map.357 = (f32[128,1536]{1,0:T(8,128)}, f32[128,1536]{1,0:T(8,128)}, f32[128,3072]{1,0:T(8,128)}, f32[6,128,1]{2,1,0:T(8,128)}, f32[6,128,128]{2,1,0:T(8,...) custom-call(f32[128,6144]{1,0:T(8,128)} %get-tuple-element.158.q_ref.k_ref.v_ref, ...), custom_call_target="tpu_custom_call" | custom-call | flops 12000000000 | bytes 20000000 | tf_op jit(solution)/shard_map/pallas_call | solution.py:566
  641.1 3.4 multiply_reduce_fusion.3
  657.1 3.1 shard_map.358
  671.8 34.5 %shard_map.359 = bf16[8,128,1280]{2,1,0:T(8,128)(2,1)} custom-call(bf16[8,128,1280]{2,1,0:T(8,128)(2,1)} %pad_maximum_fusion.2.x_ref), custom_call_target="tpu_custom_call" | custom-call | bytes 90000000 | tf_op jit(solution)/shard_map/pallas_call | solution.py:278
  706.3 9.7 bitcast_convert_fusion
  717.2 4.2 bitcast_convert_fusion.1
  721.4 3.8 fusion.25
  725.3 8.3 convolution_convert_fusion
  733.6 16.0 %pad_maximum_fusion = bf16[2048,2496]{0,1:T(8,128)(2,1)} fusion(bf16[2048,704]{0,1:T(8,128)(2,1)S(1)} %fusion.25, bf16[2048,1408]{0,1:T(8,128)(2,1)S(1)} %convolution_convert_fusion, bf16[2048,384]{0,1:T(8,128)(2,1)S(1)} %bitcast_convert_fusion.1), kind=kLoop, calls=%fused_computation.1 | loop fusion | flops 30670848 | bytes 20447232 | tf_op jit(solution)/shard_map/concatenate | solution.py:789
  752.4 9.6 fusion.11
  762.0 29.3 %shard_map.360 = bf16[4,128,2048]{2,1,0:T(8,128)(2,1)} custom-call(bf16[8,128,2048]{2,1,0:T(8,128)(2,1)} %bitcast.196), custom_call_target="tpu_custom_call" | custom-call | bytes 90000000 | tf_op jit(solution)/shard_map/pallas_call | solution.py:278
  796.9 10.5 shard_map.361
  809.3 17.6 %shard_map.362 = f32[4,232,128]{2,1,0:T(8,128)} custom-call(f32[232,128]{1,0:T(8,128)} %reduce_sum.271.x_ref), custom_call_target="tpu_custom_call" | custom-call | bytes 90000000 | tf_op jit(solution)/shard_map/pallas_call | solution.py:278
  832.6 8.0 convolution_convert_fusion.2
  840.6 28.5 %shard_map.350 = bf16[4,128,2048]{2,1,0:T(8,128)(2,1)} custom-call(bf16[8,128,2048]{2,1,0:T(8,128)(2,1)} %bitcast.195), custom_call_target="tpu_custom_call" | custom-call | bytes 90000000 | tf_op jit(solution)/shard_map/pallas_call | solution.py:278
  882.7 17.8 %shard_map.363 = bf16[8,64,1280]{2,1,0:T(8,128)(2,1)} custom-call(bf16[8,64,1280]{2,1,0:T(8,128)(2,1)} %bitcast.211), custom_call_target="tpu_custom_call" | custom-call | bytes 90000000 | tf_op jit(solution)/shard_map/pallas_call | solution.py:278
  906.8 79.4 %reduce-scatter.5.cloned.1.call-done = bf16[512,2496]{0,1:T(8,128)(2,1)} async-done(((bf16[2048,2496]{0,1:T(8,128)(2,1)}), bf16[512,2496]{0,1:T(8,128)(2,1)}) %reduce-scatter.5.cloned.1.call-update) | async-done | bytes 2555920 | tf_op jit(solution)/shard_map/reduce_scatter | solution.py:788
  986.2 4.6 copy.230
  990.8 32.4 %shard_map.364 = bf16[8,64,2496]{2,1,0:T(8,128)(2,1)} custom-call(bf16[8,64,2496]{2,1,0:T(8,128)(2,1)} %bitcast.174), custom_call_target="tpu_custom_call" | custom-call | bytes 90000000 | tf_op jit(solution)/shard_map/pallas_call | solution.py:278
  (301 shorter events, 144.2 us)
Async XLA Ops:
  7.2 140.1 %all-gather.3.cloned.1.call-start = ((), (), s32[]{:S(2)}) async-start(), calls=%async_computation.2 | async-start | bytes 6553600 | tf_op jit(solution)/shard_map/all_gather | solution.py:677
  13.4 21.1 %copy-start.19 = (f32[64,3072]{1,0:T(8,128)S(1)}, f32[64,3072]{1,0:T(8,128)}, u32[]{:S(2)}) copy-start(f32[64,3072]{1,0:T(8,128)} %param.37) | copy-start | bytes 2359300
  14.6 20.1 %copy-start.18 = (f32[64,5632]{1,0:T(8,128)S(1)}, f32[64,5632]{1,0:T(8,128)}, u32[]{:S(2)}) copy-start(f32[64,5632]{1,0:T(8,128)} %param.39) | copy-start | bytes 4325380
  34.5 297.5 %all-gather.5.cloned.1.call-start = ((), (), s32[]{:S(2)}) async-start(), calls=%async_computation.3 | async-start | bytes 13107200 | tf_op jit(solution)/shard_map/all_gather | solution.py:679
  46.1 32.2 %copy-start.39 = (s32[1,128]{1,0:T(1,128)S(1)}, s32[1,128]{1,0:T(1,128)}, u32[]{:S(2)}) copy-start(s32[1,128]{1,0:T(1,128)} %param.23) | copy-start | bytes 1540
  46.1 35.4 %copy-start.29 = (f32[2048]{0:T(1024)S(1)}, f32[2048]{0:T(1024)}, u32[]{:S(2)}) copy-start(f32[2048]{0:T(1024)} %param.38) | copy-start | bytes 24580
  46.1 35.4 %copy-start.26 = (f32[2048]{0:T(1024)S(1)}, f32[2048]{0:T(1024)}, u32[]{:S(2)}) copy-start(f32[2048]{0:T(1024)} %param.25) | copy-start | bytes 24580
  46.1 35.4 %copy-start.21 = (bf16[1,128,2048]{2,1,0:T(8,128)(2,1)S(1)}, bf16[1,128,2048]{2,1,0:T(8,128)(2,1)}, u32[]{:S(2)}) copy-start(bf16[1,128,2048]{2,1,0:T(8,128)(2,1)} %param.22) | copy-start | bytes 1572868
  78.2 3.6 copy-start.15
  78.3 804.5 %reduce-scatter.3.cloned.1.call-start = ((), (), s32[]{:S(2)}) async-start(), calls=%async_computation.4 | async-start | bytes 6553600 | tf_op jit(solution)/shard_map/reduce_scatter | solution.py:856
  78.4 66.8 %collective-permute-start = (s32[3]{0:T(128)S(1)}, s32[3]{0:T(128)S(1)}, u32[]{:S(2)}, u32[]{:S(2)}) collective-permute-start(s32[3]{0:T(128)S(1)} %slice_bitcast_fusion.5), channel_id=1, source_target_pairs={{0,1},{1,2},{2,3},{3,4},{4,5},{5,6},{6,7},{8,9},{9,10},{10,11},{11... | collective-permute-start | bytes 44 | tf_op jit(solution)/shard_map/ppermute | solution.py:698
  81.8 3.6 copy-start.4
  84.1 32.0 %copy-start = (f32[128,4,4,128]{3,1,2,0:T(4,128)}, f32[128,4,4,128]{3,1,2,0:T(4,128)S(1)}, u32[]{:S(2)}) copy-start(f32[128,4,4,128]{3,1,2,0:T(4,128)S(1)} %copy.191) | copy-start | bytes 3145732
  85.1 31.1 %copy-start.42 = (f32[128]{0:T(128)}, f32[128]{0:T(128)S(1)}, u32[]{:S(2)}) copy-start(f32[128]{0:T(128)S(1)} %fusion.84) | copy-start | bytes 1540
  116.2 28.8 %copy-start.54 = (f32[6]{0:T(128)S(1)}, f32[6]{0:T(128)}, u32[]{:S(2)}) copy-start(f32[6]{0:T(128)} %param.32) | copy-start | bytes 76
  116.2 28.9 %copy-start.32 = (f32[4,1536]{1,0:T(4,128)S(1)}, f32[4,1536]{1,0:T(4,128)}, u32[]{:S(2)}) copy-start(f32[4,1536]{1,0:T(4,128)} %param.33) | copy-start | bytes 73732
  116.2 28.9 %copy-start.33 = (f32[4,1536]{1,0:T(4,128)S(1)}, f32[4,1536]{1,0:T(4,128)}, u32[]{:S(2)}) copy-start(f32[4,1536]{1,0:T(4,128)} %param.34) | copy-start | bytes 73732
  116.2 28.9 %copy-start.28 = (f32[4,3072]{1,0:T(4,128)S(1)}, f32[4,3072]{1,0:T(4,128)}, u32[]{:S(2)}) copy-start(f32[4,3072]{1,0:T(4,128)} %param.35) | copy-start | bytes 147460
  145.0 47.9 %copy-start.57 = (f32[6]{0:T(128)}, f32[6]{0:T(128)S(1)}, u32[]{:S(2)}) copy-start(f32[6]{0:T(128)S(1)} %exponential_negate_fusion) | copy-start | bytes 76
  145.1 55.4 %copy-start.23 = (pred[128,128]{1,0:T(8,128)(4,1)}, pred[128,128]{1,0:T(8,128)(4,1)S(1)}, u32[]{:S(2)}) copy-start(pred[128,128]{1,0:T(8,128)(4,1)S(1)} %fusion.53) | copy-start | bytes 49156
  146.5 46.7 %copy-start.52 = (f32[128]{0:T(128)}, f32[128]{0:T(128)S(1)}, u32[]{:S(2)}) copy-start(f32[128]{0:T(128)S(1)} %fusion.83) | copy-start | bytes 1540
  147.3 46.0 %copy-start.44 = (pred[128]{0:T(512)(128)(4,1)}, pred[128]{0:T(512)(128)(4,1)S(1)}, u32[]{:S(2)}) copy-start(pred[128]{0:T(512)(128)(4,1)S(1)} %get-tuple-element.194) | copy-start | bytes 388
  147.3 56.0 %copy-start.35 = (f32[128]{0:T(128)}, f32[128]{0:T(128)S(1)}, u32[]{:S(2)}) copy-start(f32[128]{0:T(128)S(1)} %get-tuple-element.192) | copy-start | bytes 1540
  147.3 56.0 %copy-start.37 = (f32[128]{0:T(128)}, f32[128]{0:T(128)S(1)}, u32[]{:S(2)}) copy-start(f32[128]{0:T(128)S(1)} %get-tuple-element.193) | copy-start | bytes 1540
  192.9 7.6 copy-start.25
  193.3 10.0 copy-start.46
  375.5 97.6 %copy-start.40 = (f32[128]{0:T(128)}, f32[128]{0:T(128)S(1)}, u32[]{:S(2)}) copy-start(f32[128]{0:T(128)S(1)} %fusion.85) | copy-start | bytes 1540
  408.6 10.7 %copy-start.10 = (bf16[8,128,2048]{2,1,0:T(8,128)(2,1)S(1)}, bf16[8,128,2048]{2,1,0:T(8,128)(2,1)}, u32[]{:S(2)}) copy-start(bf16[8,128,2048]{2,1,0:T(8,128)(2,1)} %shard_map.351) | copy-start | bytes 12582916
  408.6 18.2 %slice-start = ((s8[10485760]{0:T(1024)(128)(4,1)}), s8[4194304]{0:T(1024)(128)(4,1)S(1)}, s32[]{:S(2)}) async-start(s8[10485760]{0:T(1024)(128)(4,1)} %bitcast.249), calls=%async_computation.6 | async-start | bytes 8388608
  408.6 18.1 %slice-start.1 = ((s8[10485760]{0:T(1024)(128)(4,1)}), s8[4194304]{0:T(1024)(128)(4,1)S(1)}, s32[]{:S(2)}) async-start(s8[10485760]{0:T(1024)(128)(4,1)} %bitcast.249), calls=%async_computation.7 | async-start | bytes 8388608
  419.2 7.5 slice-start.2
  426.7 8.8 copy-start.60
  426.7 8.8 copy-start.62
  473.1 34.1 %copy-start.48 = (f32[128]{0:T(128)}, f32[128]{0:T(128)S(1)}, u32[]{:S(2)}) copy-start(f32[128]{0:T(128)S(1)} %multiply_multiply_fusion.4) | copy-start | bytes 1540
  647.5 5.7 copy-start.53
  647.6 5.7 copy-start.58
  716.1 5.3 copy-start.59
  716.1 270.1 %reduce-scatter.5.cloned.1.call-start = ((), (), s32[]{:S(2)}) async-start(), calls=%async_computation.5 | async-start | bytes 12779520 | tf_op jit(solution)/shard_map/reduce_scatter | solution.py:788
  717.2 4.2 copy-start.11
  721.4 3.9 copy-start.12
  721.4 3.9 copy-start.61
  721.4 3.9 copy-start.63
  795.7 34.2 %copy-start.7 = (f32[128,4,4,128]{3,2,1,0:T(4,128)S(1)}, f32[128,4,4,128]{3,2,1,0:T(4,128)}, u32[]{:S(2)}) copy-start(f32[128,4,4,128]{3,2,1,0:T(4,128)} %reshape.493) | copy-start | bytes 3145732
  796.0 35.2 %copy-start.3 = (f32[128,4,4,128]{3,2,1,0:T(4,128)S(1)}, f32[128,4,4,128]{3,2,1,0:T(4,128)}, u32[]{:S(2)}) copy-start(f32[128,4,4,128]{3,2,1,0:T(4,128)} %reshape.503) | copy-start | bytes 3145732
  871.3 4.2 copy-start.5
  871.3 4.2 copy-start.27
  872.6 3.3 copy-start.41
  872.6 3.3 copy-start.49
  (24 other events, 57.2 us)
Sparse Core Ops, SparseCore 0:
  34.6 98.8 all-gather.2
  135.1 196.9 all-gather.4
  716.2 91.8 reduce-scatter.2
  810.3 175.8 reduce-scatter.4

commit v2 on v1

--- a/solution.py
+++ b/solution.py
@@ -15,6 +15,9 @@
 F32 = jnp.float32
 BY_MESH = pl.DeviceIdType.MESH
 LANES = 128
+PIECES = 2
+CHUNKS = 2
+RIM = 16
 
 
 def rms_scale(values):
@@ -159,6 +162,496 @@
         copy.wait()
 
 
+def slab_pieces(widths, slab, t):
+    at, end, base = t * slab, (t + 1) * slab, 0
+    for source, width in enumerate(widths):
+        low, high = max(at, base), min(end, base + width)
+        if low < high:
+            yield source, low - base, low - at, high - low
+        base += width
+
+
+def start_kernel(rows, count, hidden_ref, grad_ref, gain_ref, decay_ref, beta_ref, *refs):
+    weight_refs = refs[:8]
+    all_ref, *side_outs = refs[8:11]
+    one_out_ref, two_out_ref, hidden_out_ref, one_ref, two_ref = refs[11:16]
+    raws, cut_ref, sides = refs[16:24], refs[24], refs[25:27]
+    (
+        load,
+        own,
+        deal_send,
+        deal_recv,
+        side_send,
+        side_recv,
+        round_send,
+        round_recv,
+        pair_send,
+        pair_recv,
+        up_send,
+        up_recv,
+        down_send,
+        down_recv,
+    ) = refs[27:]
+    loads = [
+        pltpu.make_async_copy(weight, raw, load.at[i])
+        for i, (weight, raw) in enumerate(zip(weight_refs, raws))
+    ]
+    for copy in loads:
+        copy.start()
+    d, z, c = place()
+    me = d * 2 + c
+    group = 2 * rows
+    pair = (d, z, 1 - c)
+    others = [(lax.rem(d + k, rows), z, c) for k in range(1, rows)]
+    above = (d, lax.rem(z + 1, count), c)
+    below = (d, lax.rem(z + count - 1, count), c)
+    has_above, has_below = z < count - 1, z > 0
+    offsets = plane_offsets(rows)
+    barrier = pltpu.get_barrier_semaphore()
+    for offset in offsets:
+        pl.semaphore_signal(
+            barrier, inc=1, device_id=plane_peer(offset, rows), device_id_type=BY_MESH
+        )
+
+    @pl.when(has_above)
+    def _():
+        pl.semaphore_signal(barrier, inc=1, device_id=above, device_id_type=BY_MESH)
+
+    @pl.when(has_below)
+    def _():
+        pl.semaphore_signal(barrier, inc=1, device_id=below, device_id_type=BY_MESH)
+
+    owned = raws[0].shape[0]
+    wide = cut_ref.shape[2]
+    heads = decay_ref.shape[1]
+    back = raws[3].shape[1] // group
+    slab = wide - LANES - back
+    for copy in loads[:4]:
+        copy.wait()
+    widths = [raw.shape[1] for raw in raws[:3]]
+    for t in range(group):
+        for source, at, to, size in slab_pieces(widths, slab, t):
+            cut_ref[t, :, to : to + size] = raws[source][:, at : at + size].astype(BF16)
+        cut_ref[t, :, slab : slab + back] = raws[3][:, t * back : (t + 1) * back].astype(BF16)
+        cut_ref[t, :, slab + back :] = jnp.concatenate(
+            [decay_ref[...], beta_ref[...], jnp.zeros((owned, LANES - 2 * heads), F32)], axis=1
+        ).astype(BF16)
+    pl.semaphore_wait(
+        barrier, len(offsets) + has_above.astype(jnp.int32) + has_below.astype(jnp.int32)
+    )
+
+    def deal(source, target, send, recv):
+        copies = []
+        for i, offset in enumerate(offsets):
+            peer = plane_peer(offset, rows)
+            copy = remote(
+                source.at[peer[0] * 2 + peer[2]], target.at[me], send.at[i], recv.at[i], peer
+            )
+            copy.start()
+            copies.append(copy)
+        return copies
+
+    def origin(offset):
+        k, flip = offset
+        return lax.rem(d + rows - k, rows) * 2 + (1 - c if flip else c)
+
+    def passed(k, i, block, upward):
+        at = z - k if upward else z + k
+        at = lax.rem(at + count, count)
+        send, recv = (up_send, up_recv) if upward else (down_send, down_recv)
+        return remote(
+            all_ref.at[at, block],
+            all_ref.at[at, block],
+            send.at[k, i],
+            recv.at[k, i],
+            above if upward else below,
+        )
+
+    def give(k, i, block):
+        @pl.when(has_above & (z - k >= 0))
+        def _():
+            passed(k, i, block, True).start()
+
+        @pl.when(has_below & (z + k <= count - 1))
+        def _():
+            passed(k, i, block, False).start()
+
+    def take(k, i, block):
+        @pl.when(z - k - 1 >= 0)
+        def _():
+            passed(k, i, block, True).wait_recv()
+
+        @pl.when(z + k + 1 <= count - 1)
+        def _():
+            passed(k, i, block, False).wait_recv()
+
+    def given(k, i, block):
+        @pl.when(has_above & (z - k >= 0))
+        def _():
+            passed(k, i, block, True).wait_send()
+
+        @pl.when(has_below & (z + k <= count - 1))
+        def _():
+            passed(k, i, block, False).wait_send()
+
+    dealt = deal(cut_ref, all_ref.at[z], deal_send, deal_recv)
+    keep = pltpu.make_async_copy(cut_ref.at[me], all_ref.at[z, me], own.at[0])
+    keep.start()
+    keep.wait()
+    blocks = [me] + [origin(offset) for offset in offsets]
+    give(0, 0, me)
+    run = 2 * owned
+    width = hidden_ref.shape[1]
+
+    def moved(values):
+        return jnp.concatenate(
+            [
+                values[:, (b * count + a) * run : (b * count + a + 1) * run]
+                for a in range(count)
+                for b in range(rows)
+            ],
+            axis=1,
+        )
+
+    hidden = moved(hidden_ref[...])
+    hidden_out_ref[...] = hidden
+    one_ref[...] = (rms_scale(hidden.astype(F32)) * moved(gain_ref[...])).astype(BF16)
+    two_ref[...] = moved(grad_ref[...])
+    rounds = []
+    for j, (source, target) in enumerate(((one_ref, one_out_ref), (two_ref, two_out_ref))):
+        copies = []
+        for i, peer in enumerate(others):
+            copies.append(
+                remote(source, target.at[me], round_send.at[j, i], round_recv.at[j, i], peer)
+            )
+        copies.append(
+            remote(source, target.at[me], pair_send.at[j, 0], pair_recv.at[j, 0], pair)
+        )
+        rounds.append(copies)
+    for i, copy in enumerate(dealt):
+        copy.wait_recv()
+        give(0, i + 1, blocks[i + 1])
+    keeps = [
+        pltpu.make_async_copy(one_ref, one_out_ref.at[me], own.at[1]),
+        pltpu.make_async_copy(two_ref, two_out_ref.at[me], own.at[2]),
+    ]
+    for copy in rounds[0] + keeps:
+        copy.start()
+    for copy in loads[4:]:
+        copy.wait()
+    deals = []
+    for j, (laid, side, side_out) in enumerate(zip((raws[4:6], raws[6:]), sides, side_outs)):
+        for t in range(group):
+            at = 0
+            for raw in laid:
+                size = raw.shape[1] // group
+                side[t, :, at : at + size] = raw[:, t * size : (t + 1) * size].astype(BF16)
+                at += size
+        deals += deal(side, side_out, side_send.at[j], side_recv.at[j])
+        keep = pltpu.make_async_copy(side.at[me], side_out.at[me], own.at[3 + j])
+        keep.start()
+        keeps.append(keep)
+    for copy in rounds[1]:
+        copy.start()
+    hands = []
+    for k in range(count - 1):
+        for i, block in enumerate(blocks):
+            take(k, i, block)
+            if k < count - 2:
+                give(k + 1, i, block)
+        if k < 2:
+            target = (one_out_ref, two_out_ref)[k]
+            for i, copy in enumerate(rounds[k][:-1]):
+                copy.wait_recv()
+                at = lax.rem(d + rows - (i + 1), rows) * 2 + c
+                hand = remote(
+                    target.at[at], target.at[at], pair_send.at[k, i + 1], pair_recv.at[k, i + 1], pair
+                )
+                hand.start()
+                hands.append(hand)
+    for copy in keeps:
+        copy.wait()
+    for copy in dealt:
+        copy.wait_send()
+    for copies in rounds:
+        for copy in copies[:-1]:
+            copy.wait_send()
+        copies[-1].wait()
+    for copy in hands + deals:
+        copy.wait()
+    for k in range(count - 1):
+        for i, block in enumerate(blocks):
+            given(k, i, block)
+
+
+def turn_kernel(rows, backward, x_ref, gain_ref, base_ref, *refs):
+    if backward:
+        out_ref, all_ref, sums_ref = refs[1:4]
+        gain_grad_ref, middle_ref = sums_ref, refs[0]
+        scratch = refs[4:]
+    else:
+        out_ref, all_ref = refs[:2]
+        scratch = refs[2:]
+    (
+        mine,
+        theirs,
+        land,
+        low,
+        load,
+        fold_pair_send,
+        fold_pair_recv,
+        fold_send,
+        fold_recv,
+        own,
+        send,
+        recv,
+        pair_send,
+        pair_recv,
+    ) = scratch
+    d, z, c = place()
+    me = d * 2 + c
+    pair = (d, z, 1 - c)
+    others = [(lax.rem(d + k, rows), z, c) for k in range(1, rows)]
+    greet(others + [pair])
+    order = [lax.rem(d + k, rows) for k in range(1, rows)] + [d]
+    step = x_ref.shape[1] // CHUNKS
+    parts = [pl.ds(j * step, step) for j in range(CHUNKS)]
+    hands, loads = {}, {}
+    for j, part in enumerate(parts):
+        for i, to in enumerate(order):
+            hands[j, i] = remote(
+                x_ref.at[to * 2 + (1 - c), part],
+                theirs.at[i, part],
+                fold_pair_send.at[j, i],
+                fold_pair_recv.at[j, i],
+                pair,
+            )
+            hands[j, i].start()
+            loads[j, i] = pltpu.make_async_copy(
+                x_ref.at[to * 2 + c, part], mine.at[i, part], load.at[j, i]
+            )
+            loads[j, i].start()
+    folds = {}
+    for j, part in enumerate(parts):
+        for i in range(rows):
+            loads[j, i].wait()
+            hands[j, i].wait_recv()
+            if i < rows - 1:
+                mine[i, part] = (mine[i, part].astype(F32) + theirs[i, part].astype(F32)).astype(
+                    BF16
+                )
+                folds[j, i] = remote(
+                    mine.at[i, part],
+                    land.at[i, part],
+                    fold_send.at[j, i],
+                    fold_recv.at[j, i],
+                    others[i],
+                )
+                folds[j, i].start()
+    gain = gain_ref[...]
+    sends, keeps = {}, []
+    if backward:
+        sums_ref[...] = jnp.zeros_like(sums_ref)
+    for j, part in enumerate(parts):
+        total = mine[rows - 1, part].astype(F32) + theirs[rows - 1, part].astype(F32)
+        for i in range(rows - 1):
+            folds[j, i].wait_recv()
+            total = total + land[i, part].astype(F32)
+        if backward:
+            middle = middle_ref[part, :]
+            scale = lax.rsqrt(jnp.mean(middle * middle, axis=-1, keepdims=True) + EPSILON)
+            normed = middle * scale
+            sums_ref[...] += jnp.sum(total * normed, axis=0, keepdims=True)
+            inner = total * gain
+            result = base_ref[part, :].astype(F32) + scale * (
+                inner - normed * jnp.mean(inner * normed, axis=-1, keepdims=True)
+            )
+            out_ref[part, :] = result
+            low[part, :] = result.astype(BF16)
+        else:
+            result = base_ref[part, :].astype(F32) + total
+            out_ref[part, :] = result
+            low[part, :] = (rms_scale(result) * gain).astype(BF16)
+        for i, peer in enumerate(others + [pair]):
+            at = (send.at[j, i], recv.at[j, i])
+            if i == rows - 1:
+                at = (pair_send.at[j, rows - 1], pair_recv.at[j, rows - 1])
+            sends[j, i] = remote(low.at[part], all_ref.at[me, part], *at, peer)
+            sends[j, i].start()
+        keep = pltpu.make_async_copy(low.at[part], all_ref.at[me, part], own.at[j])
+        keep.start()
+        keeps.append(keep)
+    for j, part in enumerate(parts):
+        for i in range(rows - 1):
+            sends[j, i].wait_recv()
+            at = lax.rem(d + rows - (i + 1), rows) * 2 + c
+            hand = remote(
+                all_ref.at[at, part],
+                all_ref.at[at, part],
+                pair_send.at[j, i],
+                pair_recv.at[j, i],
+                pair,
+            )
+            hand.start()
+            hands[j, rows + i] = hand
+    for keep in keeps:
+        keep.wait()
+    for (j, i), hand in hands.items():
+        hand.wait_send()
+        if i >= rows:
+            hand.wait_recv()
+    for copy in folds.values():
+        copy.wait_send()
+    for (j, i), copy in sends.items():
+        copy.wait_send()
+        if i == rows - 1:
+            copy.wait_recv()
+
+
+def greet_plane_and_line(rows, count):
+    d, z, c = place()
+    spot, before, after = neighbours(count)
+    offsets = plane_offsets(rows)
+    lower, upper = (c == 0) & (z > 0), (c == 1) & (z < count - 1)
+    barrier = pltpu.get_barrier_semaphore()
+    for offset in offsets:
+        pl.semaphore_signal(
+            barrier, inc=1, device_id=plane_peer(offset, rows), device_id_type=BY_MESH
+        )
+
+    @pl.when(lower)
+    def _():
+        pl.semaphore_signal(barrier, inc=1, device_id=before, device_id_type=BY_MESH)
+
+    @pl.when(upper)
+    def _():
+        pl.semaphore_signal(barrier, inc=1, device_id=after, device_id_type=BY_MESH)
+
+    pl.semaphore_wait(
+        barrier, len(offsets) + lower.astype(jnp.int32) + upper.astype(jnp.int32)
+    )
+
+
+def swap_on_kernel(rows, count, x_ref, o_ref, rim_ref, land, own, send, recv, rim_send, rim_recv):
+    d, z, c = place()
+    me = d * 2 + c
+    spot, before, after = neighbours(count)
+    greet_plane_and_line(rows, count)
+    copies = []
+    for i, offset in enumerate(plane_offsets(rows)):
+        peer = plane_peer(offset, rows)
+        copy = remote(
+            x_ref.at[peer[0] * 2 + peer[2]], o_ref.at[me], send.at[i], recv.at[i], peer
+        )
+        copy.start()
+        copies.append(copy)
+    keep = pltpu.make_async_copy(x_ref.at[me], o_ref.at[me], own)
+    keep.start()
+    keep.wait()
+    for copy in copies:
+        copy.wait_recv()
+    size = x_ref.shape[1]
+    rim = remote(o_ref.at[:, pl.ds(size - RIM, RIM)], land, rim_send, rim_recv, after)
+    gives, takes = spot < 2 * count - 1, spot > 0
+
+    @pl.when(gives)
+    def _():
+        rim.start()
+
+    @pl.when(takes)
+    def _():
+        rim.wait_recv()
+
+    @pl.when(jnp.logical_not(takes))
+    def _():
+        land[...] = jnp.zeros_like(land)
+
+    rim_ref[...] = land[...]
+    for copy in copies:
+        copy.wait_send()
+
+    @pl.when(gives)
+    def _():
+        rim.wait_send()
+
+
+def swap_back_kernel(
+    rows,
+    count,
+    x_ref,
+    tail_ref,
+    rim_ref,
+    small_ref,
+    o_ref,
+    land,
+    fixed,
+    own,
+    send,
+    recv,
+    rim_send,
+    rim_recv,
+):
+    d, z, c = place()
+    me = d * 2 + c
+    spot, before, after = neighbours(count)
+    greet_plane_and_line(rows, count)
+    size, part = x_ref.shape[1:]
+    wide = o_ref.shape[2]
+    rim = remote(rim_ref, land, rim_send, rim_recv, before)
+    gives, takes = spot > 0, spot < 2 * count - 1
+
+    @pl.when(gives)
+    def _():
+        rim.start()
+
+    body, end = pl.ds(0, size - RIM), pl.ds(size - RIM, RIM)
+    left, right = pl.ds(0, part), pl.ds(part, wide - part)
+    copies = []
+    for i, offset in enumerate(plane_offsets(rows)):
+        peer = plane_peer(offset, rows)
+        to = peer[0] * 2 + peer[2]
+        copies.append(
+            (
+                remote(
+                    x_ref.at[to, body], o_ref.at[me, body, left], send.at[0, i], recv.at[0, i], peer
+                ),
+                remote(small_ref, o_ref.at[me, :, right], send.at[1, i], recv.at[1, i], peer),
+                remote(fixed.at[to], o_ref.at[me, end, left], send.at[2, i], recv.at[2, i], peer),
+            )
+        )
+        copies[-1][0].start()
+        copies[-1][1].start()
+    keeps = [
+        pltpu.make_async_copy(x_ref.at[me, body], o_ref.at[me, body, left], own.at[0]),
+        pltpu.make_async_copy(small_ref, o_ref.at[me, :, right], own.at[1]),
+        pltpu.make_async_copy(fixed.at[me], o_ref.at[me, end, left], own.at[2]),
+    ]
+    keeps[0].start()
+    keeps[1].start()
+
+    @pl.when(takes)
+    def _():
+        rim.wait_recv()
+
+    @pl.when(jnp.logical_not(takes))
+    def _():
+        land[...] = jnp.zeros_like(land)
+
+    fixed[...] = (tail_ref[...] + land[...].astype(F32)).astype(BF16)
+    keeps[2].start()
+    for group in copies:
+        group[2].start()
+    for keep in keeps:
+        keep.wait()
+    for group in copies:
+        for copy in group:
+            copy.wait()
+
+    @pl.when(gives)
+    def _():
+        rim.wait_send()
+
+
 def column_kernel(count, x_ref, o_ref, own, send, recv):
     d, z, c = place()
     others = [(d, lax.rem(z + k, count), c) for k in range(1, count)]
@@ -228,46 +721,105 @@
 
 
 def chain_kernel(
-    count, heads, forward, high_ref, low_ref, add_ref, o_ref, land, stage, send, recv
+    count,
+    rows,
+    heads,
+    sides,
+    forward,
+    high_ref,
+    low_ref,
+    add_ref,
+    *refs,
 ):
+    side_refs, (o_ref, *side_out_refs) = refs[:sides], refs[sides : 2 * sides + 1]
+    land, stage, send, recv, own, side_send, side_recv = refs[2 * sides + 1 :]
+    d, z, c = place()
+    me = d * 2 + c
     spot, before, after = neighbours(count)
-    greet_chain(count)
+    offsets = plane_offsets(rows)
+    barrier = pltpu.get_barrier_semaphore()
+    for offset in offsets:
+        pl.semaphore_signal(
+            barrier, inc=1, device_id=plane_peer(offset, rows), device_id_type=BY_MESH
+        )
+
+    @pl.when((c == 0) & (z > 0))
+    def _():
+        pl.semaphore_signal(barrier, inc=1, device_id=before, device_id_type=BY_MESH)
+
+    @pl.when((c == 1) & (z < count - 1))
+    def _():
+        pl.semaphore_signal(barrier, inc=1, device_id=after, device_id_type=BY_MESH)
+
+    pl.semaphore_wait(
+        barrier,
+        len(offsets)
+        + ((c == 0) & (z > 0)).astype(jnp.int32)
+        + ((c == 1) & (z < count - 1)).astype(jnp.int32),
+    )
+    waits = []
+    for j in range(sides):
+        for i, offset in enumerate(offsets):
+            peer = plane_peer(offset, rows)
+            waits.append(
+                remote(
+                    side_refs[j].at[peer[0] * 2 + peer[2]],
+                    side_out_refs[j].at[me],
+                    side_send.at[j, i],
+                    side_recv.at[j, i],
+                    peer,
+                )
+            )
+        waits.append(
+            pltpu.make_async_copy(side_refs[j].at[me], side_out_refs[j].at[me], own.at[j])
+        )
+    for copy in waits:
+        copy.start()
     if forward:
         gives, takes, to = spot < 2 * count - 1, spot > 0, after
     else:
         gives, takes, to = spot > 0, spot < 2 * count - 1, before
-    over = (1, 0) if forward else (0, 0)
+    part = o_ref.shape[2] // PIECES
     copies = [
-        remote(stage.at[h], land.at[h], send.at[h], recv.at[h], to) for h in range(heads)
+        remote(stage.at[i], land.at[i], send.at[i], recv.at[i], to)
+        for i in range(heads * PIECES)
     ]
     for h in range(heads):
-
-        @pl.when(jnp.logical_not(takes))
-        def _():
-            land[h] = jnp.zeros_like(land[h])
-
-        @pl.when(takes)
-        def _():
-            copies[h].wait_recv()
+        for j in range(PIECES):
+            i = h * PIECES + j
+            columns = slice(j * part, (j + 1) * part)
+
+            @pl.when(jnp.logical_not(takes))
+            def _():
+                land[i] = jnp.zeros_like(land[i])
+
+            @pl.when(takes)
+            def _():
+                copies[i].wait_recv()
+
+            @pl.when(gives)
+            def _():
+                state = land[i]
+                leaving = add_ref[h, :, columns] + mm(high_ref[h], state) + mm(low_ref[h], state)
+                stage[i] = leaving.astype(BF16)
+                copies[i].start()
+
+    for copy in copies:
 
         @pl.when(gives)
         def _():
-            state = land[h]
-            leaving = add_ref[h] + mm(high_ref[h], state, over) + mm(low_ref[h], state, over)
-            stage[h] = leaving.astype(BF16)
-            copies[h].start()
+            copy.wait_send()
 
     for h in range(heads):
-
-        @pl.when(gives)
-        def _():
-            copies[h].wait_send()
-
-    o_ref[...] = land[...]
+        for j in range(PIECES):
+            o_ref[h, :, j * part : (j + 1) * part] = land[h * PIECES + j]
+    for copy in waits:
+        copy.wait()
 
 
 ANY = pl.BlockSpec(memory_space=pl.ANY)
 IN_VMEM = pl.BlockSpec(memory_space=pltpu.VMEM)
+IN_HBM = pl.BlockSpec(memory_space=pltpu.HBM)
 
 
 def dma(*shape):
@@ -333,6 +885,130 @@
     return jnp.sum(received.astype(F32), axis=0)
 
 
+def turn(x, gain, base, middle, ident):
+    rows = lax.axis_size("dp")
+    group, length, width = x.shape
+    backward = middle is not None
+    part = (rows, length, width)
+    return pl.pallas_call(
+        partial(turn_kernel, rows, backward),
+        out_shape=[
+            jax.ShapeDtypeStruct((length, width), F32),
+            jax.ShapeDtypeStruct((group, length, width), BF16),
+        ]
+        + ([jax.ShapeDtypeStruct((1, width), F32)] if backward else []),
+        in_specs=[ANY, IN_VMEM, IN_VMEM] + ([IN_VMEM] if backward else []),
+        out_specs=[IN_VMEM, ANY] + ([IN_VMEM] if backward else []),
+        scratch_shapes=[
+            pltpu.VMEM(part, BF16),
+            pltpu.VMEM(part, BF16),
+            pltpu.VMEM((rows - 1, length, width), BF16),
+            pltpu.VMEM((length, width), BF16),
+        ]
+        + [dma(CHUNKS, rows)] * 3
+        + [dma(CHUNKS, rows - 1)] * 2
+        + [dma(CHUNKS)]
+        + [dma(CHUNKS, rows - 1)] * 2
+        + [dma(CHUNKS, rows)] * 2,
+        compiler_params=pltpu.CompilerParams(collective_id=ident, has_side_effects=True),
+        cost_estimate=pl.CostEstimate(
+            flops=0, bytes_accessed=150_000_000, transcendentals=0
+        ),
+    )(x, gain, base, *([middle] if backward else []))
+
+
+def swap_on(x, ident):
+    rows, count = lax.axis_size("dp"), lax.axis_size("zq")
+    group, length, part = x.shape
+    links = 2 * rows - 1
+    return pl.pallas_call(
+        partial(swap_on_kernel, rows, count),
+        out_shape=[
+            jax.ShapeDtypeStruct(x.shape, x.dtype),
+            jax.ShapeDtypeStruct((group, RIM, part), x.dtype),
+        ],
+        in_specs=[ANY],
+        out_specs=[ANY, IN_VMEM],
+        scratch_shapes=[
+            pltpu.VMEM((group, RIM, part), x.dtype),
+            pltpu.SemaphoreType.DMA,
+            dma(links),
+            dma(links),
+            pltpu.SemaphoreType.DMA,
+            pltpu.SemaphoreType.DMA,
+        ],
+        compiler_params=pltpu.CompilerParams(collective_id=ident, has_side_effects=True),
+        cost_estimate=pl.CostEstimate(flops=0, bytes_accessed=90_000_000, transcendentals=0),
+    )(x)
+
+
+def swap_back(x, tail, rim, small, ident):
+    rows, count = lax.axis_size("dp"), lax.axis_size("zq")
+    group, length, part = x.shape
+    links = 2 * rows - 1
+    return pl.pallas_call(
+        partial(swap_back_kernel, rows, count),
+        out_shape=jax.ShapeDtypeStruct((group, length, part + small.shape[1]), x.dtype),
+        in_specs=[ANY, IN_VMEM, ANY, ANY],
+        out_specs=ANY,
+        scratch_shapes=[
+            pltpu.VMEM((group, RIM, part), x.dtype),
+            pltpu.VMEM((group, RIM, part), x.dtype),
+            dma(3),
+            dma(3, links),
+            dma(3, links),
+            pltpu.SemaphoreType.DMA,
+            pltpu.SemaphoreType.DMA,
+        ],
+        compiler_params=pltpu.CompilerParams(collective_id=ident, has_side_effects=True),
+        cost_estimate=pl.CostEstimate(flops=0, bytes_accessed=90_000_000, transcendentals=0),
+    )(x, tail, rim, small)
+
+
+def begin(hidden, grad, gain, decay, beta, weights, ident):
+    rows, count = lax.axis_size("dp"), lax.axis_size("zq")
+    group, links = 2 * rows, 2 * rows - 1
+    owned = decay.shape[0]
+    parts = [weight.shape[1] // group for weight in weights]
+    wide = sum(parts[:4]) + LANES
+    cut = (group, owned, wide)
+    side_shapes = [(group, owned, sum(parts[4:6])), (group, owned, sum(parts[6:]))]
+    assert count > 2
+    tokens = jax.ShapeDtypeStruct(hidden.shape, BF16)
+    everyone = jax.ShapeDtypeStruct((group,) + hidden.shape, BF16)
+    return pl.pallas_call(
+        partial(start_kernel, rows, count),
+        out_shape=[jax.ShapeDtypeStruct((count,) + cut, BF16)]
+        + [jax.ShapeDtypeStruct(shape, BF16) for shape in side_shapes]
+        + [everyone] * 2
+        + [tokens] * 3,
+        in_specs=[IN_VMEM] * 5 + [IN_HBM] * 8,
+        out_specs=[ANY] * 5 + [IN_VMEM] * 3,
+        scratch_shapes=[pltpu.VMEM(weight.shape, F32) for weight in weights]
+        + [pltpu.VMEM(cut, BF16)]
+        + [pltpu.VMEM(shape, BF16) for shape in side_shapes]
+        + [
+            dma(8),
+            dma(5),
+            dma(links),
+            dma(links),
+            dma(2, links),
+            dma(2, links),
+            dma(2, rows - 1),
+            dma(2, rows - 1),
+            dma(2, rows),
+            dma(2, rows),
+        ]
+        + [dma(count - 1, group)] * 4,
+        compiler_params=pltpu.CompilerParams(
+            collective_id=ident, has_side_effects=True, vmem_limit_bytes=40 << 20
+        ),
+        cost_estimate=pl.CostEstimate(
+            flops=0, bytes_accessed=300_000_000, transcendentals=0
+        ),
+    )(hidden, grad, gain, decay, beta, *weights)
+
+
 def column(x, ident):
     count = lax.axis_size("zq")
     return comm_call(
@@ -356,22 +1032,31 @@
     )
 
 
-def chain(high, low, add, forward, ident):
-    count = lax.axis_size("zq")
-    heads = add.shape[0]
-    return comm_call(
-        partial(chain_kernel, count, heads, forward),
-        jax.ShapeDtypeStruct(add.shape, BF16),
-        [
-            pltpu.VMEM(add.shape, BF16),
-            pltpu.VMEM(add.shape, BF16),
-            dma(heads),
-            dma(heads),
+def chain(high, low, add, sides, forward, ident):
+    rows, count = lax.axis_size("dp"), lax.axis_size("zq")
+    heads, key_size, value_size = add.shape
+    links = 2 * rows - 1
+    pieces = (heads * PIECES, key_size, value_size // PIECES)
+    return pl.pallas_call(
+        partial(chain_kernel, count, rows, heads, len(sides), forward),
+        out_shape=[jax.ShapeDtypeStruct(add.shape, BF16)]
+        + [jax.ShapeDtypeStruct(side.shape, side.dtype) for side in sides],
+        in_specs=[IN_VMEM] * 3 + [ANY] * len(sides),
+        out_specs=[IN_VMEM] + [ANY] * len(sides),
+        scratch_shapes=[
+            pltpu.VMEM(pieces, BF16),
+            pltpu.VMEM(pieces, BF16),
+            dma(heads * PIECES),
+            dma(heads * PIECES),
+            dma(len(sides)),
+            dma(len(sides), links),
+            dma(len(sides), links),
         ],
-        ident,
-        (high, low, add),
-        IN_VMEM,
-    )
+        compiler_params=pltpu.CompilerParams(collective_id=ident, has_side_effects=True),
+        cost_estimate=pl.CostEstimate(
+            flops=0, bytes_accessed=200_000_000, transcendentals=0
+        ),
+    )(high, low, add, *sides)
 
 
 def unit_lower_inverse(low):
@@ -413,31 +1098,68 @@
     return (row > col).astype(F32)
 
 
+def convolve(x_ref, rim_ref, taps_ref, same_ref, ext):
+    size = x_ref.shape[1]
+    ext[:RIM] = rim_ref[0].astype(F32)
+    ext[RIM:] = x_ref[0].astype(F32)
+    mixed = taps_ref[0:1] * ext[RIM:]
+    for lag in range(1, CONV):
+        mixed = mixed + taps_ref[lag : lag + 1] * ext[RIM - lag : RIM - lag + size] * (
+            same_ref[:, lag : lag + 1]
+        )
+    return mixed
+
+
+def convolve_back(grad, taps_ref, same_ref, ext, back):
+    size = grad.shape[0]
+    back[:RIM] = jnp.zeros((RIM, grad.shape[1]), F32)
+    back[RIM:] = taps_ref[0:1] * grad
+    sums = [jnp.sum(grad * ext[RIM:], axis=0, keepdims=True)]
+    for lag in range(1, CONV):
+        kept = grad * same_ref[:, lag : lag + 1]
+        sums.append(
+            jnp.sum(kept * ext[RIM - lag : RIM - lag + size], axis=0, keepdims=True)
+        )
+        back[RIM - lag : RIM - lag + size] += taps_ref[lag : lag + 1] * kept
+    return jnp.concatenate(sums, axis=0)
+
+
+def silu_parts(values):
+    sig = jax.nn.sigmoid(values)
+    return values * sig, sig * (1.0 + values * (1.0 - sig))
+
+
 def chunk_forward_kernel(
-    q_ref,
-    k_ref,
-    v_ref,
-    beta_ref,
-    decay_ref,
-    start_ref,
-    tail_ref,
-    inverse_ref,
-    scores_ref,
-    own_ref,
-    effect_ref,
-    offset_ref,
-    high_ref,
-    low_ref,
+    *refs,
 ):
-    size, key_size = q_ref.shape
+    pre_refs, rim_refs, tap_refs = refs[:4], refs[4:8], refs[8:12]
+    same_ref, beta_ref, decay_ref, start_ref, tail_ref = refs[12:17]
+    (
+        inverse_ref,
+        scores_ref,
+        own_ref,
+        effect_ref,
+        offset_ref,
+        high_ref,
+        low_ref,
+        back_high_ref,
+        back_low_ref,
+    ) = refs[17:26]
+    ext = refs[26]
+    active = []
+    for i in range(4):
+        mixed = convolve(pre_refs[i], rim_refs[i], tap_refs[i], same_ref, ext.at[i])
+        active.append(silu_parts(mixed)[0])
+    size, key_size = active[0].shape
     beta, start, tail = beta_ref[0], start_ref[0], tail_ref[0]
     decay = decay_ref[0]
-    query = unit_parts(q_ref[...])[0] * key_size ** (-0.5)
-    key = unit_parts(k_ref[...])[0]
+    query = unit_parts(active[0])[0] * key_size ** (-0.5)
+    key = unit_parts(active[1])[0]
+    values = jnp.concatenate(active[2:], axis=1)
     inner = exact(key, key, (1, 1))
     inverse = unit_lower_inverse(beta * inner * (decay * strict_lower(size)))
     scores = exact(query, key, (1, 1)) * decay
-    update = exact(inverse, beta * v_ref[...])
+    update = exact(inverse, beta * values)
     reach = exact(inverse, (beta * start) * key)
     inverse_ref[0] = inverse
     scores_ref[0] = scores
@@ -448,9 +1170,13 @@
     row = lax.broadcasted_iota(jnp.int32, (key_size, key_size), 0)
     col = lax.broadcasted_iota(jnp.int32, (key_size, key_size), 1)
     transfer = jnp.where(row == col, start[size - 1 :, :], 0.0) - exact(last, reach, (0, 0))
-    high = transfer.astype(BF16)
-    high_ref[0] = high
-    low_ref[0] = (transfer - high.astype(F32)).astype(BF16)
+    for matrix, top_ref, rest_ref in (
+        (transfer, high_ref, low_ref),
+        (transfer.T, back_high_ref, back_low_ref),
+    ):
+        top = matrix.astype(BF16)
+        top_ref[0] = top
+        rest_ref[0] = (matrix - top.astype(F32)).astype(BF16)
 
 
 def gate_forward_kernel(own_ref, effect_ref, state_ref, gate_ref, gain_ref, mixed_ref, gated_ref):
@@ -483,41 +1209,42 @@
     add_ref[0] = exact(effect_ref[0], mixed_grad, (0, 0))
 
 
-def chunk_backward_kernel(
-    q_ref,
-    k_ref,
-    v_ref,
-    beta_ref,
-    decay_ref,
-    start_ref,
-    tail_ref,
-    inverse_ref,
-    scores_ref,
-    state_ref,
-    mixed_ref,
-    ending_ref,
-    dq_ref,
-    dk_ref,
-    dv_ref,
-    dbeta_ref,
-    ddecay_ref,
-    dstart_ref,
-    dtail_ref,
-):
-    size, key_size = q_ref.shape
+def chunk_backward_kernel(heads, *refs):
+    pre_refs, rim_refs, tap_refs = refs[:4], refs[4:8], refs[8:12]
+    same_ref, beta_ref, decay_ref, start_ref, tail_ref = refs[12:17]
+    inverse_ref, scores_ref, state_ref, mixed_ref, ending_ref = refs[17:22]
+    (
+        grad_ref,
+        grad_tail_ref,
+        grad_rim_ref,
+        taps_grad_ref,
+        dbeta_ref,
+        ddecay_ref,
+        dstart_ref,
+        dtail_ref,
+    ) = refs[22:30]
+    ext, back = refs[30:]
+    active, slopes = [], []
+    for i in range(4):
+        mixed = convolve(pre_refs[i], rim_refs[i], tap_refs[i], same_ref, ext.at[i])
+        value, slope = silu_parts(mixed)
+        active.append(value)
+        slopes.append(slope)
+    size, key_size = active[0].shape
+    values = jnp.concatenate(active[2:], axis=1)
     beta, start, tail = beta_ref[0], start_ref[0], tail_ref[0]
     decay, inverse, scores = decay_ref[0], inverse_ref[0], scores_ref[0]
     state = state_ref[0].astype(F32)
     ending = ending_ref[0].astype(F32)
     mixed_grad = mixed_ref[...]
-    unit_q, scale_q = unit_parts(q_ref[...])
+    unit_q, scale_q = unit_parts(active[0])
     query = unit_q * key_size ** (-0.5)
-    key, scale_k = unit_parts(k_ref[...])
+    key, scale_k = unit_parts(active[1])
     below = strict_lower(size)
     inner = exact(key, key, (1, 1))
     raw = exact(query, key, (1, 1))
     recalled = exact(key, state)
-    miss = v_ref[...] - start * recalled
+    miss = values - start * recalled
     update = exact(inverse, beta * miss)
     mixed_state = exact(mixed_grad, state, (1, 1))
     last = tail * key
@@ -526,7 +1253,6 @@
     dlast = exact(update, ending, (1, 1))
     dright = exact(inverse, dupdate, (0, 0))
     dlower = -exact(dright, update, (1, 1)) * below
-    dv_ref[...] = beta * dright
     dscaled = dscores * decay
     dquery = start * mixed_state + exact(dscaled, key)
     dinner = beta * dlower * decay
@@ -550,8 +1276,23 @@
     )
     dtail_ref[0] = jnp.sum(key * dlast, axis=-1, keepdims=True)
     ddecay_ref[0] = dscores * raw + beta * dlower * inner
-    dq_ref[...] = unit_back(unit_q, scale_q, dquery * key_size ** (-0.5))
-    dk_ref[...] = unit_back(key, scale_k, dkey)
+    dvalues = beta * dright
+    grads = [
+        unit_back(unit_q, scale_q, dquery * key_size ** (-0.5)),
+        unit_back(key, scale_k, dkey),
+        dvalues[:, :key_size],
+        dvalues[:, key_size:],
+    ]
+    head = pl.program_id(0)
+    per = grad_ref.shape[2] // key_size
+    for i, block in enumerate((head, heads + head, 2 * heads + 2 * head, 2 * heads + 2 * head + 1)):
+        sums = convolve_back(grads[i] * slopes[i], tap_refs[i], same_ref, ext.at[i], back)
+        slab = block // per
+        columns = pl.ds(pl.multiple_of((block % per) * key_size, key_size), key_size)
+        grad_ref[slab, :, columns] = back[RIM:].astype(BF16)
+        grad_tail_ref[slab, :, columns] = back[size:]
+        grad_rim_ref[slab, :, columns] = back[:RIM].astype(BF16)
+        taps_grad_ref[slab, 0:CONV, columns] = sums
 
 
 def by_head(*shape):
@@ -562,9 +1303,10 @@
     return pl.BlockSpec((rows, width), lambda h: (0, h + offset))
 
 
-def head_call(body, heads, in_specs, out_specs, out_shape, operands, flops):
+def head_call(body, heads, in_specs, out_specs, out_shape, operands, flops, scratch=()):
     return pl.pallas_call(
         body,
+        scratch_shapes=scratch,
         grid=(heads,),
         in_specs=in_specs,
         out_specs=out_specs,
@@ -575,18 +1317,6 @@
 
 def shaped(*shape, dtype=F32):
     return jax.ShapeDtypeStruct(shape, dtype)
-
-
-def short_conv(seg_ext, pre_ext, conv_query, conv_key, conv_value):
-    kernel = jnp.concatenate([conv_query, conv_key, conv_value], axis=1)
-    margin = CONV - 1
-    length = pre_ext.shape[0] - margin
-    mixed = jnp.zeros((length, kernel.shape[1]), F32)
-    for lag in range(CONV):
-        offset = margin - lag
-        same = (seg_ext[margin:] == seg_ext[offset : offset + length]).astype(F32)
-        mixed = mixed + kernel[lag] * pre_ext[offset : offset + length] * same[:, None]
-    return jax.nn.silu(mixed)
 
 
 def decays(segment, before, decay_pre, beta_pre, a_log):
@@ -630,10 +1360,8 @@
 ):
     rows, count = lax.axis_size("dp"), lax.axis_size("zq")
     group = 2 * rows
-    inputs = hidden_in[0].astype(F32)
     segment = segment_ids[0]
-    grad_low = grad_out[0]
-    length, width = inputs.shape
+    length, width = hidden_in.shape[1:]
     heads = a_log.shape[0]
     key_width, value_width = w_query.shape[1], w_value.shape[1]
     key_size, value_size = key_width // heads, out_gain.shape[0]
@@ -641,11 +1369,10 @@
     hidden_width = w_gate.shape[1]
     owned = w_query.shape[0]
     margin = CONV - 1
-    spot = lax.axis_index("zq") * 2 + lax.axis_index("c")
     me = lax.axis_index("dp") * 2 + lax.axis_index("c")
-    project_width = (mixer_width + value_width) // group
+    mixer_part = mixer_width // group
+    back_width = value_width // group
     ffn_width = hidden_width // group
-    back_width = value_width // group
 
     def shuffled(values):
         return (
@@ -663,64 +1390,100 @@
     def joined(values):
         return values.swapaxes(0, 1).reshape(values.shape[1], -1)
 
-    small = jnp.concatenate([w_decay, w_beta], axis=1).astype(BF16)
-    small = jnp.pad(small, ((0, 0), (0, LANES - 2 * heads)))
-    mixer_cut = jnp.concatenate(
-        [
-            cut(jnp.concatenate([w_query, w_key, w_value, w_outgate], axis=1)),
-            jnp.broadcast_to(small[None], (group, owned, LANES)),
-        ],
-        axis=2,
-    )
-    ffn_cut = jnp.concatenate([cut(w_output), cut(w_gate), cut(w_up), cut(w_down)], axis=2)
-    mixer_own = swap(mixer_cut, 0).reshape(group * owned, -1)
-    mixer_weights = lax.all_gather(mixer_own, "zq", axis=0, tiled=True)
-    ffn_own = swap(ffn_cut, 1).reshape(group * owned, -1)
-    ffn_weights = lax.all_gather(ffn_own, "zq", axis=0, tiled=True)
-    project = mixer_weights[:, :project_width]
-    small_weights = mixer_weights[:, project_width:]
-    output_weights = ffn_weights[:, :back_width]
-    gate_up = ffn_weights[:, back_width : back_width + 2 * ffn_width]
-    down = ffn_weights[:, back_width + 2 * ffn_width :]
-
+    def gathered(values):
+        return lax.all_gather(values.reshape(group * owned, -1), "zq", axis=0, tiled=True)
+
+    def scattered(values):
+        return lax.psum_scatter(
+            values, "zq", scatter_dimension=0, tiled=True
+        ).reshape(group, owned, -1)
+
+    def blocks(values):
+        return values.astype(BF16).reshape(group, length, -1)
+
+    (
+        mixer_weights,
+        first_own,
+        gate_up_own,
+        normed_all,
+        grad_all,
+        hidden_low,
+        normed_low,
+        grad_low,
+    ) = begin(
+        hidden_in[0],
+        grad_out[0],
+        attn_gain[None],
+        w_decay,
+        w_beta,
+        (w_query, w_key, w_value, w_outgate, w_output, w_down, w_gate, w_up),
+        0,
+    )
+    mixer_weights = mixer_weights.reshape(width, -1)
+    normed_all = normed_all.reshape(-1, width)
+    grad_all = grad_all.reshape(-1, width)
+    project = mixer_weights[:, : mixer_part + back_width]
+    small_weights = mixer_weights[:, mixer_part + back_width :]
+    first_weights = gathered(first_own)
+    output_weights, down = first_weights[:, :back_width], first_weights[:, back_width:]
+
+    inputs = hidden_low.astype(F32)
+    attn_row, mlp_row = shuffled(attn_gain[None]), shuffled(mlp_gain[None])
     normed, norm_pull = jax.vjp(rms_scale, inputs)
-    normed_low = shuffled((normed * attn_gain).astype(BF16))
-    normed_all = spread(normed_low, 2).reshape(-1, width)
-    grad_all = spread(shuffled(grad_low), 2).reshape(-1, width)
-    projected = mm(normed_all, project).astype(BF16)
-    mixed_low = joined(swap(projected.reshape(group, length, project_width), 3))
-    pre_low = mixed_low[:, :mixer_width]
-    gate_pre = mixed_low[:, mixer_width:]
+    pre_all = mm(normed_all, project[:, :mixer_part])
+    gate_all = mm(normed_all, project[:, mixer_part:])
+    pre, rim = swap_on(blocks(pre_all), 3)
     small_pre = mm(normed_low, small_weights)
     decay_pre, beta_pre = small_pre[:, :heads], small_pre[:, heads : 2 * heads]
-
-    rim = hop(pre_low[length - 16 :], True, 4)[16 - margin :]
     rim_ids = lax.ppermute(
         segment[-margin:],
         ("zq", "c"),
         [(i, i + 1) for i in range(2 * count - 1)],
     )
     seg_ext = jnp.concatenate([rim_ids, segment])
-    pre_ext = jnp.concatenate([rim, pre_low], axis=0).astype(F32)
-    active, conv_pull = jax.vjp(
-        partial(short_conv, seg_ext), pre_ext, conv_query, conv_key, conv_value
+    same = jnp.stack(
+        [
+            (segment == seg_ext[margin - lag : margin - lag + length]).astype(F32)
+            for lag in range(CONV)
+        ],
+        axis=1,
     )
     (beta, decay, start, tail), decay_pull = jax.vjp(
         partial(decays, segment, seg_ext[margin - 1]), decay_pre, beta_pre, a_log
     )
-    token_specs = [
-        by_columns(length, key_size),
-        by_columns(length, key_size, heads),
-        by_columns(length, value_size, 2 * key_width // value_size),
-        by_head(length, 1),
-        by_head(length, length),
-        by_head(length, 1),
-        by_head(length, 1),
+    slabs, slab = group, mixer_part
+    if slab % key_size:
+        slabs, slab = mixer_width // (3 * key_size), 3 * key_size
+        pre, rim = [
+            joined(part).reshape(-1, slabs, slab).swapaxes(0, 1) for part in (pre, rim)
+        ]
+    per = slab // key_size
+    taps = jnp.concatenate([conv_query, conv_key, conv_value], axis=1)
+    channel_blocks = [
+        lambda h: h,
+        lambda h: heads + h,
+        lambda h: 2 * heads + 2 * h,
+        lambda h: 2 * heads + 2 * h + 1,
     ]
-    token_args = (active, active, active, beta, decay, start, tail)
+
+    def slab_specs(lines):
+        return [
+            pl.BlockSpec((1, lines, key_size), lambda h, b=b: (b(h) // per, 0, b(h) % per))
+            for b in channel_blocks
+        ]
+
+    token_specs = (
+        slab_specs(length)
+        + slab_specs(RIM)
+        + [pl.BlockSpec((CONV, key_size), lambda h, b=b: (0, b(h))) for b in channel_blocks]
+        + [pl.BlockSpec((length, CONV), lambda h: (0, 0))]
+        + [by_head(length, 1), by_head(length, length), by_head(length, 1), by_head(length, 1)]
+    )
+    token_args = (pre,) * 4 + (rim,) * 4 + (taps,) * 4 + (same, beta, decay, start, tail)
+    ext_shape = pltpu.VMEM((4, RIM + length, key_size), F32)
     values_spec = by_columns(length, value_size)
     state_spec = by_head(key_size, value_size)
-    inverse, scores, own, effect, offset, high, low = head_call(
+    inverse, scores, own, effect, offset, high, low, back_high, back_low = head_call(
         chunk_forward_kernel,
         heads,
         token_specs,
@@ -730,22 +1493,26 @@
             values_spec,
             by_head(length, key_size),
             state_spec,
-            by_head(key_size, key_size),
-            by_head(key_size, key_size),
-        ],
+        ]
+        + [by_head(key_size, key_size)] * 4,
         [
             shaped(heads, length, length),
             shaped(heads, length, length),
             shaped(length, value_width),
             shaped(heads, length, key_size),
             shaped(heads, key_size, value_size),
-            shaped(heads, key_size, key_size, dtype=BF16),
-            shaped(heads, key_size, key_size, dtype=BF16),
-        ],
+        ]
+        + [shaped(heads, key_size, key_size, dtype=BF16)] * 4,
         token_args,
         6_000_000_000,
-    )
-    state = chain(high, low, offset, True, 5)
+        [ext_shape],
+    )
+    state, gate_back = chain(high, low, offset, (gate_all.reshape(group, length, -1),), True, 5)
+    gate_pre = joined(gate_back)
+    gate_up_own, state, first_weights = lax.optimization_barrier(
+        (gate_up_own, state, first_weights)
+    )
+    gate_up = gathered(gate_up_own)
     gain_spec = pl.BlockSpec((1, value_size), lambda h: (0, 0))
     gain_row = out_gain[None]
     mixed, gated = head_call(
@@ -759,38 +1526,31 @@
     )
     gated_cut = gated.reshape(length, group, back_width).swapaxes(0, 1)
     gated_all = swap(gated_cut, 6).reshape(-1, back_width)
-    attended = fold(
-        mm(gated_all, output_weights, (1, 1)).astype(BF16).reshape(group, length, width), 7
-    )
-    middle = inputs + unshuffled(attended)
-
-    normed_two, norm_pull_two = jax.vjp(rms_scale, middle)
-    normed_two_all = spread(shuffled((normed_two * mlp_gain).astype(BF16)), 2).reshape(-1, width)
+    middle, normed_two_all = turn(
+        blocks(mm(gated_all, output_weights, (1, 1))), mlp_row, inputs, None, 4
+    )
+    normed_two_all = normed_two_all.reshape(-1, width)
+
     both = mm(normed_two_all, gate_up)
     hidden, swiglu_pull = jax.vjp(swiglu, both[:, :ffn_width], both[:, ffn_width:])
     hidden_low = hidden.astype(BF16)
     grad_gate, grad_up = swiglu_pull(mm(grad_all, down))
     both_grad_low = jnp.concatenate([grad_gate, grad_up], axis=1).astype(BF16)
-    grad_normed_two = unshuffled(
-        fold(mm(both_grad_low, gate_up, (1, 1)).astype(BF16).reshape(group, length, width), 7)
-    )
-    mlp_part = fold(mm(hidden_low, down, (1, 1)).astype(BF16).reshape(group, length, width), 7)
-    result = (middle + unshuffled(mlp_part)).astype(BF16)
+    grad_normed_two_parts = blocks(mm(both_grad_low, gate_up, (1, 1)))
     gate_up_rows = mm(normed_two_all, both_grad_low, (0, 0)).astype(BF16)
+    grad_normed_two_parts, gate_up_rows = lax.optimization_barrier(
+        (grad_normed_two_parts, gate_up_rows)
+    )
+    gate_up_rows = scattered(gate_up_rows)
+    grad_middle, attended_grad_all, grad_mlp_gain = turn(
+        grad_normed_two_parts, mlp_row, grad_low, middle, 2
+    )
+    attended_grad_all = attended_grad_all.reshape(-1, width)
+
+    grad_gated = joined(swap(blocks(mm(attended_grad_all, output_weights)), 6))
+    output_rows = mm(attended_grad_all, gated_all, (0, 0)).astype(BF16)
     down_rows = mm(grad_all, hidden_low, (0, 0)).astype(BF16)
-    grad_mlp_gain = jnp.sum(grad_normed_two * normed_two, axis=0)
-    grad_middle = grad_low.astype(F32) + norm_pull_two(grad_normed_two * mlp_gain)[0]
-
-    attended_grad_all = spread(shuffled(grad_middle.astype(BF16)), 2).reshape(-1, width)
-    grad_gated_all = mm(attended_grad_all, output_weights).astype(BF16)
-    grad_gated = joined(swap(grad_gated_all.reshape(group, length, back_width), 6))
-    output_rows = mm(attended_grad_all, gated_all, (0, 0)).astype(BF16)
-    ffn_rows = lax.psum_scatter(
-        jnp.concatenate([output_rows, gate_up_rows, down_rows], axis=1),
-        "zq",
-        scatter_dimension=0,
-        tiled=True,
-    )
+    mlp_parts = blocks(mm(hidden_low, down, (1, 1)))
     mixed_grad, gate_pre_grad, gain_grad, state_add = head_call(
         gate_backward_kernel,
         heads,
@@ -806,9 +1566,25 @@
         1_000_000_000,
     )
     grad_out_gain = jnp.sum(gain_grad, axis=(0, 1))
-    ending = chain(high, low, state_add, False, 8)
-    dq, dk, dv, dbeta, ddecay, dstart, dtail = head_call(
-        chunk_backward_kernel,
+    side_rows = jnp.concatenate([down_rows, output_rows], axis=1)
+    state_add, mlp_parts, gate_up_rows, side_rows = lax.optimization_barrier(
+        (state_add, mlp_parts, gate_up_rows, side_rows)
+    )
+    ending, gate_grad_back, mlp_back = chain(
+        back_high,
+        back_low,
+        state_add,
+        (gate_pre_grad.reshape(length, group, back_width).swapaxes(0, 1), mlp_parts),
+        False,
+        8,
+    )
+    gate_grad_all = gate_grad_back.reshape(-1, back_width)
+    side_rows, ending = lax.optimization_barrier((side_rows, ending))
+    side_rows = scattered(side_rows)
+    gate_up_back = lax.all_to_all(gate_up_rows, ("dp", "c"), 0, 0, tiled=True)
+    whole = lambda *shape: pl.BlockSpec(shape, lambda h: (0, 0, 0))
+    grad_pre, grad_tail, grad_rim, grad_taps, dbeta, ddecay, dstart, dtail = head_call(
+        partial(chunk_backward_kernel, heads),
         heads,
         token_specs
         + [
@@ -819,14 +1595,17 @@
             state_spec,
         ],
         [
-            values_spec if size == value_size else by_columns(length, size)
-            for size in (key_size, key_size, value_size)
+            whole(slabs, length, slab),
+            whole(slabs, RIM, slab),
+            whole(slabs, RIM, slab),
+            whole(slabs, 2 * CONV, slab),
         ]
         + [by_head(length, 1), by_head(length, length), by_head(length, 1), by_head(length, 1)],
         [
-            shaped(length, key_width),
-            shaped(length, key_width),
-            shaped(length, value_width),
+            shaped(slabs, length, slab, dtype=BF16),
+            shaped(slabs, RIM, slab),
+            shaped(slabs, RIM, slab, dtype=BF16),
+            shaped(slabs, 2 * CONV, slab),
             shaped(heads, length, 1),
             shaped(heads, length, length),
             shaped(heads, length, 1),
@@ -834,50 +1613,54 @@
         ],
         token_args + (inverse, scores, state, mixed_grad, ending),
         12_000_000_000,
+        [ext_shape, pltpu.VMEM((RIM + length, key_size), F32)],
     )
     grad_decay, grad_beta, grad_alog = decay_pull((dbeta, ddecay, dstart, dtail))
-    grad_ext, grad_conv_one, grad_conv_two, grad_conv_three = conv_pull(
-        jnp.concatenate([dq, dk, dv], axis=1)
-    )
-    rim_grad = jnp.pad(grad_ext[:margin].astype(BF16), ((16 - margin, 0), (0, 0)))
-    returned = hop(rim_grad, False, 9).astype(F32)[16 - margin :]
-    grad_pre = grad_ext[margin:].at[length - margin :].add(returned)
+    grad_taps = joined(grad_taps)[:CONV]
+    grad_conv_one = grad_taps[:, :key_width]
+    grad_conv_two = grad_taps[:, key_width : 2 * key_width]
+    grad_conv_three = grad_taps[:, 2 * key_width :]
     small_grad = jnp.concatenate([grad_decay, grad_beta], axis=1).astype(BF16)
     small_grad = jnp.pad(small_grad, ((0, 0), (0, LANES - 2 * heads)))
-    wide_grad = jnp.concatenate([grad_pre.astype(BF16), gate_pre_grad], axis=1)
-    grads_cut = jnp.concatenate(
+    if slabs != group:
+        grad_pre, grad_tail, grad_rim = [
+            joined(part).reshape(-1, group, mixer_part).swapaxes(0, 1)
+            for part in (grad_pre, grad_tail, grad_rim)
+        ]
+    grad_pre, gate_up_back = lax.optimization_barrier((grad_pre, gate_up_back))
+    grads_all = swap_back(grad_pre, grad_tail, grad_rim, small_grad, 10).reshape(
+        group * length, -1
+    )
+    mixer_parts = jnp.concatenate(
         [
-            wide_grad.reshape(length, group, project_width).swapaxes(0, 1),
-            jnp.broadcast_to(small_grad[None], (group, length, LANES)),
+            mm(normed_all, grads_all, (0, 0)).astype(BF16),
+            mm(normed_all, gate_grad_all, (0, 0)).astype(BF16),
         ],
-        axis=2,
-    )
-    grads_all = swap(grads_cut, 10).reshape(group * length, -1)
-    mixer_rows = lax.psum_scatter(
-        mm(normed_all, grads_all, (0, 0)).astype(BF16),
-        "zq",
-        scatter_dimension=0,
-        tiled=True,
-    )
+        axis=1,
+    )
+    mixer_parts, side_rows = lax.optimization_barrier((mixer_parts, side_rows))
+    mixer_rows = scattered(mixer_parts)
     combined = fold(
-        mm(grads_all[:, :project_width], project, (1, 1))
-        .astype(BF16)
-        .reshape(group, length, width),
+        blocks(
+            mm(
+                jnp.concatenate([grads_all[:, :mixer_part], gate_grad_all], axis=1),
+                project,
+                (1, 1),
+            )
+        ),
         7,
     )
-    combined = unshuffled(combined + mm(small_grad, small_weights, (1, 1)))
+    mlp_part = jnp.sum(mlp_back.astype(F32), axis=0)
+    result = (middle + mlp_part).astype(BF16)
+    combined = combined + mm(small_grad, small_weights, (1, 1))
     grad_attn_gain = jnp.sum(combined * normed, axis=0)
-    grad_inputs = grad_middle + norm_pull(combined * attn_gain)[0]
-
-    ffn_back = joined_rows(swap(ffn_rows.reshape(group, owned, -1), 1))
-    output_grad = joined(ffn_back[:, :, :back_width])
-    gate_grad = joined(ffn_back[:, :, back_width : back_width + ffn_width])
-    up_grad = joined(ffn_back[:, :, back_width + ffn_width : back_width + 2 * ffn_width])
-    down_grad = joined(ffn_back[:, :, back_width + 2 * ffn_width :])
-    mixer_parts = mixer_rows.reshape(group, owned, -1)
-    mixer_back = joined(joined_rows(swap(mixer_parts, 0))[:, :, :project_width])
-    small_rows = lax.dynamic_index_in_dim(mixer_parts, me, 0, keepdims=False)
-    small_rows = small_rows[:, project_width:].astype(F32)
+    grad_inputs = grad_middle + norm_pull(combined * attn_row)[0]
+
+    side_back = lax.all_to_all(side_rows, ("dp", "c"), 0, 0, tiled=True).astype(F32)
+    gate_grad = joined(gate_up_back[:, :, :ffn_width].astype(F32))
+    up_grad = joined(gate_up_back[:, :, ffn_width:].astype(F32))
+    down_grad = joined(side_back[:, :, :ffn_width])
+    output_grad = joined(side_back[:, :, ffn_width:])
 
     pieces = (
         grad_attn_gain,
@@ -893,36 +1676,43 @@
     flat = jnp.pad(flat, (0, lines * LANES - flat.shape[0])).reshape(lines, LANES)
     flat = jnp.sum(spread(flat, 11), axis=0)
     flat = jnp.sum(column(flat, 12), axis=0).reshape(-1)
+    mixer_rows, _ = lax.optimization_barrier((mixer_rows, (flat, grad_inputs, side_back)))
+    mixer_swapped = swap(
+        jnp.concatenate(
+            [mixer_rows[:, :, :mixer_part], mixer_rows[:, :, mixer_part + LANES :]], axis=2
+        ),
+        15,
+    ).astype(F32)
+    mixer_back = joined(mixer_swapped[:, :, :mixer_part])
+    outgate_grad = joined(mixer_swapped[:, :, mixer_part:])
+    small_rows = lax.dynamic_index_in_dim(mixer_rows, me, 0, keepdims=False)
+    small_rows = small_rows[:, mixer_part : mixer_part + LANES].astype(F32)
     summed, at = [], 0
     for piece in pieces:
         summed.append(flat[at : at + piece.size].reshape(piece.shape))
         at += piece.size
 
     return (
-        result[None],
-        grad_inputs.astype(BF16)[None],
-        summed[0],
+        unshuffled(result)[None],
+        unshuffled(grad_inputs.astype(BF16))[None],
+        unshuffled(summed[0][None])[0],
         mixer_back[:, :key_width],
         mixer_back[:, key_width : 2 * key_width],
-        mixer_back[:, 2 * key_width : mixer_width],
+        mixer_back[:, 2 * key_width :],
         small_rows[:, :heads],
         small_rows[:, heads : 2 * heads],
-        mixer_back[:, mixer_width:],
+        outgate_grad,
         summed[1],
         summed[2],
         summed[3],
         summed[4],
         summed[5],
         output_grad,
-        summed[6],
+        unshuffled(summed[6][None])[0],
         gate_grad,
         up_grad,
         down_grad,
     )
-
-
-def joined_rows(values):
-    return values.astype(F32)
 
 
 def solution(mesh):

time: 1060 us -> 806 us (0.76)
  Pallas kernels: 666 us -> 536 us
  waiting for transfers between devices: 87.5 us -> 31.3 us
  other arithmetic: 80.3 us -> 30.7 us
  local copies, waits for them, and re-layouts: 98.7 us -> 65.5 us
    pallas_call x22 -> x6, Pallas kernels: 595 us -> 100 us  [comm_call(): pl.pallas_call(body, out_shape=out, in_specs=[spec] * len(operands), out_...]
    pallas_call x4 -> x11, Pallas kernels: 71.1 us -> 436 us  [the longest x2 111 us: turn(): pl.pallas_call(partial(turn_kernel, rows, backward), out_shape=[jax.Shape...]
    reduce_scatter x2 -> x3, waiting for transfers between devices: 79.4 us -> 0.01 us  [scattered(): lax.psum_scatter(values, 'zq', scatter_dimension=0, tiled=True)]
    all_gather x2, waiting for transfers between devices: 8.07 us -> 31.2 us  [gathered(): lax.all_gather(values.reshape(group * owned, -1), 'zq', axis=0, tiled=True)]
    concatenate x6 -> x3, other arithmetic: 20.8 us -> 6.65 us  [the longest x1 2.79 us: local(): jnp.concatenate([mm(normed_all, grads_all, (0, 0)).astype(BF16), mm(norme...]
    reshape x10 -> x1, local copies, waits for them, and re-layouts: 12 us -> 1.17 us  [local(): gate_pre_grad.reshape(length, group, back_width).swapaxes(0, 1)]
    dot_general x14 -> x16, matrix products: 95.3 us -> 104 us  [mm(): lax.dot_general(left, right, (((over[0],), (over[1],)), ((), ())), prefer...]
  transfers between devices with their start and end apart: 5 -> 8, of which waited for: 2 -> 1; matrix products, arithmetic and copies ran while one was open for 13% -> 17% of each run, Pallas kernels for 32% -> 45%
where the time goes in v2:
time: 806 us; the launch traced here: 793 us
  Pallas kernels  536 us (67%)
  matrix products  104 us (13%)
  local copies, waits for them, and re-layouts  65.5 us (8%)
  waiting for transfers between devices  31.3 us (4%)
  other arithmetic  30.7 us (4%)
  between operations  14.8 us (2%)
  starting transfers between devices  10 us (1%)
    pallas_call x2, Pallas kernels, turn(): pl.pallas_call(partial(turn_kernel, rows, backward), out_shape=[jax.Shape...  111 us
    dot_general x16, matrix products, mm(): lax.dot_general(left, right, (((over[0],), (over[1],)), ((), ())), prefer...  104 us
    pallas_call x1, Pallas kernels, begin(): pl.pallas_call(partial(start_kernel, rows, count), out_shape=[jax.ShapeDt...  101 us
    pallas_call x6, Pallas kernels, comm_call(): pl.pallas_call(body, out_shape=out, in_specs=[spec] * len(operands), out_...  100 us
    pallas_call x2, Pallas kernels, chain(): pl.pallas_call(partial(chain_kernel, count, rows, heads, len(sides), forw...  93 us
    pallas_call x4, Pallas kernels, head_call(): pl.pallas_call(body, scratch_shapes=scratch, grid=(heads,), in_specs=in_s...  81.8 us
    all_gather x2, waiting for transfers between devices, gathered(): lax.all_gather(values.reshape(group * owned, -1), 'zq', axis=0, tiled=True)  31.2 us
    pallas_call x1, Pallas kernels, swap_back(): pl.pallas_call(partial(swap_back_kernel, rows, count), out_shape=jax.Shap...  26 us
  transfers between devices with their start and end apart: 8, of which 1 were waited for; matrix products, arithmetic and copies ran while one was open for 17% of the time, Pallas kernels for 45%

profile of v2, /device:TPU:0, one launch (start us, length us, event | category | flops | bytes accessed | tf_op | source)
XLA Modules:
  0.0 792.8 jit_solution(18195521900182166813)
XLA Ops:
  21.1 100.8 %shard_map.339 = (bf16[4,8,64,1280]{3,2,1,0:T(8,128)(2,1)}, bf16[8,64,1088]{2,1,0:T(8,128)(2,1)}, bf16[8,64,1408]{2,1,0:T(8,128)(2,1)}, bf16[8,128,2048]{2,1,0:T...) custom-call(bf16[128,2048]{1,0:T(8,128)(2,1)S(1)} %bitcast.137, ...), custom_call_target="tpu_custom_call" | custom-call | bytes 300000000 | tf_op jit(solution)/shard_map/pallas_call | solution.py:979
  122.8 2.3 collective-permute-start
  125.7 7.7 fusion.17
  133.4 23.1 %shard_map.340 = (bf16[8,128,768]{2,1,0:T(8,128)(2,1)}, bf16[8,16,768]{2,1,0:T(8,128)(2,1)}) custom-call(bf16[8,128,768]{2,1,0:T(8,128)(2,1)} %bitcast.162), custom_call_target="tpu_custom_call" | custom-call | bytes 90000000 | tf_op jit(solution)/shard_map/pallas_call | solution.py:924
  160.4 6.2 fusion.20.refs_0_
  171.4 32.7 %shard_map.341 = (f32[6,128,128]{2,1,0:T(8,128)}, f32[6,128,128]{2,1,0:T(8,128)}, f32[128,3072]{1,0:T(8,128)}, f32[6,128,256]{2,1,0:T(8,128)}, f32[6,256,512]{2,...) custom-call(bf16[8,128,768]{2,1,0:T(8,128)(2,1)} %get-tuple-element., ...), custom_call_target="tpu_custom_call" | custom-call | flops 6000000000 | bytes 20000000 | tf_op jit(solution)/shard_map/pallas_call | solution.py:1307
  204.2 31.8 %shard_map.342 = (bf16[6,256,512]{2,1,0:T(8,128)(2,1)}, f32[8,128,384]{2,1,0:T(8,128)}) custom-call(bf16[6,256,256]{2,1,0:T(8,128)(2,1)} %get-tuple-element.85.high_ref, bf16[6,256,256]{2,1,0:T(8,128)(2,1)} %get-tuple-element.86.low_ref, f32[6,256,512]{2,1,0:T(8,128)} %get-tuple-element.87.add_ref, f32[8,128,384]{2,1,0:T(8,128)} %fusion.20.refs_0_), custom_call_target="tpu_custom_call" | custom-call | bytes 200000000 | tf_op jit(solution)/shard_map/pallas_call | solution.py:1040
  239.3 6.5 shard_map.343
  248.6 12.5 %shard_map.344 = bf16[8,128,384]{2,1,0:T(8,128)(2,1)} custom-call(bf16[8,128,384]{2,1,0:T(8,128)(2,1)} %bitcast.155), custom_call_target="tpu_custom_call" | custom-call | bytes 90000000 | tf_op jit(solution)/shard_map/pallas_call | solution.py:830
  261.0 6.0 convolution_convert_fusion.1
  267.0 55.4 %shard_map.345 = (f32[128,2048]{1,0:T(8,128)}, bf16[8,128,2048]{2,1,0:T(8,128)(2,1)}) custom-call(bf16[8,128,2048]{2,1,0:T(8,128)(2,1)} %bitcast.150, f32[1,2048]{1,0:T(1,128)} %bitcast.182, f32[128,2048]{1,0:T(8,128)} %convert_element_type.76.base_ref), custom_call_target="tpu_custom_call" | custom-call | bytes 150000000 | tf_op jit(solution)/shard_map/pallas_call | solution.py:893
  322.4 31.2 %all-gather.5.cloned.1.call-done = bf16[2048,1408]{1,0:T(8,128)(2,1)} async-done(((bf16[512,1408]{1,0:T(8,128)(2,1)}), bf16[2048,1408]{1,0:T(8,128)(2,1)}) %all-gather.5.cloned.1.call-update) | async-done | bytes 5767184 | tf_op jit(solution)/shard_map/all_gather | solution.py:1394
  353.6 11.5 %fusion.75 = f32[1024,1408]{0,1:T(8,128)} fusion(bf16[1024,2048]{1,0:T(8,128)(2,1)} %bitcast.202, bf16[2048,1408]{1,0:T(8,128)(2,1)} %all-gather.5.cloned.1.call-done), kind=kOutput, calls=%fused_computation.137 | convolution fusion | flops 5905580032 | bytes 15728640 | tf_op jit(solution)/shard_map/dot_general | solution.py:32
  365.1 7.3 fusion.9
  374.0 8.8 %convolution_convert_fusion = bf16[2048,1408]{1,0:T(8,128)(2,1)} fusion(bf16[1024,2048]{1,0:T(8,128)(2,1)S(1)} %bitcast.203, bf16[1024,704]{0,1:T(8,128)(2,1)S(1)} %get-tuple-element.216, bf16[1024,704]{0,1:T(8,128)(2,1)S(1)} %get-tuple-element.215), kind=kOutput, calls=%fused_computation.1 | convolution fusion | flops 5914230784 | bytes 12845056 | tf_op jit(solution)/shard_map/dot_general | solution.py:32
  382.7 11.3 %convolution_convert_fusion.3 = bf16[1024,2048]{1,0:T(8,128)(2,1)} fusion(bf16[2048,1408]{1,0:T(8,128)(2,1)} %all-gather.5.cloned.1.call-done, bf16[1024,704]{0,1:T(8,128)(2,1)} %copy-done.37, bf16[1024,704]{0,1:T(8,128)(2,1)} %copy-done.36), kind=kOutput, calls=%fused_computation.12 | convolution fusion | flops 5913444352 | bytes 12845056 | tf_op jit(solution)/shard_map/dot_general | solution.py:32
  394.2 55.5 %shard_map.346 = (f32[128,2048]{1,0:T(8,128)}, bf16[8,128,2048]{2,1,0:T(8,128)(2,1)}, f32[1,2048]{1,0:T(1,128)}) custom-call(bf16[8,128,2048]{2,1,0:T(8,128)(2,1)} %bitcast.152, f32[1,2048]{1,0:T(1,128)} %bitcast.183, bf16[128,2048]{1,0:T(8,128)(2,1)} %copy-done.8, f32[128,2048]{1,0:T(8,128)} %get-tuple-element.94.refs_0_), custom_call_target="tpu_custom_call" | custom-call | bytes 150000000 | tf_op jit(solution)/shard_map/pallas_call | solution.py:893
  449.7 5.9 convolution_convert_fusion.5
  455.6 12.3 %shard_map.347 = bf16[8,128,384]{2,1,0:T(8,128)(2,1)} custom-call(bf16[8,128,384]{2,1,0:T(8,128)(2,1)} %bitcast.166), custom_call_target="tpu_custom_call" | custom-call | bytes 90000000 | tf_op jit(solution)/shard_map/pallas_call | solution.py:830
  467.9 2.1 copy.230
  470.1 8.6 %shard_map.348 = (f32[128,3072]{1,0:T(8,128)}, bf16[128,3072]{1,0:T(8,128)(2,1)}, f32[6,1,512]{2,1,0:T(1,128)}, f32[6,256,512]{2,1,0:T(8,128)}) custom-call(f32[128,3072]{1,0:T(8,128)} %get-tuple-element.97.mixed_ref, f32[128,3072]{1,0:T(8,128)} %bitcast.142, f32[1,512]{1,0:T(1,128)} %bitcast.188, bf16[128,3072]{1,0:T(8,128)(2,1)} %bitcast.158, ...), custom_call_target="tpu_custom_call" | custom-call | flops 1000000000 | bytes 20000000 | tf_op jit(solution)/shard_map/pallas_call | solution.py:1307
  481.4 4.2 bitcast_convert_fusion.2
  485.6 3.4 convolution_convert_fusion.4
  489.0 2.7 pad_maximum_fusion.1
  491.7 7.1 convolution_convert_fusion.2
  498.7 61.2 %shard_map.349 = (bf16[6,256,512]{2,1,0:T(8,128)(2,1)}, bf16[8,128,384]{2,1,0:T(8,128)(2,1)}, bf16[8,128,2048]{2,1,0:T(8,128)(2,1)}) custom-call(bf16[6,256,256]{2,1,0:T(8,128)(2,1)} %get-tuple-element.95.high_ref, bf16[6,256,256]{2,1,0:T(8,128)(2,1)} %get-tuple-element.96.low_ref, f32[6,256,512]{2,1,0:T(8,128)} %get-tuple-element.106.add_ref, ...), custom_call_target="tpu_custom_call" | custom-call | bytes 200000000 | tf_op jit(solution)/shard_map/pallas_call | solution.py:1040
  560.0 3.6 all-to-all-start
  563.6 33.9 %shard_map.350 = (bf16[8,128,768]{2,1,0:T(8,128)(2,1)}, f32[8,16,768]{2,1,0:T(8,128)}, bf16[8,16,768]{2,1,0:T(8,128)(2,1)}, f32[8,8,768]{2,1,0:T(8,128)}, f32[6,...) custom-call(bf16[8,128,768]{2,1,0:T(8,128)(2,1)} %get-tuple-element.79.refs_0_.refs_1_.ref, ...), custom_call_target="tpu_custom_call" | custom-call | flops 12000000000 | bytes 20000000 | tf_op jit(solution)/shard_map/pallas_call | solution.py:1307
  603.8 4.2 bitcast_convert_fusion.1
  608.1 26.0 %shard_map.351 = bf16[8,128,896]{2,1,0:T(8,128)(2,1)} custom-call(bf16[8,128,768]{2,1,0:T(8,128)(2,1)} %get-tuple-element.119.x_ref, f32[8,16,768]{2,1,0:T(8,128)} %get-tuple-element.120.tail_ref, bf16[8,16,768]{2,1,0:T(8,128)(2,1)} %get-tuple-element.121.rim_ref, bf16[128,128]{1,0:T(8,128)(2,1)} %pad.12.small_ref), custom_call_target="tpu_custom_call" | custom-call | bytes 90000000 | tf_op jit(solution)/shard_map/pallas_call | solution.py:949
  634.1 6.9 bitcast_convert_fusion
  641.0 2.8 pad_maximum_fusion
  643.7 2.4 copy.214
  647.1 3.0 convert_reduce_fusion
  655.3 9.7 %fusion.2 = bf16[1024,2048]{1,0:T(8,128)(2,1)} fusion(bf16[2048,1280]{1,0:T(8,128)(2,1)} %bitcast.177, bf16[1024,384]{1,0:T(8,128)(2,1)S(1)} %bitcast.204, bf16[1024,768]{1,0:T(8,128)(2,1)S(1)} %slice.193), kind=kOutput, calls=%fused_computation.10 | convolution fusion | flops 4838653952 | bytes 11272192 | tf_op jit(solution)/shard_map/dot_general | solution.py:32
  665.0 29.0 %shard_map.352 = bf16[4,128,2048]{2,1,0:T(8,128)(2,1)} custom-call(bf16[8,128,2048]{2,1,0:T(8,128)(2,1)} %bitcast.151), custom_call_target="tpu_custom_call" | custom-call | bytes 90000000 | tf_op jit(solution)/shard_map/pallas_call | solution.py:830
  694.0 2.1 convert_reduce_fusion.1
  696.1 2.5 multiply_reduce_fusion
  699.3 10.5 %shard_map.353 = f32[8,232,128]{2,1,0:T(8,128)} custom-call(f32[232,128]{1,0:T(8,128)} %pad_bitcast_fusion.x_ref), custom_call_target="tpu_custom_call" | custom-call | bytes 90000000 | tf_op jit(solution)/shard_map/pallas_call | solution.py:830
  709.8 1.9 reduce_sum.155.x_ref
  711.7 18.6 %shard_map.354 = f32[4,232,128]{2,1,0:T(8,128)} custom-call(f32[232,128]{1,0:T(8,128)} %reduce_sum.155.x_ref), custom_call_target="tpu_custom_call" | custom-call | bytes 90000000 | tf_op jit(solution)/shard_map/pallas_call | solution.py:830
  732.7 3.8 all-to-all-start.1
  736.6 2.8 fusion.23
  741.7 2.2 broadcast_in_dim_reshape.7
  747.1 1.7 convert_bitcast_fusion
  749.7 1.7 reshape.263
  751.4 2.3 copy.221
  762.4 17.5 %shard_map.355 = bf16[8,64,1152]{2,1,0:T(8,128)(2,1)} custom-call(bf16[8,64,1152]{2,1,0:T(8,128)(2,1)} %pad_maximum_fusion.5.x_ref), custom_call_target="tpu_custom_call" | custom-call | bytes 90000000 | tf_op jit(solution)/shard_map/pallas_call | solution.py:830
  (197 shorter events, 70.9 us)
Async XLA Ops:
  7.2 228.9 %all-gather.3.cloned.1.call-start = ((), (), s32[]{:S(2)}) async-start(), calls=%async_computation.5 | async-start | bytes 5898240 | tf_op jit(solution)/shard_map/all_gather | solution.py:1394
  8.8 1.4 copy-start
  10.2 1.4 copy-start.1
  11.5 1.4 copy-start.2
  12.9 1.1 copy-start.3
  14.0 1.1 copy-start.4
  15.1 1.1 copy-start.5
  16.3 1.0 copy-start.6
  17.3 1.0 copy-start.7
  18.4 1.0 copy-start.9
  19.4 1.0 copy-start.10
  20.4 0.7 copy-start.11
  21.1 101.7 %copy-start.26 = (s32[1,128]{1,0:T(1,128)S(1)}, s32[1,128]{1,0:T(1,128)}, u32[]{:S(2)}) copy-start(s32[1,128]{1,0:T(1,128)} %param.21) | copy-start | bytes 1540
  121.9 0.8 copy-start.8
  122.7 230.9 %all-gather.5.cloned.1.call-start = ((), (), s32[]{:S(2)}) async-start(), calls=%async_computation.6 | async-start | bytes 7208960 | tf_op jit(solution)/shard_map/all_gather | solution.py:1394
  122.8 43.7 %collective-permute-start = (s32[3]{0:T(128)S(1)}, s32[3]{0:T(128)S(1)}, u32[]{:S(2)}, u32[]{:S(2)}) collective-permute-start(s32[3]{0:T(128)S(1)} %slice_bitcast_fusion.7), channel_id=1, source_target_pairs={{0,1},{1,2},{2,3},{3,4},{4,5},{5,6},{6,7},{8,9},{9,10},{10,11},{11... | collective-permute-start | bytes 44 | tf_op jit(solution)/shard_map/ppermute | solution.py:1438
  133.4 25.5 %copy-start.33 = (f32[6]{0:T(128)S(1)}, f32[6]{0:T(128)}, u32[]{:S(2)}) copy-start(f32[6]{0:T(128)} %param.30) | copy-start | bytes 76
  133.4 26.0 %copy-start.22 = (f32[4,1536]{1,0:T(4,128)S(1)}, f32[4,1536]{1,0:T(4,128)}, u32[]{:S(2)}) copy-start(f32[4,1536]{1,0:T(4,128)} %param.31) | copy-start | bytes 73732
  133.4 26.0 %copy-start.23 = (f32[4,1536]{1,0:T(4,128)S(1)}, f32[4,1536]{1,0:T(4,128)}, u32[]{:S(2)}) copy-start(f32[4,1536]{1,0:T(4,128)} %param.32) | copy-start | bytes 73732
  133.4 27.0 %copy-start.21 = (f32[4,3072]{1,0:T(4,128)S(1)}, f32[4,3072]{1,0:T(4,128)}, u32[]{:S(2)}) copy-start(f32[4,3072]{1,0:T(4,128)} %param.33) | copy-start | bytes 147460
  160.4 6.2 copy-start.28
  204.2 32.1 %copy-start.27 = (f32[2048]{0:T(1024)S(1)}, f32[2048]{0:T(1024)}, u32[]{:S(2)}) copy-start(f32[2048]{0:T(1024)} %param.36) | copy-start | bytes 24580
  236.0 2.0 copy-start.17
  236.1 262.7 %reduce-scatter.4.cloned.1.call-start = ((), (), s32[]{:S(2)}) async-start(), calls=%async_computation.7 | async-start | bytes 7208960 | tf_op jit(solution)/shard_map/reduce_scatter | solution.py:1397
  267.0 98.1 %slice-start = ((s8[4718592]{0:T(1024)(128)(4,1)}), s8[524288]{0:T(1024)(128)(4,1)S(1)}, s32[]{:S(2)}) async-start(s8[4718592]{0:T(1024)(128)(4,1)} %bitcast.196), calls=%async_computation.10 | async-start | bytes 1048576
  353.6 11.5 %slice-start.1 = ((s8[4718592]{0:T(1024)(128)(4,1)}), s8[4194304]{0:T(1024)(128)(4,1)S(1)}, s32[]{:S(2)}) async-start(s8[4718592]{0:T(1024)(128)(4,1)} %bitcast.196), calls=%async_computation.11 | async-start | bytes 8388608
  353.6 11.5 %copy-start.29 = (bf16[8,128,2048]{2,1,0:T(8,128)(2,1)S(1)}, bf16[8,128,2048]{2,1,0:T(8,128)(2,1)}, u32[]{:S(2)}) copy-start(bf16[8,128,2048]{2,1,0:T(8,128)(2,1)} %get-tuple-element.98) | copy-start | bytes 12582916
  365.1 8.9 %copy-start.31 = (bf16[8,128,2048]{2,1,0:T(8,128)(2,1)S(1)}, bf16[8,128,2048]{2,1,0:T(8,128)(2,1)}, u32[]{:S(2)}) copy-start(bf16[8,128,2048]{2,1,0:T(8,128)(2,1)} %get-tuple-element.99) | copy-start | bytes 12582916
  372.4 1.1 copy-start.36
  372.4 1.6 copy-start.37
  394.1 249.6 %reduce-scatter.6.cloned.1.call-start = ((), (), s32[]{:S(2)}) async-start(), calls=%async_computation.8 | async-start | bytes 5570560 | tf_op jit(solution)/shard_map/reduce_scatter | solution.py:1397
  470.1 11.3 %copy-start.18 = (bf16[8,128,384]{2,1,0:T(8,128)(2,1)S(1)}, bf16[8,128,384]{2,1,0:T(8,128)(2,1)}, u32[]{:S(2)}) copy-start(bf16[8,128,384]{2,1,0:T(8,128)(2,1)} %shard_map.344) | copy-start | bytes 2359300
  481.4 4.2 copy-start.30
  481.4 4.2 copy-start.34
  489.0 2.7 copy-start.35
  560.0 48.1 %all-to-all-start = ((bf16[8,64,1408]{2,1,0:T(8,128)(2,1)}), bf16[8,64,1408]{2,1,0:T(8,128)(2,1)S(1)}, u32[]{:S(2)}, u32[]{:S(2)}) async-start(bf16[8,64,1408]{2,1,0:T(8,128)(2,1)} %bitcast.37), calls=%async_computation.1 | async-start | bytes 2883584 | tf_op jit(solution)/shard_map/all_to_all | solution.py:1584
  563.6 196.0 %reduce-scatter.8.cloned.1.call-start = ((), (), s32[]{:S(2)}) async-start(), calls=%async_computation.9 | async-start | bytes 6553600 | tf_op jit(solution)/shard_map/reduce_scatter | solution.py:1397
  603.2 0.6 copy-start.19
  608.1 32.9 %copy-start.14 = (bf16[8,64,1408]{2,1,0:T(8,128)(2,1)}, bf16[8,64,1408]{2,1,0:T(8,128)(2,1)S(1)}, u32[]{:S(2)}) copy-start(bf16[8,64,1408]{2,1,0:T(8,128)(2,1)S(1)} %all-to-all-done) | copy-start | bytes 4325380
  646.1 0.7 copy-start.12
  646.1 0.9 copy-start.24
  646.8 3.3 copy-start.16
  650.1 5.0 copy-start.13
  654.0 1.2 copy-start.32
  694.0 2.1 copy-start.20
  694.0 4.6 copy-start.25
  732.7 22.7 %all-to-all-start.1 = ((bf16[8,64,1088]{2,1,0:T(8,128)(2,1)}), bf16[8,64,1088]{2,1,0:T(8,128)(2,1)S(1)}, u32[]{:S(2)}, u32[]{:S(2)}) async-start(bf16[8,64,1088]{2,1,0:T(8,128)(2,1)} %bitcast.61), calls=%async_computation.4 | async-start | bytes 2359296 | tf_op jit(solution)/shard_map/all_to_all | solution.py:1659
  736.5 10.6 %copy-start.15 = (bf16[8,64,1408]{2,1,0:T(8,128)(2,1)S(1)}, bf16[8,64,1408]{2,1,0:T(8,128)(2,1)}, u32[]{:S(2)}) copy-start(bf16[8,64,1408]{2,1,0:T(8,128)(2,1)} %copy-done.14) | copy-start | bytes 4325380
Sparse Core Ops, SparseCore 0:
  122.8 89.1 all-gather.2
  236.2 117.3 all-gather.4
  394.2 100.5 reduce-scatter.3
  560.1 81.1 reduce-scatter.5
  646.3 99.3 reduce-scatter.7

commit v3 on v2

--- a/solution.py
+++ b/solution.py
@@ -386,15 +386,15 @@
 
 def turn_kernel(rows, backward, x_ref, gain_ref, base_ref, *refs):
     if backward:
-        out_ref, all_ref, sums_ref = refs[1:4]
-        gain_grad_ref, middle_ref = sums_ref, refs[0]
-        scratch = refs[4:]
+        middle_ref, extra_ref, out_ref, all_ref, sums_ref, paired_ref = refs[:6]
+        *scratch, extra, extra_load, extra_send, extra_recv = refs[6:]
     else:
         out_ref, all_ref = refs[:2]
         scratch = refs[2:]
     (
         mine,
         theirs,
+        stage,
         land,
         low,
         load,
@@ -431,29 +431,46 @@
                 x_ref.at[to * 2 + c, part], mine.at[i, part], load.at[j, i]
             )
             loads[j, i].start()
-    folds = {}
+    folds, extras = {}, []
+    if backward:
+        for i, to in enumerate(order):
+            extras.append(
+                (
+                    remote(
+                        extra_ref.at[to * 2 + (1 - c)],
+                        extra.at[i],
+                        extra_send.at[i],
+                        extra_recv.at[i],
+                        pair,
+                    ),
+                    pltpu.make_async_copy(
+                        extra_ref.at[to * 2 + c], paired_ref.at[i], extra_load.at[i]
+                    ),
+                )
+            )
     for j, part in enumerate(parts):
         for i in range(rows):
             loads[j, i].wait()
             hands[j, i].wait_recv()
             if i < rows - 1:
-                mine[i, part] = (mine[i, part].astype(F32) + theirs[i, part].astype(F32)).astype(
-                    BF16
-                )
+                stage[i, part] = (mine[i, part] + theirs[i, part]).astype(BF16)
                 folds[j, i] = remote(
-                    mine.at[i, part],
+                    stage.at[i, part],
                     land.at[i, part],
                     fold_send.at[j, i],
                     fold_recv.at[j, i],
                     others[i],
                 )
                 folds[j, i].start()
+    for pieces in extras:
+        for copy in pieces:
+            copy.start()
     gain = gain_ref[...]
     sends, keeps = {}, []
     if backward:
         sums_ref[...] = jnp.zeros_like(sums_ref)
     for j, part in enumerate(parts):
-        total = mine[rows - 1, part].astype(F32) + theirs[rows - 1, part].astype(F32)
+        total = mine[rows - 1, part] + theirs[rows - 1, part]
         for i in range(rows - 1):
             folds[j, i].wait_recv()
             total = total + land[i, part].astype(F32)
@@ -481,6 +498,12 @@
         keep = pltpu.make_async_copy(low.at[part], all_ref.at[me, part], own.at[j])
         keep.start()
         keeps.append(keep)
+    for i, (hand, copy) in enumerate(extras):
+        copy.wait()
+        hand.wait_recv()
+        paired_ref[i] = (paired_ref[i].astype(F32) + extra[i].astype(F32)).astype(BF16)
+    for hand, _ in extras:
+        hand.wait_send()
     for j, part in enumerate(parts):
         for i in range(rows - 1):
             sends[j, i].wait_recv()
@@ -759,6 +782,23 @@
     )
     waits = []
     for j in range(sides):
+        if side_refs[j].shape[0] == rows:
+            for i in range(rows - 1):
+                waits.append(
+                    remote(
+                        side_refs[j].at[i],
+                        side_out_refs[j].at[i],
+                        side_send.at[j, i],
+                        side_recv.at[j, i],
+                        (lax.rem(d + i + 1, rows), z, c),
+                    )
+                )
+            waits.append(
+                pltpu.make_async_copy(
+                    side_refs[j].at[rows - 1], side_out_refs[j].at[rows - 1], own.at[j]
+                )
+            )
+            continue
         for i, offset in enumerate(offsets):
             peer = plane_peer(offset, rows)
             waits.append(
@@ -885,36 +925,42 @@
     return jnp.sum(received.astype(F32), axis=0)
 
 
-def turn(x, gain, base, middle, ident):
+def turn(x, gain, base, more, ident):
     rows = lax.axis_size("dp")
     group, length, width = x.shape
-    backward = middle is not None
-    part = (rows, length, width)
+    backward = bool(more)
+    part, sent = (rows, length, width), (rows - 1, length, width)
     return pl.pallas_call(
         partial(turn_kernel, rows, backward),
         out_shape=[
             jax.ShapeDtypeStruct((length, width), F32),
             jax.ShapeDtypeStruct((group, length, width), BF16),
         ]
-        + ([jax.ShapeDtypeStruct((1, width), F32)] if backward else []),
-        in_specs=[ANY, IN_VMEM, IN_VMEM] + ([IN_VMEM] if backward else []),
-        out_specs=[IN_VMEM, ANY] + ([IN_VMEM] if backward else []),
+        + (
+            [jax.ShapeDtypeStruct((1, width), F32), jax.ShapeDtypeStruct(part, BF16)]
+            if backward
+            else []
+        ),
+        in_specs=[ANY, IN_VMEM, IN_VMEM] + ([IN_VMEM, ANY] if backward else []),
+        out_specs=[IN_VMEM, ANY] + ([IN_VMEM, IN_VMEM] if backward else []),
         scratch_shapes=[
-            pltpu.VMEM(part, BF16),
-            pltpu.VMEM(part, BF16),
-            pltpu.VMEM((rows - 1, length, width), BF16),
+            pltpu.VMEM(part, F32),
+            pltpu.VMEM(part, F32),
+            pltpu.VMEM(sent, BF16),
+            pltpu.VMEM(sent, BF16),
             pltpu.VMEM((length, width), BF16),
         ]
         + [dma(CHUNKS, rows)] * 3
         + [dma(CHUNKS, rows - 1)] * 2
         + [dma(CHUNKS)]
         + [dma(CHUNKS, rows - 1)] * 2
-        + [dma(CHUNKS, rows)] * 2,
+        + [dma(CHUNKS, rows)] * 2
+        + ([pltpu.VMEM(part, BF16)] + [dma(rows)] * 3 if backward else []),
         compiler_params=pltpu.CompilerParams(collective_id=ident, has_side_effects=True),
         cost_estimate=pl.CostEstimate(
             flops=0, bytes_accessed=150_000_000, transcendentals=0
         ),
-    )(x, gain, base, *([middle] if backward else []))
+    )(x, gain, base, *more)
 
 
 def swap_on(x, ident):
@@ -1527,7 +1573,11 @@
     gated_cut = gated.reshape(length, group, back_width).swapaxes(0, 1)
     gated_all = swap(gated_cut, 6).reshape(-1, back_width)
     middle, normed_two_all = turn(
-        blocks(mm(gated_all, output_weights, (1, 1))), mlp_row, inputs, None, 4
+        mm(gated_all, output_weights, (1, 1)).reshape(group, length, width),
+        mlp_row,
+        inputs,
+        (),
+        4,
     )
     normed_two_all = normed_two_all.reshape(-1, width)
 
@@ -1536,21 +1586,21 @@
     hidden_low = hidden.astype(BF16)
     grad_gate, grad_up = swiglu_pull(mm(grad_all, down))
     both_grad_low = jnp.concatenate([grad_gate, grad_up], axis=1).astype(BF16)
-    grad_normed_two_parts = blocks(mm(both_grad_low, gate_up, (1, 1)))
+    grad_normed_two_parts = mm(both_grad_low, gate_up, (1, 1)).reshape(group, length, width)
+    mlp_parts = blocks(mm(hidden_low, down, (1, 1)))
     gate_up_rows = mm(normed_two_all, both_grad_low, (0, 0)).astype(BF16)
     grad_normed_two_parts, gate_up_rows = lax.optimization_barrier(
         (grad_normed_two_parts, gate_up_rows)
     )
     gate_up_rows = scattered(gate_up_rows)
-    grad_middle, attended_grad_all, grad_mlp_gain = turn(
-        grad_normed_two_parts, mlp_row, grad_low, middle, 2
+    grad_middle, attended_grad_all, grad_mlp_gain, mlp_pairs = turn(
+        grad_normed_two_parts, mlp_row, grad_low, (middle, mlp_parts), 2
     )
     attended_grad_all = attended_grad_all.reshape(-1, width)
 
     grad_gated = joined(swap(blocks(mm(attended_grad_all, output_weights)), 6))
     output_rows = mm(attended_grad_all, gated_all, (0, 0)).astype(BF16)
     down_rows = mm(grad_all, hidden_low, (0, 0)).astype(BF16)
-    mlp_parts = blocks(mm(hidden_low, down, (1, 1)))
     mixed_grad, gate_pre_grad, gain_grad, state_add = head_call(
         gate_backward_kernel,
         heads,
@@ -1567,14 +1617,14 @@
     )
     grad_out_gain = jnp.sum(gain_grad, axis=(0, 1))
     side_rows = jnp.concatenate([down_rows, output_rows], axis=1)
-    state_add, mlp_parts, gate_up_rows, side_rows = lax.optimization_barrier(
-        (state_add, mlp_parts, gate_up_rows, side_rows)
+    state_add, gate_up_rows, side_rows = lax.optimization_barrier(
+        (state_add, gate_up_rows, side_rows)
     )
     ending, gate_grad_back, mlp_back = chain(
         back_high,
         back_low,
         state_add,
-        (gate_pre_grad.reshape(length, group, back_width).swapaxes(0, 1), mlp_parts),
+        (gate_pre_grad.reshape(length, group, back_width).swapaxes(0, 1), mlp_pairs),
         False,
         8,
     )
@@ -1672,11 +1722,12 @@
         grad_mlp_gain,
     )
     flat = jnp.concatenate([piece.reshape(-1) for piece in pieces])
-    lines = -(-flat.shape[0] // (8 * LANES)) * 8
-    flat = jnp.pad(flat, (0, lines * LANES - flat.shape[0])).reshape(lines, LANES)
-    flat = jnp.sum(spread(flat, 11), axis=0)
-    flat = jnp.sum(column(flat, 12), axis=0).reshape(-1)
-    mixer_rows, _ = lax.optimization_barrier((mixer_rows, (flat, grad_inputs, side_back)))
+    lines = -(-flat.shape[0] // (group * 8 * LANES)) * 8
+    flat = jnp.pad(flat, (0, group * lines * LANES - flat.shape[0])).reshape(group, lines, LANES)
+    flat = jnp.sum(swap(flat, 11), axis=0)
+    flat = jnp.sum(column(flat, 12), axis=0)
+    flat = spread(flat, 16).reshape(-1)
+    mixer_rows, _ = lax.optimization_barrier((mixer_rows, (flat, grad_inputs)))
     mixer_swapped = swap(
         jnp.concatenate(
             [mixer_rows[:, :, :mixer_part], mixer_rows[:, :, mixer_part + LANES :]], axis=2

time: 806 us -> 776 us (0.963)
  Pallas kernels: 536 us -> 502 us
    pallas_call x2, Pallas kernels: 93 us -> 70.8 us  [chain(): pl.pallas_call(partial(chain_kernel, count, rows, heads, len(sides), forw...]
    pallas_call x6 -> x7, Pallas kernels: 100 us -> 87.9 us  [comm_call(): pl.pallas_call(body, out_shape=out, in_specs=[spec] * len(operands), out_...]
    unnamed x91 -> x90, local copies, waits for them, and re-layouts: 18.7 us -> 19.3 us
  transfers between devices with their start and end apart: 8 -> 8, of which waited for: 1 -> 2; matrix products, arithmetic and copies ran while one was open for 17% -> 18% of each run, Pallas kernels for 45% -> 45%
where the time goes in v3:
time: 776 us; the launch traced here: 769 us
  Pallas kernels  502 us (65%)
  matrix products  106 us (14%)
  local copies, waits for them, and re-layouts  68 us (9%)
  waiting for transfers between devices  38.4 us (5%)
  other arithmetic  28.7 us (4%)
  between operations  14.9 us (2%)
  starting transfers between devices  10.7 us (1%)
    pallas_call x2, Pallas kernels, turn(): pl.pallas_call(partial(turn_kernel, rows, backward), out_shape=[jax.Shape...  112 us
    dot_general x16, matrix products, mm(): lax.dot_general(left, right, (((over[0],), (over[1],)), ((), ())), prefer...  105 us
    pallas_call x1, Pallas kernels, begin(): pl.pallas_call(partial(start_kernel, rows, count), out_shape=[jax.ShapeDt...  101 us
    pallas_call x7, Pallas kernels, comm_call(): pl.pallas_call(body, out_shape=out, in_specs=[spec] * len(operands), out_...  87.9 us
    pallas_call x4, Pallas kernels, head_call(): pl.pallas_call(body, scratch_shapes=scratch, grid=(heads,), in_specs=in_s...  81.5 us
    pallas_call x2, Pallas kernels, chain(): pl.pallas_call(partial(chain_kernel, count, rows, heads, len(sides), forw...  70.8 us
    all_gather x2, waiting for transfers between devices, gathered(): lax.all_gather(values.reshape(group * owned, -1), 'zq', axis=0, tiled=True)  30.7 us
    pallas_call x1, Pallas kernels, swap_back(): pl.pallas_call(partial(swap_back_kernel, rows, count), out_shape=jax.Shap...  26 us
  transfers between devices with their start and end apart: 8, of which 2 were waited for; matrix products, arithmetic and copies ran while one was open for 18% of the time, Pallas kernels for 45%

profile of v3, /device:TPU:0, one launch (start us, length us, event | category | flops | bytes accessed | tf_op | source)
XLA Modules:
  0.0 769.2 jit_solution(9195201298324252554)
XLA Ops:
  21.1 100.8 %shard_map.339 = (bf16[4,8,64,1280]{3,2,1,0:T(8,128)(2,1)}, bf16[8,64,1088]{2,1,0:T(8,128)(2,1)}, bf16[8,64,1408]{2,1,0:T(8,128)(2,1)}, bf16[8,128,2048]{2,1,0:T...) custom-call(bf16[128,2048]{1,0:T(8,128)(2,1)S(1)} %bitcast.137, ...), custom_call_target="tpu_custom_call" | custom-call | bytes 300000000 | tf_op jit(solution)/shard_map/pallas_call | solution.py:1025
  122.8 2.3 collective-permute-start
  128.1 8.5 %fusion.18 = bf16[1024,768]{1,0:T(8,128)(2,1)} fusion(bf16[1024,2048]{1,0:T(8,128)(2,1)} %bitcast.195, bf16[2048,1280]{1,0:T(8,128)(2,1)} %bitcast.175), kind=kOutput, calls=%fused_computation.32 | convolution fusion | flops 3222011904 | bytes 8912896 | tf_op jit(solution)/shard_map/dot_general | solution.py:32
  136.6 22.9 %shard_map.340 = (bf16[8,128,768]{2,1,0:T(8,128)(2,1)}, bf16[8,16,768]{2,1,0:T(8,128)(2,1)}) custom-call(bf16[8,128,768]{2,1,0:T(8,128)(2,1)} %bitcast.161), custom_call_target="tpu_custom_call" | custom-call | bytes 90000000 | tf_op jit(solution)/shard_map/pallas_call | solution.py:970
  161.1 6.2 fusion.21.refs_0_
  172.1 32.7 %shard_map.341 = (f32[6,128,128]{2,1,0:T(8,128)}, f32[6,128,128]{2,1,0:T(8,128)}, f32[128,3072]{1,0:T(8,128)}, f32[6,128,256]{2,1,0:T(8,128)}, f32[6,256,512]{2,...) custom-call(bf16[8,128,768]{2,1,0:T(8,128)(2,1)} %get-tuple-element., ...), custom_call_target="tpu_custom_call" | custom-call | flops 6000000000 | bytes 20000000 | tf_op jit(solution)/shard_map/pallas_call | solution.py:1353
  204.8 31.7 %shard_map.342 = (bf16[6,256,512]{2,1,0:T(8,128)(2,1)}, f32[8,128,384]{2,1,0:T(8,128)}) custom-call(bf16[6,256,256]{2,1,0:T(8,128)(2,1)} %get-tuple-element.85.high_ref, bf16[6,256,256]{2,1,0:T(8,128)(2,1)} %get-tuple-element.86.low_ref, f32[6,256,512]{2,1,0:T(8,128)} %get-tuple-element.87.add_ref, f32[8,128,384]{2,1,0:T(8,128)} %fusion.21.refs_0_), custom_call_target="tpu_custom_call" | custom-call | bytes 200000000 | tf_op jit(solution)/shard_map/pallas_call | solution.py:1086
  239.8 6.5 shard_map.343
  249.0 12.7 %shard_map.344 = bf16[8,128,384]{2,1,0:T(8,128)(2,1)} custom-call(bf16[8,128,384]{2,1,0:T(8,128)(2,1)} %bitcast.154), custom_call_target="tpu_custom_call" | custom-call | bytes 90000000 | tf_op jit(solution)/shard_map/pallas_call | solution.py:870
  261.7 7.3 fusion.22.x_ref
  269.0 55.7 %shard_map.345 = (f32[128,2048]{1,0:T(8,128)}, bf16[8,128,2048]{2,1,0:T(8,128)(2,1)}) custom-call(f32[8,128,2048]{2,1,0:T(8,128)} %fusion.22.x_ref, f32[1,2048]{1,0:T(1,128)} %bitcast.182, f32[128,2048]{1,0:T(8,128)} %convert_element_type.69.base_ref), custom_call_target="tpu_custom_call" | custom-call | bytes 150000000 | tf_op jit(solution)/shard_map/pallas_call | solution.py:933
  324.7 30.6 %all-gather.5.cloned.1.call-done = bf16[2048,1408]{1,0:T(8,128)(2,1)} async-done(((bf16[512,1408]{1,0:T(8,128)(2,1)}), bf16[2048,1408]{1,0:T(8,128)(2,1)}) %all-gather.5.cloned.1.call-update) | async-done | bytes 5767184 | tf_op jit(solution)/shard_map/all_gather | solution.py:1440
  355.4 10.9 %fusion.78 = f32[1024,1408]{0,1:T(8,128)S(1)} fusion(bf16[1024,2048]{1,0:T(8,128)(2,1)} %bitcast.199, bf16[2048,1408]{1,0:T(8,128)(2,1)} %all-gather.5.cloned.1.call-done), kind=kOutput, calls=%fused_computation.137 | convolution fusion | flops 5905580032 | bytes 15728640 | tf_op jit(solution)/shard_map/dot_general | solution.py:32
  366.3 6.8 fusion.9
  374.7 8.6 %convolution_convert_fusion = bf16[2048,1408]{1,0:T(8,128)(2,1)} fusion(bf16[1024,2048]{1,0:T(8,128)(2,1)S(1)} %bitcast.200, bf16[1024,704]{0,1:T(8,128)(2,1)S(1)} %get-tuple-element.216, bf16[1024,704]{0,1:T(8,128)(2,1)S(1)} %get-tuple-element.215), kind=kOutput, calls=%fused_computation | convolution fusion | flops 5914230784 | bytes 12845056 | tf_op jit(solution)/shard_map/dot_general | solution.py:32
  383.3 12.0 %fusion.17 = f32[1024,2048]{1,0:T(8,128)} fusion(bf16[2048,1408]{1,0:T(8,128)(2,1)} %all-gather.5.cloned.1.call-done, bf16[1024,704]{0,1:T(8,128)(2,1)} %copy-done.38, bf16[1024,704]{0,1:T(8,128)(2,1)} %copy-done.37), kind=kOutput, calls=%fused_computation.31 | convolution fusion | flops 5911347200 | bytes 17039360 | tf_op jit(solution)/shard_map/dot_general | solution.py:32
  395.4 7.5 convolution_convert_fusion.1
  402.9 56.7 %shard_map.346 = (f32[128,2048]{1,0:T(8,128)}, bf16[8,128,2048]{2,1,0:T(8,128)(2,1)}, f32[1,2048]{1,0:T(1,128)}, bf16[4,128,2048]{2,1,0:T(8,128)(2,1)}) custom-call(f32[8,128,2048]{2,1,0:T(8,128)} %bitcast.143, f32[1,2048]{1,0:T(1,128)} %bitcast.183, bf16[128,2048]{1,0:T(8,128)(2,1)} %copy-done.8, f32[128,2048]{1,0:T(8,128)} %get-tuple-element.94.refs_0_, ...), custom_call_target="tpu_custom_call" | custom-call | bytes 150000000 | tf_op jit(solution)/shard_map/pallas_call | solution.py:933
  459.6 5.9 convolution_convert_fusion.3
  465.5 12.3 %shard_map.347 = bf16[8,128,384]{2,1,0:T(8,128)(2,1)} custom-call(bf16[8,128,384]{2,1,0:T(8,128)(2,1)} %bitcast.164), custom_call_target="tpu_custom_call" | custom-call | bytes 90000000 | tf_op jit(solution)/shard_map/pallas_call | solution.py:870
  477.8 2.1 copy.232
  480.0 8.3 %shard_map.348 = (f32[128,3072]{1,0:T(8,128)}, bf16[128,3072]{1,0:T(8,128)(2,1)}, f32[6,1,512]{2,1,0:T(1,128)}, f32[6,256,512]{2,1,0:T(8,128)}) custom-call(f32[128,3072]{1,0:T(8,128)} %get-tuple-element.97.mixed_ref, f32[128,3072]{1,0:T(8,128)} %bitcast.142, f32[1,512]{1,0:T(1,128)} %bitcast.187, bf16[128,3072]{1,0:T(8,128)(2,1)} %bitcast.157, ...), custom_call_target="tpu_custom_call" | custom-call | flops 1000000000 | bytes 20000000 | tf_op jit(solution)/shard_map/pallas_call | solution.py:1353
  491.0 4.2 bitcast_convert_fusion.2
  495.2 3.4 convolution_convert_fusion.2
  498.6 2.6 pad_maximum_fusion.1
  501.2 39.1 %shard_map.349 = (bf16[6,256,512]{2,1,0:T(8,128)(2,1)}, bf16[8,128,384]{2,1,0:T(8,128)(2,1)}, bf16[4,128,2048]{2,1,0:T(8,128)(2,1)}) custom-call(bf16[6,256,256]{2,1,0:T(8,128)(2,1)} %get-tuple-element.95.high_ref, bf16[6,256,256]{2,1,0:T(8,128)(2,1)} %get-tuple-element.96.low_ref, f32[6,256,512]{2,1,0:T(8,128)} %get-tuple-element.106.add_ref, ...), custom_call_target="tpu_custom_call" | custom-call | bytes 200000000 | tf_op jit(solution)/shard_map/pallas_call | solution.py:1086
  540.3 3.6 all-to-all-start
  544.0 33.9 %shard_map.350 = (bf16[8,128,768]{2,1,0:T(8,128)(2,1)}, f32[8,16,768]{2,1,0:T(8,128)}, bf16[8,16,768]{2,1,0:T(8,128)(2,1)}, f32[8,8,768]{2,1,0:T(8,128)}, f32[6,...) custom-call(bf16[8,128,768]{2,1,0:T(8,128)(2,1)} %get-tuple-element.79.refs_0_.refs_1_.ref, ...), custom_call_target="tpu_custom_call" | custom-call | flops 12000000000 | bytes 20000000 | tf_op jit(solution)/shard_map/pallas_call | solution.py:1353
  584.7 4.2 bitcast_convert_fusion.1
  589.0 26.0 %shard_map.351 = bf16[8,128,896]{2,1,0:T(8,128)(2,1)} custom-call(bf16[8,128,768]{2,1,0:T(8,128)(2,1)} %get-tuple-element.119.x_ref, f32[8,16,768]{2,1,0:T(8,128)} %get-tuple-element.120.tail_ref, bf16[8,16,768]{2,1,0:T(8,128)(2,1)} %get-tuple-element.121.rim_ref, bf16[128,128]{1,0:T(8,128)(2,1)} %pad.12.small_ref), custom_call_target="tpu_custom_call" | custom-call | bytes 90000000 | tf_op jit(solution)/shard_map/pallas_call | solution.py:995
  614.9 6.9 bitcast_convert_fusion
  621.8 2.8 pad_maximum_fusion
  624.6 2.4 copy.215
  627.9 2.1 convert_reduce_fusion.1
  631.0 1.8 reshape.229
  635.5 9.7 %fusion.2 = bf16[1024,2048]{1,0:T(8,128)(2,1)} fusion(bf16[2048,1280]{1,0:T(8,128)(2,1)} %bitcast.177, bf16[1024,384]{1,0:T(8,128)(2,1)S(1)} %bitcast.201, bf16[1024,768]{1,0:T(8,128)(2,1)S(1)} %slice.196), kind=kOutput, calls=%fused_computation.9 | convolution fusion | flops 4838653952 | bytes 11272192 | tf_op jit(solution)/shard_map/dot_general | solution.py:32
  645.1 28.8 %shard_map.352 = bf16[4,128,2048]{2,1,0:T(8,128)(2,1)} custom-call(bf16[8,128,2048]{2,1,0:T(8,128)(2,1)} %bitcast.151), custom_call_target="tpu_custom_call" | custom-call | bytes 90000000 | tf_op jit(solution)/shard_map/pallas_call | solution.py:870
  673.9 2.1 convert_reduce_fusion
  678.5 5.5 shard_map.353
  685.5 6.4 shard_map.354
  693.4 6.5 shard_map.355
  708.8 4.5 all-to-all-start.1
  718.2 1.7 reshape.261
  720.8 1.7 reshape.259
  722.4 7.7 all-to-all-done.1
  731.7 2.1 copy.223
  733.8 2.8 reshape.253
  740.7 15.7 %shard_map.356 = bf16[8,64,1152]{2,1,0:T(8,128)(2,1)} custom-call(bf16[8,64,1152]{2,1,0:T(8,128)(2,1)} %pad_maximum_fusion.5.x_ref), custom_call_target="tpu_custom_call" | custom-call | bytes 90000000 | tf_op jit(solution)/shard_map/pallas_call | solution.py:870
  (195 shorter events, 77.0 us)
Async XLA Ops:
  7.2 229.4 %all-gather.3.cloned.1.call-start = ((), (), s32[]{:S(2)}) async-start(), calls=%async_computation.5 | async-start | bytes 5898240 | tf_op jit(solution)/shard_map/all_gather | solution.py:1440
  8.8 1.4 copy-start
  10.2 1.4 copy-start.1
  11.5 1.4 copy-start.2
  12.9 1.1 copy-start.3
  14.0 1.1 copy-start.4
  15.1 1.1 copy-start.5
  16.3 1.0 copy-start.6
  17.3 1.0 copy-start.7
  18.4 1.0 copy-start.9
  19.4 1.0 copy-start.10
  20.4 0.7 copy-start.11
  21.1 101.7 %copy-start.26 = (s32[1,128]{1,0:T(1,128)S(1)}, s32[1,128]{1,0:T(1,128)}, u32[]{:S(2)}) copy-start(s32[1,128]{1,0:T(1,128)} %param.21) | copy-start | bytes 1540
  121.9 0.8 copy-start.8
  122.7 232.7 %all-gather.5.cloned.1.call-start = ((), (), s32[]{:S(2)}) async-start(), calls=%async_computation.6 | async-start | bytes 7208960 | tf_op jit(solution)/shard_map/all_gather | solution.py:1440
  122.8 44.4 %collective-permute-start = (s32[3]{0:T(128)S(1)}, s32[3]{0:T(128)S(1)}, u32[]{:S(2)}, u32[]{:S(2)}) collective-permute-start(s32[3]{0:T(128)S(1)} %slice_bitcast_fusion.7), channel_id=1, source_target_pairs={{0,1},{1,2},{2,3},{3,4},{4,5},{5,6},{6,7},{8,9},{9,10},{10,11},{11... | collective-permute-start | bytes 44 | tf_op jit(solution)/shard_map/ppermute | solution.py:1484
  128.0 31.5 %copy-start.33 = (f32[6]{0:T(128)S(1)}, f32[6]{0:T(128)}, u32[]{:S(2)}) copy-start(f32[6]{0:T(128)} %param.30) | copy-start | bytes 76
  128.0 32.0 %copy-start.22 = (f32[4,1536]{1,0:T(4,128)S(1)}, f32[4,1536]{1,0:T(4,128)}, u32[]{:S(2)}) copy-start(f32[4,1536]{1,0:T(4,128)} %param.31) | copy-start | bytes 73732
  128.0 32.0 %copy-start.23 = (f32[4,1536]{1,0:T(4,128)S(1)}, f32[4,1536]{1,0:T(4,128)}, u32[]{:S(2)}) copy-start(f32[4,1536]{1,0:T(4,128)} %param.32) | copy-start | bytes 73732
  128.1 33.0 %copy-start.21 = (f32[4,3072]{1,0:T(4,128)S(1)}, f32[4,3072]{1,0:T(4,128)}, u32[]{:S(2)}) copy-start(f32[4,3072]{1,0:T(4,128)} %param.33) | copy-start | bytes 147460
  161.0 6.2 copy-start.28
  204.8 32.0 %copy-start.27 = (f32[2048]{0:T(1024)S(1)}, f32[2048]{0:T(1024)}, u32[]{:S(2)}) copy-start(f32[2048]{0:T(1024)} %param.36) | copy-start | bytes 24580
  236.5 2.0 copy-start.18
  236.6 264.6 %reduce-scatter.4.cloned.1.call-start = ((), (), s32[]{:S(2)}) async-start(), calls=%async_computation.7 | async-start | bytes 7208960 | tf_op jit(solution)/shard_map/reduce_scatter | solution.py:1443
  355.4 10.9 %copy-start.29 = (bf16[8,128,2048]{2,1,0:T(8,128)(2,1)S(1)}, bf16[8,128,2048]{2,1,0:T(8,128)(2,1)}, u32[]{:S(2)}) copy-start(bf16[8,128,2048]{2,1,0:T(8,128)(2,1)} %get-tuple-element.98) | copy-start | bytes 12582916
  366.3 8.4 %copy-start.31 = (bf16[8,128,2048]{2,1,0:T(8,128)(2,1)S(1)}, bf16[8,128,2048]{2,1,0:T(8,128)(2,1)}, u32[]{:S(2)}) copy-start(bf16[8,128,2048]{2,1,0:T(8,128)(2,1)} %get-tuple-element.99) | copy-start | bytes 12582916
  373.1 1.1 copy-start.37
  373.1 1.6 copy-start.38
  373.2 22.3 %copy-start.35 = (bf16[1024,704]{0,1:T(8,128)(2,1)}, bf16[1024,704]{0,1:T(8,128)(2,1)S(1)}, u32[]{:S(2)}) copy-start(bf16[1024,704]{0,1:T(8,128)(2,1)S(1)} %get-tuple-element.217) | copy-start | bytes 4325380
  395.4 229.2 %reduce-scatter.6.cloned.1.call-start = ((), (), s32[]{:S(2)}) async-start(), calls=%async_computation.8 | async-start | bytes 5570560 | tf_op jit(solution)/shard_map/reduce_scatter | solution.py:1443
  480.0 11.0 %copy-start.17 = (bf16[8,128,384]{2,1,0:T(8,128)(2,1)S(1)}, bf16[8,128,384]{2,1,0:T(8,128)(2,1)}, u32[]{:S(2)}) copy-start(bf16[8,128,384]{2,1,0:T(8,128)(2,1)} %shard_map.344) | copy-start | bytes 2359300
  491.0 4.2 copy-start.30
  491.0 4.2 copy-start.36
  540.3 48.6 %all-to-all-start = ((bf16[8,64,1408]{2,1,0:T(8,128)(2,1)}), bf16[8,64,1408]{2,1,0:T(8,128)(2,1)S(1)}, u32[]{:S(2)}, u32[]{:S(2)}) async-start(bf16[8,64,1408]{2,1,0:T(8,128)(2,1)} %bitcast.36), calls=%async_computation.1 | async-start | bytes 2883584 | tf_op jit(solution)/shard_map/all_to_all | solution.py:1634
  543.9 193.9 %reduce-scatter.8.cloned.1.call-start = ((), (), s32[]{:S(2)}) async-start(), calls=%async_computation.9 | async-start | bytes 6553600 | tf_op jit(solution)/shard_map/reduce_scatter | solution.py:1443
  584.1 0.6 copy-start.19
  588.9 32.9 %copy-start.14 = (bf16[8,64,1408]{2,1,0:T(8,128)(2,1)}, bf16[8,64,1408]{2,1,0:T(8,128)(2,1)S(1)}, u32[]{:S(2)}) copy-start(bf16[8,64,1408]{2,1,0:T(8,128)(2,1)S(1)} %all-to-all-done) | copy-start | bytes 4325380
  627.0 0.7 copy-start.12
  627.0 0.9 copy-start.24
  627.0 3.0 copy-start.16
  630.0 5.3 copy-start.34
  630.0 5.3 copy-start.13
  634.2 1.2 copy-start.32
  673.9 2.2 copy-start.20
  673.9 3.8 copy-start.25
  708.8 21.3 %all-to-all-start.1 = ((bf16[8,64,1088]{2,1,0:T(8,128)(2,1)}), bf16[8,64,1088]{2,1,0:T(8,128)(2,1)}, u32[]{:S(2)}, u32[]{:S(2)}) async-start(bf16[8,64,1088]{2,1,0:T(8,128)(2,1)} %bitcast.60), calls=%async_computation.4 | async-start | bytes 2359296 | tf_op jit(solution)/shard_map/all_to_all | solution.py:1709
  713.3 3.5 copy-start.15
Sparse Core Ops, SparseCore 0:
  122.8 89.2 all-gather.2
  236.7 118.6 all-gather.4
  395.5 100.5 reduce-scatter.3
  540.5 81.6 reduce-scatter.5
  627.1 92.7 reduce-scatter.7

commit v4 on v3

--- a/solution.py
+++ b/solution.py
@@ -1047,7 +1047,7 @@
         ]
         + [dma(count - 1, group)] * 4,
         compiler_params=pltpu.CompilerParams(
-            collective_id=ident, has_side_effects=True, vmem_limit_bytes=40 << 20
+            collective_id=ident, has_side_effects=True
         ),
         cost_estimate=pl.CostEstimate(
             flops=0, bytes_accessed=300_000_000, transcendentals=0
@@ -1105,26 +1105,32 @@
     )(high, low, add, *sides)
 
 
-def unit_lower_inverse(low):
-    size = low.shape[0]
-    row = lax.broadcasted_iota(jnp.int32, low.shape, 0)
-    col = lax.broadcasted_iota(jnp.int32, low.shape, 1)
+def unit_lower_inverses(lows):
+    shape = lows[0].shape
+    row = lax.broadcasted_iota(jnp.int32, shape, 0)
+    col = lax.broadcasted_iota(jnp.int32, shape, 1)
 
     def same(width):
         shift = width.bit_length() - 1
         return (row >> shift) == (col >> shift)
 
+    def products(lefts, rights):
+        return [exact(left, right) for left, right in zip(lefts, rights)]
+
     eye = (row == col).astype(F32)
     width = 8
-    near = jnp.where(same(width), low, 0.0)
-    square = exact(near, near)
-    inverse = eye - near
-    inverse = inverse + exact(inverse, square)
-    square = exact(square, square)
-    inverse = inverse + exact(inverse, square)
-    while width < size:
-        cross = jnp.where(same(2 * width) & jnp.logical_not(same(width)), low, 0.0)
-        inverse = inverse - exact(inverse, exact(cross, inverse))
+    near = [jnp.where(same(width), low, 0.0) for low in lows]
+    square = products(near, near)
+    inverse = [eye - block for block in near]
+    inverse = [x + y for x, y in zip(inverse, products(inverse, square))]
+    square = products(square, square)
+    inverse = [x + y for x, y in zip(inverse, products(inverse, square))]
+    while width < shape[0]:
+        picked = same(2 * width) & jnp.logical_not(same(width))
+        cross = [jnp.where(picked, low, 0.0) for low in lows]
+        inverse = [
+            x - y for x, y in zip(inverse, products(inverse, products(cross, inverse)))
+        ]
         width *= 2
     return inverse
 
@@ -1175,11 +1181,10 @@
     return values * sig, sig * (1.0 + values * (1.0 - sig))
 
 
-def chunk_forward_kernel(
-    *refs,
-):
-    pre_refs, rim_refs, tap_refs = refs[:4], refs[4:8], refs[8:12]
-    same_ref, beta_ref, decay_ref, start_ref, tail_ref = refs[12:17]
+def chunk_forward_kernel(step, *refs):
+    count = 4 * step
+    pre_refs, rim_refs, tap_refs = refs[:count], refs[count : 2 * count], refs[2 * count : 3 * count]
+    same_ref, lines_ref, decay_ref = refs[3 * count : 3 * count + 3]
     (
         inverse_ref,
         scores_ref,
@@ -1190,39 +1195,50 @@
         low_ref,
         back_high_ref,
         back_low_ref,
-    ) = refs[17:26]
-    ext = refs[26]
-    active = []
-    for i in range(4):
-        mixed = convolve(pre_refs[i], rim_refs[i], tap_refs[i], same_ref, ext.at[i])
-        active.append(silu_parts(mixed)[0])
-    size, key_size = active[0].shape
-    beta, start, tail = beta_ref[0], start_ref[0], tail_ref[0]
-    decay = decay_ref[0]
-    query = unit_parts(active[0])[0] * key_size ** (-0.5)
-    key = unit_parts(active[1])[0]
-    values = jnp.concatenate(active[2:], axis=1)
-    inner = exact(key, key, (1, 1))
-    inverse = unit_lower_inverse(beta * inner * (decay * strict_lower(size)))
-    scores = exact(query, key, (1, 1)) * decay
-    update = exact(inverse, beta * values)
-    reach = exact(inverse, (beta * start) * key)
-    inverse_ref[0] = inverse
-    scores_ref[0] = scores
-    own_ref[...] = exact(scores, update)
-    effect_ref[0] = start * query - exact(scores, reach)
-    last = tail * key
-    offset_ref[0] = exact(last, update, (0, 0))
+    ) = refs[3 * count + 3 : 3 * count + 12]
+    ext = refs[3 * count + 12]
+    heads, lows = [], []
+    for u in range(step):
+        active = []
+        for i in range(4 * u, 4 * u + 4):
+            mixed = convolve(pre_refs[i], rim_refs[i], tap_refs[i], same_ref, ext.at[i])
+            active.append(silu_parts(mixed)[0])
+        size, key_size = active[0].shape
+        columns = lines_ref[u].T
+        beta, start, tail = columns[:, 0:1], columns[:, 1:2], columns[:, 2:3]
+        decay = decay_ref[u]
+        query = unit_parts(active[0])[0] * key_size ** (-0.5)
+        key = unit_parts(active[1])[0]
+        values = jnp.concatenate(active[2:], axis=1)
+        inner = exact(key, key, (1, 1))
+        lows.append(beta * inner * (decay * strict_lower(size)))
+        heads.append((query, key, values, beta, start, tail, decay))
+    inverses = unit_lower_inverses(lows)
     row = lax.broadcasted_iota(jnp.int32, (key_size, key_size), 0)
     col = lax.broadcasted_iota(jnp.int32, (key_size, key_size), 1)
-    transfer = jnp.where(row == col, start[size - 1 :, :], 0.0) - exact(last, reach, (0, 0))
-    for matrix, top_ref, rest_ref in (
-        (transfer, high_ref, low_ref),
-        (transfer.T, back_high_ref, back_low_ref),
-    ):
-        top = matrix.astype(BF16)
-        top_ref[0] = top
-        rest_ref[0] = (matrix - top.astype(F32)).astype(BF16)
+    for u in range(step):
+        query, key, values, beta, start, tail, decay = heads[u]
+        inverse = inverses[u]
+        width = values.shape[1]
+        scores = exact(query, key, (1, 1)) * decay
+        update = exact(inverse, beta * values)
+        reach = exact(inverse, (beta * start) * key)
+        inverse_ref[u] = inverse
+        scores_ref[u] = scores
+        own_ref[:, u * width : (u + 1) * width] = exact(scores, update)
+        effect_ref[u] = start * query - exact(scores, reach)
+        last = tail * key
+        offset_ref[u] = exact(last, update, (0, 0))
+        transfer = jnp.where(row == col, start[size - 1 :, :], 0.0) - exact(
+            last, reach, (0, 0)
+        )
+        for matrix, top_ref, rest_ref in (
+            (transfer, high_ref, low_ref),
+            (transfer.T, back_high_ref, back_low_ref),
+        ):
+            top = matrix.astype(BF16)
+            top_ref[u] = top
+            rest_ref[u] = (matrix - top.astype(F32)).astype(BF16)
 
 
 def gate_forward_kernel(own_ref, effect_ref, state_ref, gate_ref, gain_ref, mixed_ref, gated_ref):
@@ -1257,19 +1273,17 @@
 
 def chunk_backward_kernel(heads, *refs):
     pre_refs, rim_refs, tap_refs = refs[:4], refs[4:8], refs[8:12]
-    same_ref, beta_ref, decay_ref, start_ref, tail_ref = refs[12:17]
-    inverse_ref, scores_ref, state_ref, mixed_ref, ending_ref = refs[17:22]
+    same_ref, lines_ref, decay_ref = refs[12:15]
+    inverse_ref, scores_ref, state_ref, mixed_ref, ending_ref = refs[15:20]
     (
         grad_ref,
         grad_tail_ref,
         grad_rim_ref,
         taps_grad_ref,
-        dbeta_ref,
+        dlines_ref,
         ddecay_ref,
-        dstart_ref,
-        dtail_ref,
-    ) = refs[22:30]
-    ext, back = refs[30:]
+    ) = refs[20:26]
+    ext, back = refs[26:]
     active, slopes = [], []
     for i in range(4):
         mixed = convolve(pre_refs[i], rim_refs[i], tap_refs[i], same_ref, ext.at[i])
@@ -1278,7 +1292,8 @@
         slopes.append(slope)
     size, key_size = active[0].shape
     values = jnp.concatenate(active[2:], axis=1)
-    beta, start, tail = beta_ref[0], start_ref[0], tail_ref[0]
+    columns = lines_ref[0].T
+    beta, start, tail = columns[:, 0:1], columns[:, 1:2], columns[:, 2:3]
     decay, inverse, scores = decay_ref[0], inverse_ref[0], scores_ref[0]
     state = state_ref[0].astype(F32)
     ending = ending_ref[0].astype(F32)
@@ -1310,17 +1325,20 @@
         + exact(dinner, key, (0, 0))
     )
     right_recalled = jnp.sum(dright * recalled, axis=-1, keepdims=True)
-    dbeta_ref[0] = jnp.sum(dright * miss, axis=-1, keepdims=True) + jnp.sum(
+    dbeta = jnp.sum(dright * miss, axis=-1, keepdims=True) + jnp.sum(
         dlower * inner * decay, axis=-1, keepdims=True
     )
     final = jnp.sum(jnp.sum(ending * state, axis=-1, keepdims=True), axis=0, keepdims=True)
     row = lax.broadcasted_iota(jnp.int32, (size, 1), 0)
-    dstart_ref[0] = (
+    dstart = (
         jnp.sum(query * mixed_state, axis=-1, keepdims=True)
         - beta * right_recalled
         + jnp.where(row == size - 1, final, 0.0)
     )
-    dtail_ref[0] = jnp.sum(key * dlast, axis=-1, keepdims=True)
+    dtail = jnp.sum(key * dlast, axis=-1, keepdims=True)
+    dlines_ref[0] = jnp.concatenate(
+        [dbeta, dstart, dtail, jnp.zeros((size, 5), F32)], axis=1
+    ).T
     ddecay_ref[0] = dscores * raw + beta * dlower * inner
     dvalues = beta * dright
     grads = [
@@ -1345,6 +1363,10 @@
     return pl.BlockSpec((1,) + shape, lambda h: (h, 0, 0))
 
 
+def by_heads(step, *shape):
+    return pl.BlockSpec((step,) + shape, lambda h: (h, 0, 0))
+
+
 def by_columns(rows, width, offset=0):
     return pl.BlockSpec((rows, width), lambda h: (0, h + offset))
 
@@ -1379,7 +1401,8 @@
     live_last = segment == segment[-1]
     last_gap = running[:, -1:] - running
     tail = jnp.where(live_last, jnp.exp(jnp.where(live_last, last_gap, 0.0)), 0.0)
-    return beta.T[:, :, None], decay, start[:, :, None], tail[:, :, None]
+    filler = jnp.zeros((5,) + start.shape, F32)
+    return jnp.moveaxis(jnp.concatenate([jnp.stack([beta.T, start, tail]), filler]), 0, 1), decay
 
 
 def local(
@@ -1494,7 +1517,7 @@
         ],
         axis=1,
     )
-    (beta, decay, start, tail), decay_pull = jax.vjp(
+    (lines, decay), decay_pull = jax.vjp(
         partial(decays, segment, seg_ext[margin - 1]), decay_pre, beta_pre, a_log
     )
     slabs, slab = group, mixer_part
@@ -1512,35 +1535,45 @@
         lambda h: 2 * heads + 2 * h + 1,
     ]
 
-    def slab_specs(lines):
+    step = 2 if heads % 2 == 0 else 1
+
+    def at_blocks(make, step):
         return [
-            pl.BlockSpec((1, lines, key_size), lambda h, b=b: (b(h) // per, 0, b(h) % per))
-            for b in channel_blocks
+            make(lambda h, b=b, u=u: b(step * h + u)) for u in range(step) for b in channel_blocks
         ]
 
-    token_specs = (
-        slab_specs(length)
-        + slab_specs(RIM)
-        + [pl.BlockSpec((CONV, key_size), lambda h, b=b: (0, b(h))) for b in channel_blocks]
-        + [pl.BlockSpec((length, CONV), lambda h: (0, 0))]
-        + [by_head(length, 1), by_head(length, length), by_head(length, 1), by_head(length, 1)]
-    )
-    token_args = (pre,) * 4 + (rim,) * 4 + (taps,) * 4 + (same, beta, decay, start, tail)
-    ext_shape = pltpu.VMEM((4, RIM + length, key_size), F32)
+    def token_specs(step):
+        def in_slab(lines):
+            return lambda at: pl.BlockSpec(
+                (1, lines, key_size), lambda h: (at(h) // per, 0, at(h) % per)
+            )
+
+        return (
+            at_blocks(in_slab(length), step)
+            + at_blocks(in_slab(RIM), step)
+            + at_blocks(lambda at: pl.BlockSpec((CONV, key_size), lambda h: (0, at(h))), step)
+            + [pl.BlockSpec((length, CONV), lambda h: (0, 0))]
+            + [by_heads(step, 8, length), by_heads(step, length, length)]
+        )
+
+    def token_args(step):
+        blocks = 4 * step
+        return (pre,) * blocks + (rim,) * blocks + (taps,) * blocks + (same, lines, decay)
+
     values_spec = by_columns(length, value_size)
     state_spec = by_head(key_size, value_size)
     inverse, scores, own, effect, offset, high, low, back_high, back_low = head_call(
-        chunk_forward_kernel,
-        heads,
-        token_specs,
+        partial(chunk_forward_kernel, step),
+        heads // step,
+        token_specs(step),
         [
-            by_head(length, length),
-            by_head(length, length),
-            values_spec,
-            by_head(length, key_size),
-            state_spec,
+            by_heads(step, length, length),
+            by_heads(step, length, length),
+            by_columns(length, step * value_size),
+            by_heads(step, length, key_size),
+            by_heads(step, key_size, value_size),
         ]
-        + [by_head(key_size, key_size)] * 4,
+        + [by_heads(step, key_size, key_size)] * 4,
         [
             shaped(heads, length, length),
             shaped(heads, length, length),
@@ -1549,9 +1582,9 @@
             shaped(heads, key_size, value_size),
         ]
         + [shaped(heads, key_size, key_size, dtype=BF16)] * 4,
-        token_args,
+        token_args(step),
         6_000_000_000,
-        [ext_shape],
+        [pltpu.VMEM((4 * step, RIM + length, key_size), F32)],
     )
     state, gate_back = chain(high, low, offset, (gate_all.reshape(group, length, -1),), True, 5)
     gate_pre = joined(gate_back)
@@ -1633,10 +1666,10 @@
     side_rows = scattered(side_rows)
     gate_up_back = lax.all_to_all(gate_up_rows, ("dp", "c"), 0, 0, tiled=True)
     whole = lambda *shape: pl.BlockSpec(shape, lambda h: (0, 0, 0))
-    grad_pre, grad_tail, grad_rim, grad_taps, dbeta, ddecay, dstart, dtail = head_call(
+    grad_pre, grad_tail, grad_rim, grad_taps, dlines, ddecay = head_call(
         partial(chunk_backward_kernel, heads),
         heads,
-        token_specs
+        token_specs(1)
         + [
             by_head(length, length),
             by_head(length, length),
@@ -1650,22 +1683,20 @@
             whole(slabs, RIM, slab),
             whole(slabs, 2 * CONV, slab),
         ]
-        + [by_head(length, 1), by_head(length, length), by_head(length, 1), by_head(length, 1)],
+        + [by_head(8, length), by_head(length, length)],
         [
             shaped(slabs, length, slab, dtype=BF16),
             shaped(slabs, RIM, slab),
             shaped(slabs, RIM, slab, dtype=BF16),
             shaped(slabs, 2 * CONV, slab),
-            shaped(heads, length, 1),
+            shaped(heads, 8, length),
             shaped(heads, length, length),
-            shaped(heads, length, 1),
-            shaped(heads, length, 1),
         ],
-        token_args + (inverse, scores, state, mixed_grad, ending),
+        token_args(1) + (inverse, scores, state, mixed_grad, ending),
         12_000_000_000,
-        [ext_shape, pltpu.VMEM((RIM + length, key_size), F32)],
-    )
-    grad_decay, grad_beta, grad_alog = decay_pull((dbeta, ddecay, dstart, dtail))
+        [pltpu.VMEM((4, RIM + length, key_size), F32), pltpu.VMEM((RIM + length, key_size), F32)],
+    )
+    grad_decay, grad_beta, grad_alog = decay_pull((dlines, ddecay))
     grad_taps = joined(grad_taps)[:CONV]
     grad_conv_one = grad_taps[:, :key_width]
     grad_conv_two = grad_taps[:, key_width : 2 * key_width]

time: 776 us -> 755 us (0.973)
  local copies, waits for them, and re-layouts: 68 us -> 54 us
    unnamed x90 -> x68, local copies, waits for them, and re-layouts: 19.3 us -> 7.67 us
    pallas_call x4, Pallas kernels: 81.5 us -> 73.2 us  [head_call(): pl.pallas_call(body, scratch_shapes=scratch, grid=(heads,), in_specs=in_s...]
  transfers between devices with their start and end apart: 8 -> 8, of which waited for: 2 -> 3; matrix products, arithmetic and copies ran while one was open for 18% -> 17% of each run, Pallas kernels for 45% -> 46%
where the time goes in v4:
time: 755 us; the launch traced here: 749 us
  Pallas kernels  498 us (66%)
  matrix products  106 us (14%)
  local copies, waits for them, and re-layouts  54 us (7%)
  waiting for transfers between devices  39.3 us (5%)
  other arithmetic  25.8 us (3%)
  between operations  14.8 us (2%)
  starting transfers between devices  10.7 us (1%)
    pallas_call x2, Pallas kernels, turn(): pl.pallas_call(partial(turn_kernel, rows, backward), out_shape=[jax.Shape...  112 us
    dot_general x16, matrix products, mm(): lax.dot_general(left, right, (((over[0],), (over[1],)), ((), ())), prefer...  105 us
    pallas_call x1, Pallas kernels, begin(): pl.pallas_call(partial(start_kernel, rows, count), out_shape=[jax.ShapeDt...  102 us
    pallas_call x7, Pallas kernels, comm_call(): pl.pallas_call(body, out_shape=out, in_specs=[spec] * len(operands), out_...  90.7 us
    pallas_call x4, Pallas kernels, head_call(): pl.pallas_call(body, scratch_shapes=scratch, grid=(heads,), in_specs=in_s...  73.2 us
    pallas_call x2, Pallas kernels, chain(): pl.pallas_call(partial(chain_kernel, count, rows, heads, len(sides), forw...  70.8 us
    all_gather x2, waiting for transfers between devices, gathered(): lax.all_gather(values.reshape(group * owned, -1), 'zq', axis=0, tiled=True)  31.3 us
    pallas_call x1, Pallas kernels, swap_back(): pl.pallas_call(partial(swap_back_kernel, rows, count), out_shape=jax.Shap...  26.1 us
  transfers between devices with their start and end apart: 8, of which 3 were waited for; matrix products, arithmetic and copies ran while one was open for 17% of the time, Pallas kernels for 46%

profile of v4, /device:TPU:0, one launch (start us, length us, event | category | flops | bytes accessed | tf_op | source)
XLA Modules:
  0.0 748.7 jit_solution(15538049468833793429)
XLA Ops:
  10.0 102.0 %shard_map.339 = (bf16[4,8,64,1280]{3,2,1,0:T(8,128)(2,1)}, bf16[8,64,1088]{2,1,0:T(8,128)(2,1)}, bf16[8,64,1408]{2,1,0:T(8,128)(2,1)}, bf16[8,128,2048]{2,1,0:T...) custom-call(bf16[128,2048]{1,0:T(8,128)(2,1)} %bitcast.200, ...), custom_call_target="tpu_custom_call" | custom-call | bytes 300000000 | tf_op jit(solution)/shard_map/pallas_call | solution.py:1025
  112.2 2.3 collective-permute-start
  116.8 8.3 %fusion.18 = bf16[1024,768]{1,0:T(8,128)(2,1)} fusion(bf16[1024,2048]{1,0:T(8,128)(2,1)} %bitcast.236, bf16[2048,1280]{1,0:T(8,128)(2,1)} %bitcast.212), kind=kOutput, calls=%fused_computation.32 | convolution fusion | flops 3222011904 | bytes 8912896 | tf_op jit(solution)/shard_map/dot_general | solution.py:32
  125.1 23.0 %shard_map.340 = (bf16[8,128,768]{2,1,0:T(8,128)(2,1)}, bf16[8,16,768]{2,1,0:T(8,128)(2,1)}) custom-call(bf16[8,128,768]{2,1,0:T(8,128)(2,1)} %bitcast.194), custom_call_target="tpu_custom_call" | custom-call | bytes 90000000 | tf_op jit(solution)/shard_map/pallas_call | solution.py:970
  149.7 6.3 fusion.21.refs_0_
  159.5 24.3 %shard_map.341 = (f32[6,128,128]{2,1,0:T(8,128)}, f32[6,128,128]{2,1,0:T(8,128)}, f32[128,3072]{1,0:T(8,128)}, f32[6,128,256]{2,1,0:T(8,128)}, f32[6,256,512]{2,...) custom-call(bf16[8,128,768]{2,1,0:T(8,128)(2,1)} %get-tuple-element., ...), custom_call_target="tpu_custom_call" | custom-call | flops 6000000000 | bytes 20000000 | tf_op jit(solution)/shard_map/pallas_call | solution.py:1375
  183.8 31.7 %shard_map.342 = (bf16[6,256,512]{2,1,0:T(8,128)(2,1)}, f32[8,128,384]{2,1,0:T(8,128)}) custom-call(bf16[6,256,256]{2,1,0:T(8,128)(2,1)} %get-tuple-element.83.high_ref, bf16[6,256,256]{2,1,0:T(8,128)(2,1)} %get-tuple-element.84.low_ref, f32[6,256,512]{2,1,0:T(8,128)} %get-tuple-element.85.add_ref, f32[8,128,384]{2,1,0:T(8,128)} %fusion.21.refs_0_), custom_call_target="tpu_custom_call" | custom-call | bytes 200000000 | tf_op jit(solution)/shard_map/pallas_call | solution.py:1086
  218.9 6.5 shard_map.343
  228.1 14.9 %shard_map.344 = bf16[8,128,384]{2,1,0:T(8,128)(2,1)} custom-call(bf16[8,128,384]{2,1,0:T(8,128)(2,1)} %bitcast.187), custom_call_target="tpu_custom_call" | custom-call | bytes 90000000 | tf_op jit(solution)/shard_map/pallas_call | solution.py:870
  243.0 7.3 fusion.22.x_ref
  250.4 55.7 %shard_map.345 = (f32[128,2048]{1,0:T(8,128)}, bf16[8,128,2048]{2,1,0:T(8,128)(2,1)}) custom-call(f32[8,128,2048]{2,1,0:T(8,128)} %fusion.22.x_ref, f32[1,2048]{1,0:T(1,128)} %bitcast.219, f32[128,2048]{1,0:T(8,128)} %convert_element_type.69.base_ref), custom_call_target="tpu_custom_call" | custom-call | bytes 150000000 | tf_op jit(solution)/shard_map/pallas_call | solution.py:933
  306.1 31.2 %all-gather.5.cloned.1.call-done = bf16[2048,1408]{1,0:T(8,128)(2,1)} async-done(((bf16[512,1408]{1,0:T(8,128)(2,1)}), bf16[2048,1408]{1,0:T(8,128)(2,1)}) %all-gather.5.cloned.1.call-update) | async-done | bytes 5767184 | tf_op jit(solution)/shard_map/all_gather | solution.py:1463
  337.3 11.1 %fusion.84 = f32[1024,1408]{0,1:T(8,128)S(1)} fusion(bf16[1024,2048]{1,0:T(8,128)(2,1)} %bitcast.240, bf16[2048,1408]{1,0:T(8,128)(2,1)} %all-gather.5.cloned.1.call-done), kind=kOutput, calls=%fused_computation.144 | convolution fusion | flops 5905580032 | bytes 15728640 | tf_op jit(solution)/shard_map/dot_general | solution.py:32
  348.4 6.8 fusion.9
  356.8 8.6 %convolution_convert_fusion = bf16[2048,1408]{1,0:T(8,128)(2,1)} fusion(bf16[1024,2048]{1,0:T(8,128)(2,1)S(1)} %bitcast.241, bf16[1024,704]{0,1:T(8,128)(2,1)S(1)} %get-tuple-element.193, bf16[1024,704]{0,1:T(8,128)(2,1)S(1)} %get-tuple-element.192), kind=kOutput, calls=%fused_computation | convolution fusion | flops 5914230784 | bytes 12845056 | tf_op jit(solution)/shard_map/dot_general | solution.py:32
  365.4 12.0 %fusion.17 = f32[1024,2048]{1,0:T(8,128)} fusion(bf16[2048,1408]{1,0:T(8,128)(2,1)} %all-gather.5.cloned.1.call-done, bf16[1024,704]{0,1:T(8,128)(2,1)} %copy-done.27, bf16[1024,704]{0,1:T(8,128)(2,1)} %copy-done.26), kind=kOutput, calls=%fused_computation.31 | convolution fusion | flops 5911347200 | bytes 17039360 | tf_op jit(solution)/shard_map/dot_general | solution.py:32
  377.5 7.2 convolution_convert_fusion.1
  384.7 56.7 %shard_map.346 = (f32[128,2048]{1,0:T(8,128)}, bf16[8,128,2048]{2,1,0:T(8,128)(2,1)}, f32[1,2048]{1,0:T(1,128)}, bf16[4,128,2048]{2,1,0:T(8,128)(2,1)}) custom-call(f32[8,128,2048]{2,1,0:T(8,128)} %bitcast.176, f32[1,2048]{1,0:T(1,128)} %bitcast.220, bf16[128,2048]{1,0:T(8,128)(2,1)} %get-tuple-element.100.base_ref, f32[128,2048]{1,0:T(8,128)} %get-tuple-element.92.refs_0_, ...), custom_call_target="tpu_custom_call" | custom-call | bytes 150000000 | tf_op jit(solution)/shard_map/pallas_call | solution.py:933
  441.4 5.9 convolution_convert_fusion.3
  447.2 12.3 %shard_map.347 = bf16[8,128,384]{2,1,0:T(8,128)(2,1)} custom-call(bf16[8,128,384]{2,1,0:T(8,128)(2,1)} %bitcast.199), custom_call_target="tpu_custom_call" | custom-call | bytes 90000000 | tf_op jit(solution)/shard_map/pallas_call | solution.py:870
  459.6 2.1 copy.190
  461.7 8.3 %shard_map.348 = (f32[128,3072]{1,0:T(8,128)}, bf16[128,3072]{1,0:T(8,128)(2,1)}, f32[6,1,512]{2,1,0:T(1,128)}, f32[6,256,512]{2,1,0:T(8,128)}) custom-call(f32[128,3072]{1,0:T(8,128)} %get-tuple-element.95.mixed_ref, f32[128,3072]{1,0:T(8,128)} %bitcast.175, f32[1,512]{1,0:T(1,128)} %bitcast.228, bf16[128,3072]{1,0:T(8,128)(2,1)} %bitcast.190, ...), custom_call_target="tpu_custom_call" | custom-call | flops 1000000000 | bytes 20000000 | tf_op jit(solution)/shard_map/pallas_call | solution.py:1375
  472.7 4.2 bitcast_convert_fusion.2
  476.9 3.4 convolution_convert_fusion.2
  480.3 2.6 pad_maximum_fusion.1
  482.9 39.1 %shard_map.349 = (bf16[6,256,512]{2,1,0:T(8,128)(2,1)}, bf16[8,128,384]{2,1,0:T(8,128)(2,1)}, bf16[4,128,2048]{2,1,0:T(8,128)(2,1)}) custom-call(bf16[6,256,256]{2,1,0:T(8,128)(2,1)} %get-tuple-element.93.high_ref, bf16[6,256,256]{2,1,0:T(8,128)(2,1)} %get-tuple-element.94.low_ref, f32[6,256,512]{2,1,0:T(8,128)} %get-tuple-element.104.add_ref, ...), custom_call_target="tpu_custom_call" | custom-call | bytes 200000000 | tf_op jit(solution)/shard_map/pallas_call | solution.py:1086
  522.0 3.6 all-to-all-start
  525.7 34.1 %shard_map.350 = (bf16[8,128,768]{2,1,0:T(8,128)(2,1)}, f32[8,16,768]{2,1,0:T(8,128)}, bf16[8,16,768]{2,1,0:T(8,128)(2,1)}, f32[8,8,768]{2,1,0:T(8,128)}, f32[6,8,128]{2,1,0:T(8,128)}, /*index=5*/f32[6,128,128]{2,1,0:T(8,128)}) custom-call(bf16[8,128,768]{2,1,0:T(8,128)(2,1)} %get-tuple-element.77.refs_0_.refs_1_.refs_2_.refs_3_.refs_4_.refs_5_.refs_6_.refs_7_, ...), custom_call_target="tpu_custom_call" | custom-call | flops 12000000000 | bytes 20000000 | tf_op jit(solution)/shard_map/pallas_call | solution.py:1375
  563.7 4.2 bitcast_convert_fusion.1
  568.0 26.1 %shard_map.351 = bf16[8,128,896]{2,1,0:T(8,128)(2,1)} custom-call(bf16[8,128,768]{2,1,0:T(8,128)(2,1)} %get-tuple-element.117.x_ref, f32[8,16,768]{2,1,0:T(8,128)} %get-tuple-element.118.tail_ref, bf16[8,16,768]{2,1,0:T(8,128)(2,1)} %get-tuple-element.119.rim_ref, bf16[128,128]{1,0:T(8,128)(2,1)} %pad.12.small_ref), custom_call_target="tpu_custom_call" | custom-call | bytes 90000000 | tf_op jit(solution)/shard_map/pallas_call | solution.py:995
  594.1 6.8 bitcast_convert_fusion
  600.9 2.7 pad_maximum_fusion
  603.9 2.4 copy.173
  607.2 2.1 convert_reduce_fusion.1
  614.6 9.6 %fusion.2 = bf16[1024,2048]{1,0:T(8,128)(2,1)} fusion(bf16[2048,1280]{1,0:T(8,128)(2,1)} %bitcast.214, bf16[1024,384]{1,0:T(8,128)(2,1)S(1)} %bitcast.242, bf16[1024,768]{1,0:T(8,128)(2,1)S(1)} %slice.199), kind=kOutput, calls=%fused_computation.9 | convolution fusion | flops 4838653952 | bytes 11272192 | tf_op jit(solution)/shard_map/dot_general | solution.py:32
  624.2 28.8 %shard_map.352 = bf16[4,128,2048]{2,1,0:T(8,128)(2,1)} custom-call(bf16[8,128,2048]{2,1,0:T(8,128)(2,1)} %bitcast.184), custom_call_target="tpu_custom_call" | custom-call | bytes 90000000 | tf_op jit(solution)/shard_map/pallas_call | solution.py:870
  653.1 2.1 convert_reduce_fusion
  657.6 5.4 shard_map.353
  664.5 7.1 shard_map.354
  673.1 6.5 shard_map.355
  688.4 4.4 all-to-all-start.1
  692.9 1.7 fusion.26
  697.7 1.7 reshape.258
  700.3 1.7 reshape.256
  702.0 7.7 %all-to-all-done.1 = bf16[8,64,1088]{2,1,0:T(8,128)(2,1)} async-done(((bf16[8,64,1088]{2,1,0:T(8,128)(2,1)}), bf16[8,64,1088]{2,1,0:T(8,128)(2,1)}, u32[]{:S(2)}, u32[]{:S(2)}) %all-to-all-start.1) | async-done | bytes 1114144 | tf_op jit(solution)/shard_map/all_to_all | solution.py:1740
  711.3 2.1 copy.181
  713.4 2.8 reshape.250
  720.3 15.7 %shard_map.356 = bf16[8,64,1152]{2,1,0:T(8,128)(2,1)} custom-call(bf16[8,64,1152]{2,1,0:T(8,128)(2,1)} %pad_maximum_fusion.5.x_ref), custom_call_target="tpu_custom_call" | custom-call | bytes 90000000 | tf_op jit(solution)/shard_map/pallas_call | solution.py:870
  (174 shorter events, 60.9 us)
Async XLA Ops:
  7.2 208.4 %all-gather.3.cloned.1.call-start = ((), (), s32[]{:S(2)}) async-start(), calls=%async_computation.5 | async-start | bytes 5898240 | tf_op jit(solution)/shard_map/all_gather | solution.py:1463
  10.0 102.1 %copy-start.15 = (s32[1,128]{1,0:T(1,128)S(1)}, s32[1,128]{1,0:T(1,128)}, u32[]{:S(2)}) copy-start(s32[1,128]{1,0:T(1,128)} %param.21) | copy-start | bytes 1540
  112.1 225.2 %all-gather.5.cloned.1.call-start = ((), (), s32[]{:S(2)}) async-start(), calls=%async_computation.6 | async-start | bytes 7208960 | tf_op jit(solution)/shard_map/all_gather | solution.py:1463
  112.2 43.7 %collective-permute-start = (s32[3]{0:T(128)S(1)}, s32[3]{0:T(128)S(1)}, u32[]{:S(2)}, u32[]{:S(2)}) collective-permute-start(s32[3]{0:T(128)S(1)} %slice_bitcast_fusion.10), channel_id=1, source_target_pairs={{0,1},{1,2},{2,3},{3,4},{4,5},{5,6},{6,7},{8,9},{9,10},{10,11},{11... | collective-permute-start | bytes 44 | tf_op jit(solution)/shard_map/ppermute | solution.py:1507
  116.7 31.4 %copy-start.22 = (f32[6]{0:T(128)S(1)}, f32[6]{0:T(128)}, u32[]{:S(2)}) copy-start(f32[6]{0:T(128)} %param.30) | copy-start | bytes 76
  116.7 31.9 %copy-start.11 = (f32[4,1536]{1,0:T(4,128)S(1)}, f32[4,1536]{1,0:T(4,128)}, u32[]{:S(2)}) copy-start(f32[4,1536]{1,0:T(4,128)} %param.31) | copy-start | bytes 73732
  116.7 31.9 %copy-start.12 = (f32[4,1536]{1,0:T(4,128)S(1)}, f32[4,1536]{1,0:T(4,128)}, u32[]{:S(2)}) copy-start(f32[4,1536]{1,0:T(4,128)} %param.32) | copy-start | bytes 73732
  116.8 32.9 %copy-start.9 = (f32[4,3072]{1,0:T(4,128)S(1)}, f32[4,3072]{1,0:T(4,128)}, u32[]{:S(2)}) copy-start(f32[4,3072]{1,0:T(4,128)} %param.33) | copy-start | bytes 147460
  149.6 6.3 copy-start.17
  183.8 32.1 %copy-start.16 = (f32[2048]{0:T(1024)S(1)}, f32[2048]{0:T(1024)}, u32[]{:S(2)}) copy-start(f32[2048]{0:T(1024)} %param.36) | copy-start | bytes 24580
  183.8 32.7 %copy-start = (bf16[128,2048]{1,0:T(8,128)(2,1)S(1)}, bf16[128,2048]{1,0:T(8,128)(2,1)}, u32[]{:S(2)}) copy-start(bf16[128,2048]{1,0:T(8,128)(2,1)} %get-tuple-element.91) | copy-start | bytes 1572868
  215.6 2.0 copy-start.6
  215.6 267.3 %reduce-scatter.4.cloned.1.call-start = ((), (), s32[]{:S(2)}) async-start(), calls=%async_computation.7 | async-start | bytes 7208960 | tf_op jit(solution)/shard_map/reduce_scatter | solution.py:1466
  337.3 11.1 %copy-start.18 = (bf16[8,128,2048]{2,1,0:T(8,128)(2,1)S(1)}, bf16[8,128,2048]{2,1,0:T(8,128)(2,1)}, u32[]{:S(2)}) copy-start(bf16[8,128,2048]{2,1,0:T(8,128)(2,1)} %get-tuple-element.96) | copy-start | bytes 12582916
  348.4 8.4 %copy-start.20 = (bf16[8,128,2048]{2,1,0:T(8,128)(2,1)S(1)}, bf16[8,128,2048]{2,1,0:T(8,128)(2,1)}, u32[]{:S(2)}) copy-start(bf16[8,128,2048]{2,1,0:T(8,128)(2,1)} %get-tuple-element.97) | copy-start | bytes 12582916
  355.3 1.1 copy-start.26
  355.3 1.6 copy-start.27
  355.3 22.2 %copy-start.24 = (bf16[1024,704]{0,1:T(8,128)(2,1)}, bf16[1024,704]{0,1:T(8,128)(2,1)S(1)}, u32[]{:S(2)}) copy-start(bf16[1024,704]{0,1:T(8,128)(2,1)S(1)} %get-tuple-element.194) | copy-start | bytes 4325380
  377.5 226.4 %reduce-scatter.6.cloned.1.call-start = ((), (), s32[]{:S(2)}) async-start(), calls=%async_computation.8 | async-start | bytes 5570560 | tf_op jit(solution)/shard_map/reduce_scatter | solution.py:1466
  461.7 11.0 %copy-start.5 = (bf16[8,128,384]{2,1,0:T(8,128)(2,1)S(1)}, bf16[8,128,384]{2,1,0:T(8,128)(2,1)}, u32[]{:S(2)}) copy-start(bf16[8,128,384]{2,1,0:T(8,128)(2,1)} %shard_map.344) | copy-start | bytes 2359300
  472.7 4.2 copy-start.19
  472.7 4.2 copy-start.25
  522.0 45.9 %all-to-all-start = ((bf16[8,64,1408]{2,1,0:T(8,128)(2,1)}), bf16[8,64,1408]{2,1,0:T(8,128)(2,1)S(1)}, u32[]{:S(2)}, u32[]{:S(2)}) async-start(bf16[8,64,1408]{2,1,0:T(8,128)(2,1)} %bitcast.36), calls=%async_computation.1 | async-start | bytes 2883584 | tf_op jit(solution)/shard_map/all_to_all | solution.py:1667
  525.6 191.7 %reduce-scatter.8.cloned.1.call-start = ((), (), s32[]{:S(2)}) async-start(), calls=%async_computation.9 | async-start | bytes 6553600 | tf_op jit(solution)/shard_map/reduce_scatter | solution.py:1466
  563.1 0.6 copy-start.7
  568.0 32.9 %copy-start.2 = (bf16[8,64,1408]{2,1,0:T(8,128)(2,1)}, bf16[8,64,1408]{2,1,0:T(8,128)(2,1)S(1)}, u32[]{:S(2)}) copy-start(bf16[8,64,1408]{2,1,0:T(8,128)(2,1)S(1)} %all-to-all-done) | copy-start | bytes 4325380
  606.3 0.7 copy-start.10
  606.3 0.9 copy-start.13
  606.3 3.0 copy-start.4
  609.3 4.9 copy-start.23
  609.3 5.0 copy-start.1
  613.1 1.5 copy-start.21
  653.0 2.1 copy-start.8
  653.0 3.8 copy-start.14
  688.4 21.3 %all-to-all-start.1 = ((bf16[8,64,1088]{2,1,0:T(8,128)(2,1)}), bf16[8,64,1088]{2,1,0:T(8,128)(2,1)}, u32[]{:S(2)}, u32[]{:S(2)}) async-start(bf16[8,64,1088]{2,1,0:T(8,128)(2,1)} %bitcast.63), calls=%async_computation.4 | async-start | bytes 2359296 | tf_op jit(solution)/shard_map/all_to_all | solution.py:1740
  692.9 3.5 copy-start.3
Sparse Core Ops, SparseCore 0:
  112.2 89.1 all-gather.2
  215.7 121.5 all-gather.4
  377.6 100.5 reduce-scatter.3
  522.1 81.6 reduce-scatter.5
  606.4 95.2 reduce-scatter.7

commit v5 on v4

--- a/solution.py
+++ b/solution.py
@@ -15,8 +15,8 @@
 F32 = jnp.float32
 BY_MESH = pl.DeviceIdType.MESH
 LANES = 128
-PIECES = 2
-CHUNKS = 2
+PIECES = 4
+CHUNKS = 4
 RIM = 16
 
 
@@ -1535,7 +1535,7 @@
         lambda h: 2 * heads + 2 * h + 1,
     ]
 
-    step = 2 if heads % 2 == 0 else 1
+    step = 3 if heads % 3 == 0 else 1
 
     def at_blocks(make, step):
         return [

time: 755 us -> 755 us (level)
  no operation moved by 1% of the time
where the time goes in v5:
time: 755 us; the launch traced here: 748 us
  Pallas kernels  499 us (66%)
  matrix products  106 us (14%)
  local copies, waits for them, and re-layouts  54 us (7%)
  waiting for transfers between devices  38.1 us (5%)
  other arithmetic  25.8 us (3%)
  between operations  14.9 us (2%)
  starting transfers between devices  10.6 us (1%)
    pallas_call x2, Pallas kernels, turn(): pl.pallas_call(partial(turn_kernel, rows, backward), out_shape=[jax.Shape...  112 us
    dot_general x16, matrix products, mm(): lax.dot_general(left, right, (((over[0],), (over[1],)), ((), ())), prefer...  105 us
    pallas_call x1, Pallas kernels, begin(): pl.pallas_call(partial(start_kernel, rows, count), out_shape=[jax.ShapeDt...  102 us
    pallas_call x7, Pallas kernels, comm_call(): pl.pallas_call(body, out_shape=out, in_specs=[spec] * len(operands), out_...  93.5 us
    pallas_call x2, Pallas kernels, chain(): pl.pallas_call(partial(chain_kernel, count, rows, heads, len(sides), forw...  71.5 us
    pallas_call x4, Pallas kernels, head_call(): pl.pallas_call(body, scratch_shapes=scratch, grid=(heads,), in_specs=in_s...  70.8 us
    all_gather x2, waiting for transfers between devices, gathered(): lax.all_gather(values.reshape(group * owned, -1), 'zq', axis=0, tiled=True)  30.2 us
    pallas_call x1, Pallas kernels, swap_back(): pl.pallas_call(partial(swap_back_kernel, rows, count), out_shape=jax.Shap...  26 us
  transfers between devices with their start and end apart: 8, of which 3 were waited for; matrix products, arithmetic and copies ran while one was open for 17% of the time, Pallas kernels for 46%

profile of v5, /device:TPU:0, one launch (start us, length us, event | category | flops | bytes accessed | tf_op | source)
XLA Modules:
  0.0 748.4 jit_solution(4126860988500691645)
XLA Ops:
  10.0 102.0 %shard_map.339 = (bf16[4,8,64,1280]{3,2,1,0:T(8,128)(2,1)}, bf16[8,64,1088]{2,1,0:T(8,128)(2,1)}, bf16[8,64,1408]{2,1,0:T(8,128)(2,1)}, bf16[8,128,2048]{2,1,0:T...) custom-call(bf16[128,2048]{1,0:T(8,128)(2,1)} %bitcast.200, ...), custom_call_target="tpu_custom_call" | custom-call | bytes 300000000 | tf_op jit(solution)/shard_map/pallas_call | solution.py:1025
  112.2 2.3 collective-permute-start
  116.8 8.3 %fusion.18 = bf16[1024,768]{1,0:T(8,128)(2,1)} fusion(bf16[1024,2048]{1,0:T(8,128)(2,1)} %bitcast.236, bf16[2048,1280]{1,0:T(8,128)(2,1)} %bitcast.212), kind=kOutput, calls=%fused_computation.32 | convolution fusion | flops 3222011904 | bytes 8912896 | tf_op jit(solution)/shard_map/dot_general | solution.py:32
  125.1 23.0 %shard_map.340 = (bf16[8,128,768]{2,1,0:T(8,128)(2,1)}, bf16[8,16,768]{2,1,0:T(8,128)(2,1)}) custom-call(bf16[8,128,768]{2,1,0:T(8,128)(2,1)} %bitcast.194), custom_call_target="tpu_custom_call" | custom-call | bytes 90000000 | tf_op jit(solution)/shard_map/pallas_call | solution.py:970
  149.7 6.3 fusion.21.refs_0_
  159.6 21.8 %shard_map.341 = (f32[6,128,128]{2,1,0:T(8,128)}, f32[6,128,128]{2,1,0:T(8,128)}, f32[128,3072]{1,0:T(8,128)}, f32[6,128,256]{2,1,0:T(8,128)}, f32[6,256,512]{2,...) custom-call(bf16[8,128,768]{2,1,0:T(8,128)(2,1)} %get-tuple-element., ...), custom_call_target="tpu_custom_call" | custom-call | flops 6000000000 | bytes 20000000 | tf_op jit(solution)/shard_map/pallas_call | solution.py:1375
  181.4 32.0 %shard_map.342 = (bf16[6,256,512]{2,1,0:T(8,128)(2,1)}, f32[8,128,384]{2,1,0:T(8,128)}) custom-call(bf16[6,256,256]{2,1,0:T(8,128)(2,1)} %get-tuple-element.83.high_ref, bf16[6,256,256]{2,1,0:T(8,128)(2,1)} %get-tuple-element.84.low_ref, f32[6,256,512]{2,1,0:T(8,128)} %get-tuple-element.85.add_ref, f32[8,128,384]{2,1,0:T(8,128)} %fusion.21.refs_0_), custom_call_target="tpu_custom_call" | custom-call | bytes 200000000 | tf_op jit(solution)/shard_map/pallas_call | solution.py:1086
  216.5 6.5 shard_map.343
  225.7 17.4 %shard_map.344 = bf16[8,128,384]{2,1,0:T(8,128)(2,1)} custom-call(bf16[8,128,384]{2,1,0:T(8,128)(2,1)} %bitcast.187), custom_call_target="tpu_custom_call" | custom-call | bytes 90000000 | tf_op jit(solution)/shard_map/pallas_call | solution.py:870
  243.2 7.3 fusion.22.x_ref
  250.5 55.7 %shard_map.345 = (f32[128,2048]{1,0:T(8,128)}, bf16[8,128,2048]{2,1,0:T(8,128)(2,1)}) custom-call(f32[8,128,2048]{2,1,0:T(8,128)} %fusion.22.x_ref, f32[1,2048]{1,0:T(1,128)} %bitcast.219, f32[128,2048]{1,0:T(8,128)} %convert_element_type.69.base_ref), custom_call_target="tpu_custom_call" | custom-call | bytes 150000000 | tf_op jit(solution)/shard_map/pallas_call | solution.py:933
  306.2 30.2 %all-gather.5.cloned.1.call-done = bf16[2048,1408]{1,0:T(8,128)(2,1)} async-done(((bf16[512,1408]{1,0:T(8,128)(2,1)}), bf16[2048,1408]{1,0:T(8,128)(2,1)}) %all-gather.5.cloned.1.call-update) | async-done | bytes 5767184 | tf_op jit(solution)/shard_map/all_gather | solution.py:1463
  336.5 10.9 %fusion.84 = f32[1024,1408]{0,1:T(8,128)S(1)} fusion(bf16[1024,2048]{1,0:T(8,128)(2,1)} %bitcast.240, bf16[2048,1408]{1,0:T(8,128)(2,1)} %all-gather.5.cloned.1.call-done), kind=kOutput, calls=%fused_computation.144 | convolution fusion | flops 5905580032 | bytes 15728640 | tf_op jit(solution)/shard_map/dot_general | solution.py:32
  347.4 6.8 fusion.9
  355.8 8.6 %convolution_convert_fusion = bf16[2048,1408]{1,0:T(8,128)(2,1)} fusion(bf16[1024,2048]{1,0:T(8,128)(2,1)S(1)} %bitcast.241, bf16[1024,704]{0,1:T(8,128)(2,1)S(1)} %get-tuple-element.193, bf16[1024,704]{0,1:T(8,128)(2,1)S(1)} %get-tuple-element.192), kind=kOutput, calls=%fused_computation | convolution fusion | flops 5914230784 | bytes 12845056 | tf_op jit(solution)/shard_map/dot_general | solution.py:32
  364.4 12.0 %fusion.17 = f32[1024,2048]{1,0:T(8,128)} fusion(bf16[2048,1408]{1,0:T(8,128)(2,1)} %all-gather.5.cloned.1.call-done, bf16[1024,704]{0,1:T(8,128)(2,1)} %copy-done.27, bf16[1024,704]{0,1:T(8,128)(2,1)} %copy-done.26), kind=kOutput, calls=%fused_computation.31 | convolution fusion | flops 5911347200 | bytes 17039360 | tf_op jit(solution)/shard_map/dot_general | solution.py:32
  376.5 7.4 convolution_convert_fusion.1
  383.9 56.6 %shard_map.346 = (f32[128,2048]{1,0:T(8,128)}, bf16[8,128,2048]{2,1,0:T(8,128)(2,1)}, f32[1,2048]{1,0:T(1,128)}, bf16[4,128,2048]{2,1,0:T(8,128)(2,1)}) custom-call(f32[8,128,2048]{2,1,0:T(8,128)} %bitcast.176, f32[1,2048]{1,0:T(1,128)} %bitcast.220, bf16[128,2048]{1,0:T(8,128)(2,1)} %get-tuple-element.100.base_ref, f32[128,2048]{1,0:T(8,128)} %get-tuple-element.92.refs_0_, ...), custom_call_target="tpu_custom_call" | custom-call | bytes 150000000 | tf_op jit(solution)/shard_map/pallas_call | solution.py:933
  440.5 5.9 convolution_convert_fusion.3
  446.4 12.6 %shard_map.347 = bf16[8,128,384]{2,1,0:T(8,128)(2,1)} custom-call(bf16[8,128,384]{2,1,0:T(8,128)(2,1)} %bitcast.199), custom_call_target="tpu_custom_call" | custom-call | bytes 90000000 | tf_op jit(solution)/shard_map/pallas_call | solution.py:870
  459.0 2.1 copy.190
  461.1 8.3 %shard_map.348 = (f32[128,3072]{1,0:T(8,128)}, bf16[128,3072]{1,0:T(8,128)(2,1)}, f32[6,1,512]{2,1,0:T(1,128)}, f32[6,256,512]{2,1,0:T(8,128)}) custom-call(f32[128,3072]{1,0:T(8,128)} %get-tuple-element.95.mixed_ref, f32[128,3072]{1,0:T(8,128)} %bitcast.175, f32[1,512]{1,0:T(1,128)} %bitcast.228, bf16[128,3072]{1,0:T(8,128)(2,1)} %bitcast.190, ...), custom_call_target="tpu_custom_call" | custom-call | flops 1000000000 | bytes 20000000 | tf_op jit(solution)/shard_map/pallas_call | solution.py:1375
  472.1 4.2 bitcast_convert_fusion.2
  476.3 3.4 convolution_convert_fusion.2
  479.7 2.6 pad_maximum_fusion.1
  482.3 39.6 %shard_map.349 = (bf16[6,256,512]{2,1,0:T(8,128)(2,1)}, bf16[8,128,384]{2,1,0:T(8,128)(2,1)}, bf16[4,128,2048]{2,1,0:T(8,128)(2,1)}) custom-call(bf16[6,256,256]{2,1,0:T(8,128)(2,1)} %get-tuple-element.93.high_ref, bf16[6,256,256]{2,1,0:T(8,128)(2,1)} %get-tuple-element.94.low_ref, f32[6,256,512]{2,1,0:T(8,128)} %get-tuple-element.104.add_ref, ...), custom_call_target="tpu_custom_call" | custom-call | bytes 200000000 | tf_op jit(solution)/shard_map/pallas_call | solution.py:1086
  521.9 3.6 all-to-all-start
  525.5 34.1 %shard_map.350 = (bf16[8,128,768]{2,1,0:T(8,128)(2,1)}, f32[8,16,768]{2,1,0:T(8,128)}, bf16[8,16,768]{2,1,0:T(8,128)(2,1)}, f32[8,8,768]{2,1,0:T(8,128)}, f32[6,8,128]{2,1,0:T(8,128)}, /*index=5*/f32[6,128,128]{2,1,0:T(8,128)}) custom-call(bf16[8,128,768]{2,1,0:T(8,128)(2,1)} %get-tuple-element.77.refs_0_.refs_1_.refs_2_.refs_3_.refs_4_.refs_5_.refs_6_.refs_7_.refs_8_.refs_9_, ...), custom_call_target="tpu_custom_call" | custom-call | flops 12000000000 | bytes 20000000 | tf_op jit(solution)/shard_map/pallas_call | solution.py:1375
  563.6 4.2 bitcast_convert_fusion.1
  567.8 26.0 %shard_map.351 = bf16[8,128,896]{2,1,0:T(8,128)(2,1)} custom-call(bf16[8,128,768]{2,1,0:T(8,128)(2,1)} %get-tuple-element.117.x_ref, f32[8,16,768]{2,1,0:T(8,128)} %get-tuple-element.118.tail_ref, bf16[8,16,768]{2,1,0:T(8,128)(2,1)} %get-tuple-element.119.rim_ref, bf16[128,128]{1,0:T(8,128)(2,1)} %pad.12.small_ref), custom_call_target="tpu_custom_call" | custom-call | bytes 90000000 | tf_op jit(solution)/shard_map/pallas_call | solution.py:995
  593.9 6.8 bitcast_convert_fusion
  600.7 2.7 pad_maximum_fusion
  603.4 2.4 copy.173
  606.7 2.1 convert_reduce_fusion.1
  614.1 9.6 %fusion.2 = bf16[1024,2048]{1,0:T(8,128)(2,1)} fusion(bf16[2048,1280]{1,0:T(8,128)(2,1)} %bitcast.214, bf16[1024,384]{1,0:T(8,128)(2,1)S(1)} %bitcast.242, bf16[1024,768]{1,0:T(8,128)(2,1)S(1)} %slice.199), kind=kOutput, calls=%fused_computation.9 | convolution fusion | flops 4838653952 | bytes 11272192 | tf_op jit(solution)/shard_map/dot_general | solution.py:32
  623.7 28.9 %shard_map.352 = bf16[4,128,2048]{2,1,0:T(8,128)(2,1)} custom-call(bf16[8,128,2048]{2,1,0:T(8,128)(2,1)} %bitcast.184), custom_call_target="tpu_custom_call" | custom-call | bytes 90000000 | tf_op jit(solution)/shard_map/pallas_call | solution.py:870
  652.7 2.1 convert_reduce_fusion
  657.2 5.5 shard_map.353
  664.3 6.9 shard_map.354
  672.6 6.5 shard_map.355
  688.0 4.5 all-to-all-start.1
  692.5 1.7 fusion.26
  697.3 1.7 reshape.258
  699.9 1.7 reshape.256
  701.6 7.7 %all-to-all-done.1 = bf16[8,64,1088]{2,1,0:T(8,128)(2,1)} async-done(((bf16[8,64,1088]{2,1,0:T(8,128)(2,1)}), bf16[8,64,1088]{2,1,0:T(8,128)(2,1)}, u32[]{:S(2)}, u32[]{:S(2)}) %all-to-all-start.1) | async-done | bytes 1114144 | tf_op jit(solution)/shard_map/all_to_all | solution.py:1740
  710.9 2.1 copy.181
  713.0 2.8 reshape.250
  719.9 15.7 %shard_map.356 = bf16[8,64,1152]{2,1,0:T(8,128)(2,1)} custom-call(bf16[8,64,1152]{2,1,0:T(8,128)(2,1)} %pad_maximum_fusion.5.x_ref), custom_call_target="tpu_custom_call" | custom-call | bytes 90000000 | tf_op jit(solution)/shard_map/pallas_call | solution.py:870
  (174 shorter events, 60.4 us)
Async XLA Ops:
  7.2 206.2 %all-gather.3.cloned.1.call-start = ((), (), s32[]{:S(2)}) async-start(), calls=%async_computation.5 | async-start | bytes 5898240 | tf_op jit(solution)/shard_map/all_gather | solution.py:1463
  10.0 102.1 %copy-start.16 = (s32[1,128]{1,0:T(1,128)S(1)}, s32[1,128]{1,0:T(1,128)}, u32[]{:S(2)}) copy-start(s32[1,128]{1,0:T(1,128)} %param.21) | copy-start | bytes 1540
  112.1 224.4 %all-gather.5.cloned.1.call-start = ((), (), s32[]{:S(2)}) async-start(), calls=%async_computation.6 | async-start | bytes 7208960 | tf_op jit(solution)/shard_map/all_gather | solution.py:1463
  112.2 43.7 %collective-permute-start = (s32[3]{0:T(128)S(1)}, s32[3]{0:T(128)S(1)}, u32[]{:S(2)}, u32[]{:S(2)}) collective-permute-start(s32[3]{0:T(128)S(1)} %slice_bitcast_fusion.10), channel_id=1, source_target_pairs={{0,1},{1,2},{2,3},{3,4},{4,5},{5,6},{6,7},{8,9},{9,10},{10,11},{11... | collective-permute-start | bytes 44 | tf_op jit(solution)/shard_map/ppermute | solution.py:1507
  116.7 31.4 %copy-start.22 = (f32[6]{0:T(128)S(1)}, f32[6]{0:T(128)}, u32[]{:S(2)}) copy-start(f32[6]{0:T(128)} %param.30) | copy-start | bytes 76
  116.7 31.9 %copy-start.12 = (f32[4,1536]{1,0:T(4,128)S(1)}, f32[4,1536]{1,0:T(4,128)}, u32[]{:S(2)}) copy-start(f32[4,1536]{1,0:T(4,128)} %param.31) | copy-start | bytes 73732
  116.7 31.9 %copy-start.13 = (f32[4,1536]{1,0:T(4,128)S(1)}, f32[4,1536]{1,0:T(4,128)}, u32[]{:S(2)}) copy-start(f32[4,1536]{1,0:T(4,128)} %param.32) | copy-start | bytes 73732
  116.8 32.9 %copy-start.10 = (f32[4,3072]{1,0:T(4,128)S(1)}, f32[4,3072]{1,0:T(4,128)}, u32[]{:S(2)}) copy-start(f32[4,3072]{1,0:T(4,128)} %param.33) | copy-start | bytes 147460
  149.6 6.3 copy-start
  181.4 32.1 %copy-start.17 = (f32[2048]{0:T(1024)S(1)}, f32[2048]{0:T(1024)}, u32[]{:S(2)}) copy-start(f32[2048]{0:T(1024)} %param.36) | copy-start | bytes 24580
  181.4 32.7 %copy-start.1 = (bf16[128,2048]{1,0:T(8,128)(2,1)S(1)}, bf16[128,2048]{1,0:T(8,128)(2,1)}, u32[]{:S(2)}) copy-start(bf16[128,2048]{1,0:T(8,128)(2,1)} %get-tuple-element.91) | copy-start | bytes 1572868
  213.4 1.8 copy-start.7
  213.4 268.9 %reduce-scatter.4.cloned.1.call-start = ((), (), s32[]{:S(2)}) async-start(), calls=%async_computation.7 | async-start | bytes 7208960 | tf_op jit(solution)/shard_map/reduce_scatter | solution.py:1466
  336.5 10.9 %copy-start.18 = (bf16[8,128,2048]{2,1,0:T(8,128)(2,1)S(1)}, bf16[8,128,2048]{2,1,0:T(8,128)(2,1)}, u32[]{:S(2)}) copy-start(bf16[8,128,2048]{2,1,0:T(8,128)(2,1)} %get-tuple-element.96) | copy-start | bytes 12582916
  347.4 8.4 %copy-start.20 = (bf16[8,128,2048]{2,1,0:T(8,128)(2,1)S(1)}, bf16[8,128,2048]{2,1,0:T(8,128)(2,1)}, u32[]{:S(2)}) copy-start(bf16[8,128,2048]{2,1,0:T(8,128)(2,1)} %get-tuple-element.97) | copy-start | bytes 12582916
  354.2 1.1 copy-start.26
  354.2 1.6 copy-start.27
  354.2 22.2 %copy-start.24 = (bf16[1024,704]{0,1:T(8,128)(2,1)}, bf16[1024,704]{0,1:T(8,128)(2,1)S(1)}, u32[]{:S(2)}) copy-start(bf16[1024,704]{0,1:T(8,128)(2,1)S(1)} %get-tuple-element.194) | copy-start | bytes 4325380
  376.4 227.0 %reduce-scatter.6.cloned.1.call-start = ((), (), s32[]{:S(2)}) async-start(), calls=%async_computation.8 | async-start | bytes 5570560 | tf_op jit(solution)/shard_map/reduce_scatter | solution.py:1466
  461.1 11.0 %copy-start.6 = (bf16[8,128,384]{2,1,0:T(8,128)(2,1)S(1)}, bf16[8,128,384]{2,1,0:T(8,128)(2,1)}, u32[]{:S(2)}) copy-start(bf16[8,128,384]{2,1,0:T(8,128)(2,1)} %shard_map.344) | copy-start | bytes 2359300
  472.1 4.2 copy-start.19
  472.1 4.2 copy-start.25
  521.9 46.0 %all-to-all-start = ((bf16[8,64,1408]{2,1,0:T(8,128)(2,1)}), bf16[8,64,1408]{2,1,0:T(8,128)(2,1)S(1)}, u32[]{:S(2)}, u32[]{:S(2)}) async-start(bf16[8,64,1408]{2,1,0:T(8,128)(2,1)} %bitcast.36), calls=%async_computation.1 | async-start | bytes 2883584 | tf_op jit(solution)/shard_map/all_to_all | solution.py:1667
  525.5 191.5 %reduce-scatter.8.cloned.1.call-start = ((), (), s32[]{:S(2)}) async-start(), calls=%async_computation.9 | async-start | bytes 6553600 | tf_op jit(solution)/shard_map/reduce_scatter | solution.py:1466
  563.0 0.6 copy-start.8
  567.8 32.8 %copy-start.3 = (bf16[8,64,1408]{2,1,0:T(8,128)(2,1)}, bf16[8,64,1408]{2,1,0:T(8,128)(2,1)S(1)}, u32[]{:S(2)}) copy-start(bf16[8,64,1408]{2,1,0:T(8,128)(2,1)S(1)} %all-to-all-done) | copy-start | bytes 4325380
  605.8 0.7 copy-start.11
  605.8 0.9 copy-start.14
  605.8 3.0 copy-start.5
  608.9 4.9 copy-start.23
  608.9 5.0 copy-start.2
  612.6 1.5 copy-start.21
  652.6 2.1 copy-start.9
  652.6 3.8 copy-start.15
  688.0 21.3 %all-to-all-start.1 = ((bf16[8,64,1088]{2,1,0:T(8,128)(2,1)}), bf16[8,64,1088]{2,1,0:T(8,128)(2,1)}, u32[]{:S(2)}, u32[]{:S(2)}) async-start(bf16[8,64,1088]{2,1,0:T(8,128)(2,1)} %bitcast.63), calls=%async_computation.4 | async-start | bytes 2359296 | tf_op jit(solution)/shard_map/all_to_all | solution.py:1740
  692.5 3.5 copy-start.4
Sparse Core Ops, SparseCore 0:
  112.2 89.9 all-gather.2
  213.5 122.8 all-gather.4
  376.5 100.5 reduce-scatter.3
  522.0 81.3 reduce-scatter.5
  606.0 95.2 reduce-scatter.7
